TPU v7x, 32 devices: a whole 2x2x4 slice. The times are simulated.
32 devices in a mesh: dp: 4 (over z), krow: 8 (over y, x, core).
Axes of the slice: x: 2, y: 2, z: 4, core: 2. Of those that a mesh axis runs over, the one named last changes fastest.
Arguments:
- tokens: bfloat16 [12, 2048, 768], P('dp', 'krow'), may hold values from -6 to 6
- lengths: int32 [12], P('dp'), may hold values from 65 to 2048, as said below
- attn_gain: float32 [768], replicated, may hold values from 0.5 to 1.5
- attn_bias: float32 [768], replicated, may hold values from -1 to 1
- query_weight: bfloat16 [768, 768], replicated, may hold values from -0.4375 to 0.4375
- key_weight: bfloat16 [768, 768], replicated, may hold values from -0.21875 to 0.21875
- value_weight: bfloat16 [768, 768], replicated, may hold values from -0.21875 to 0.21875
- out_weight: bfloat16 [768, 768], replicated, may hold values from -3.5 to 3.5
- compress: bfloat16 [256, 2048], P('krow'), may hold values from -0.125 to 0.125
- ffn_gain: float32 [768], replicated, may hold values from 0.5 to 1.5
- ffn_bias: float32 [768], replicated, may hold values from -1 to 1
- up_weight: bfloat16 [768, 3072], replicated, may hold values from -0.21875 to 0.21875
- down_weight: bfloat16 [3072, 768], replicated, may hold values from -0.109375 to 0.109375
- cotangent: bfloat16 [12, 2048, 768], P('dp', 'krow'), may hold values from -6 to 6
Outputs:
- block_out: bfloat16 [12, 2048, 768], P('dp', 'krow')
- tokens_grad: bfloat16 [12, 2048, 768], P('dp', 'krow')
- attn_gain_grad: float32 [768], replicated
- attn_bias_grad: float32 [768], replicated
- query_weight_grad: float32 [768, 768], replicated
- key_weight_grad: float32 [768, 768], replicated
- value_weight_grad: float32 [768, 768], replicated
- out_weight_grad: float32 [768, 768], replicated
- compress_grad: float32 [256, 2048], P('krow')
- ffn_gain_grad: float32 [768], replicated
- ffn_bias_grad: float32 [768], replicated
- up_weight_grad: float32 [768, 3072], replicated
- down_weight_grad: float32 [3072, 768], replicated
- grad_norm: float32 [], replicated
Inputs may be any that keep to these rules, and one draw needn't show every extreme that they name: `lengths`: at least one sequence is 2048 positions long; positions at or past a sequence's length are padding.
All inputs are finite; a program needn't handle non-finite values.
Results may differ from a plain program's by a relative error of at most 0.019.
Values may be sent and summed in bfloat16 or wider, within the bound.
No kernel may reach another device: no remote copies, remote signals or barrier semaphores. Data moves between devices by JAX's collectives and lax.ppermute only.
A program may use at most 256 MiB of HBM per device.

v0:
```python
import functools

import jax
import jax.numpy as jnp
from jax import lax
from jax.experimental import pallas as pl
from jax.experimental.pallas import tpu as pltpu
from jax.sharding import PartitionSpec as P

HEAD_DIM = 64
QUAD = 256
EPSILON = 1e-05
SCALE = HEAD_DIM ** (-0.5)
LOW = jnp.bfloat16
F32 = jnp.float32
COST = 10**9


def dot(left_side, right_side, contract):
    return lax.dot_general(
        left_side, right_side, (contract, ((), ())), preferred_element_type=F32
    )


def nn(left_side, right_side):
    return dot(left_side, right_side, ((1,), (0,)))


def nt(left_side, right_side):
    return dot(left_side, right_side, ((1,), (1,)))


def shape(dims, kind=LOW):
    return jax.ShapeDtypeStruct(dims, kind)


def far(dims, kind=LOW):
    return pltpu.HBM(dims, kind)


def kept_far(*values):
    return tuple(pltpu.with_memory_space_constraint(v, pltpu.HBM) for v in values)


def whole(*dims):
    return pl.BlockSpec(dims, lambda *_: (0,) * len(dims), pipeline_mode=pl.Buffered(1))


def result(*dims):
    return pl.BlockSpec(dims, lambda *_: (0,) * len(dims))


def vector(width):
    return pl.BlockSpec((width,), lambda *_: (0,))


def per_seq(*dims):
    return pl.BlockSpec((None, *dims), lambda s, *_: (s, *(0,) * len(dims)))


def call(body, grid, ins, outs, out_specs, in_specs, scratch=(), scalars=0, limit=24, cost=1):
    return pl.pallas_call(
        body,
        grid_spec=pltpu.PrefetchScalarGridSpec(
            num_scalar_prefetch=scalars,
            grid=grid,
            in_specs=in_specs,
            out_specs=out_specs,
            scratch_shapes=scratch,
        ),
        out_shape=outs,
        compiler_params=pltpu.CompilerParams(vmem_limit_bytes=limit << 20),
        cost_estimate=pl.CostEstimate(flops=cost * COST, bytes_accessed=1, transcendentals=0),
    )(*ins)


def row(ref):
    return ref[...].reshape(1, -1)


def centre(values):
    centred = values - jnp.mean(values, axis=-1, keepdims=True)
    spread = jnp.mean(centred * centred, axis=-1, keepdims=True)
    inverse = lax.rsqrt(spread + EPSILON)
    return centred * inverse, inverse


def normalize_back(grad, unit, inverse, gain):
    scaled = grad * gain
    return inverse * (
        scaled
        - jnp.mean(scaled, axis=-1, keepdims=True)
        - unit * jnp.mean(scaled * unit, axis=-1, keepdims=True)
    )


def enter_body(tokens, gain, bias, normed):
    unit, _ = centre(tokens[...].astype(F32))
    normed[...] = (unit * row(gain) + row(bias)).astype(LOW)


def enter(tokens, gain, bias):
    seqs, span, width = tokens.shape
    block = per_seq(span, width)
    return call(
        enter_body,
        (seqs,),
        (tokens, gain, bias),
        far(tokens.shape),
        block,
        [block, vector(width), vector(width)],
        limit=10,
        cost=1,
    )


def project_body(normed, weight, queries):
    queries[...] = (nn(normed[...], weight[...]) * SCALE).astype(LOW)


def project(normed, weight):
    seqs, span, width = normed.shape
    block = per_seq(span, width)
    return call(
        project_body,
        (seqs,),
        (normed, weight),
        far(normed.shape),
        block,
        [block, whole(width, width)],
        limit=10,
        cost=1,
    )


def grad_active_body(cotangent, down, out):
    out[...] = nt(cotangent[...], down[...]).astype(LOW)


def grad_active_of(cotangent, down):
    rows, width = cotangent.shape
    hidden = down.shape[0]
    cut = QUAD * 2
    return call(
        grad_active_body,
        (hidden // cut,),
        (cotangent, down),
        far((rows, hidden)),
        pl.BlockSpec((rows, cut), lambda i: (0, i)),
        [whole(rows, width), pl.BlockSpec((cut, width), lambda i: (i, 0))],
        limit=14,
        cost=5,
    )


def block_at(step, order):
    return step - step % 2 + (order[0] ^ 1 ^ (step % 2))


def block_out_body(order, down, attended, *refs):
    *actives, out = refs
    width = attended.shape[1]
    total = attended[...]
    for at, active in enumerate(actives):
        start = pl.multiple_of(block_at(at, order) * width, width)
        total += nn(active[...], down[pl.ds(start, width), :])
    out[...] = total.astype(LOW)


def block_out_of(order, down, attended, *actives):
    seqs, span, width = attended.shape
    lines = pl.BlockSpec((span, width), lambda s, m: (s, 0))
    return call(
        block_out_body,
        (seqs,),
        (order, down, *kept_far(attended, *actives)),
        shape(attended.shape),
        per_seq(span, width),
        [whole(*down.shape), per_seq(span, width), *([lines] * len(actives))],
        scalars=1,
        limit=24,
        cost=6,
    )


def send_by_distance(me, value, held, kept, sent):
    pieces = 2 * kept.shape[0]
    cut = value.shape[0] // pieces
    held[...] = value
    for pair in range(pieces // 2):
        for other, out in enumerate((kept, sent)):
            start = pl.multiple_of(((2 * pair + other) ^ me) * cut, cut)
            out[pair] = held[pl.ds(start, cut), :].astype(LOW)


def take_by_distance(me, own, other, out):
    pieces = 2 * own.shape[0]
    cut = own.shape[1]
    for pair in range(pieces // 2):
        for at, source in enumerate((own, other)):
            start = pl.multiple_of(((2 * pair + at) ^ me) * cut, cut)
            out[pl.ds(start, cut), :] = source[pair]


def distance_rows(pairs, seqs, rows, width):
    return shape((pairs, seqs, rows // pairs // 2, width))


def distance_spec(pairs, rows, width):
    return pl.BlockSpec((pairs, None, rows // pairs // 2, width), lambda s, *_: (0, s, 0, 0))


def summarize_body(meta, columns, normed, kept, sent, held):
    seq = pl.program_id(0)
    rows, span = columns.shape
    at = meta[0] * span + lax.broadcasted_iota(jnp.int32, (rows, span), 1)
    masked = jnp.where(at < meta[1 + seq], columns[...].astype(F32), 0.0).astype(LOW)
    send_by_distance(meta[0], nn(masked, normed[...]), held, kept, sent)


def summarize(pairs, meta, columns, normed):
    seqs, span, width = normed.shape
    rows = columns.shape[0]
    return call(
        summarize_body,
        (seqs,),
        (meta, columns, normed),
        [distance_rows(pairs, seqs, rows, width)] * 2,
        [distance_spec(pairs, rows, width)] * 2,
        [whole(rows, span), per_seq(span, width)],
        [pltpu.VMEM((rows, width), F32)],
        scalars=1,
        limit=12,
        cost=2,
    )


def head_masks(dims, axis):
    lane = lax.broadcasted_iota(jnp.int32, dims, axis) // HEAD_DIM
    return [lane == h for h in range(QUAD // HEAD_DIM)]


def stack_heads(value, masks, axis):
    wide = value.astype(F32)
    return jnp.concatenate([jnp.where(m, wide, 0.0).astype(LOW) for m in masks], axis=axis)


def own_heads(stacked, masks, rows):
    parts = [stacked[h * rows : (h + 1) * rows] for h in range(len(masks))]
    out = jnp.where(masks[0], parts[0], 0.0)
    for mask, part in zip(masks[1:], parts[1:]):
        out = jnp.where(mask, part, out)
    return out


def attend_body(
    meta, tokens, queries, own, other, key_w, value_w, out_w, gain, bias,
    summary, keys, values, probs, mixed, attended, lifted, inverse_out,
):
    span, width = tokens.shape
    rows = summary.shape[0]
    take_by_distance(meta[0], own, other, summary)
    key_all = nn(summary[...], key_w[...]).astype(LOW)
    value_all = nn(summary[...], value_w[...]).astype(LOW)
    keys[...] = key_all
    values[...] = value_all
    side = head_masks((rows, QUAD), 1)
    turned = head_masks((QUAD, rows), 0)
    quads = []
    for q in range(width // QUAD):
        cut = slice(q * QUAD, (q + 1) * QUAD)
        scores = nt(stack_heads(key_all[:, cut], side, 0), queries[:, cut])
        lows = []
        for h in range(len(side)):
            part = scores[h * rows : (h + 1) * rows]
            grown = jnp.exp(part - jnp.max(part, axis=0, keepdims=True))
            lows.append((grown / jnp.sum(grown, axis=0, keepdims=True)).astype(LOW))
        low = jnp.concatenate(lows, axis=0)
        probs[q * low.shape[0] : (q + 1) * low.shape[0], :] = low
        quads.append(nn(stack_heads(value_all[:, cut].astype(F32).T, turned, 1), low).T)
    mixed_low = jnp.concatenate(quads, axis=1).astype(LOW)
    mixed[...] = mixed_low
    total = tokens[...].astype(F32) + nn(mixed_low, out_w[...])
    attended[...] = total
    unit, inverse = centre(total)
    inverse_out[...] = jnp.broadcast_to(inverse, inverse_out.shape)
    lifted[...] = (unit * row(gain) + row(bias)).astype(LOW)


def attend(meta, tokens, queries, own, other, key_w, value_w, out_w, gain, bias):
    seqs, span, width = tokens.shape
    pairs = own.shape[0]
    rows = 2 * pairs * own.shape[2]
    tall = (width // HEAD_DIM) * rows
    weight = whole(width, width)
    return call(
        attend_body,
        (seqs,),
        (meta, *kept_far(tokens, queries), own, other, key_w, value_w, out_w, gain, bias),
        [
            far((seqs, rows, width)),
            far((seqs, rows, width)),
            far((seqs, rows, width)),
            far((seqs, tall, span)),
            far((seqs, span, width)),
            far((seqs, span, width), F32),
            shape((seqs, span, width)),
            far((seqs, span, 128), F32),
        ],
        [
            per_seq(rows, width),
            per_seq(rows, width),
            per_seq(rows, width),
            per_seq(tall, span),
            per_seq(span, width),
            per_seq(span, width),
            per_seq(span, width),
            per_seq(span, 128),
        ],
        [
            per_seq(span, width),
            per_seq(span, width),
            distance_spec(pairs, rows, width),
            distance_spec(pairs, rows, width),
            weight,
            weight,
            weight,
            vector(width),
            vector(width),
        ],
        scalars=1,
        limit=32,
        cost=10,
    )


def feed_step(order, lifted, cotangent, grad_active, up, turned, outs):
    active_out, grad_out, down_grad, up_grad = outs
    hidden = nn(lifted[...], up[...])
    share = 0.5 * (1.0 + lax.erf(hidden * 0.5**0.5))
    slope = share + hidden * jnp.exp(-0.5 * hidden * hidden) * 0.3989422804014327
    active = (hidden * share).astype(LOW)
    grad_hidden = (grad_active[...].astype(F32) * slope).astype(LOW)
    active_out[...] = active
    grad_out[...] = grad_hidden
    pieces, line = down_grad.shape[0], down_grad.shape[1]
    value = nn(active.T, cotangent[...])
    for piece in range(pieces):
        down_grad[piece ^ order[1]] = value[piece * line : (piece + 1) * line].astype(LOW)
    value = nn(turned[...], grad_hidden)
    line = up_grad.shape[1]
    for piece in range(pieces):
        up_grad[piece ^ order[2]] = value[piece * line : (piece + 1) * line].astype(LOW)


def feed_body(steps, order, lifted, cotangent, grad_active, up, *refs):
    *outs, turned = refs
    step = pl.program_id(0)

    @pl.when(step == 0)
    def _():
        turned[...] = lifted[...].T

    for at in range(len(outs) // 4):
        pl.when(step // steps == at)(
            functools.partial(
                feed_step, order, lifted, cotangent, grad_active, up, turned, outs[4 * at : 4 * at + 4]
            )
        )


def feed(first, blocks, pieces, order, lifted, cotangent, grad_active, up):
    rows, width = lifted.shape
    steps = width // QUAD

    def columns(i, m):
        return (0, block_at(first + i // steps, m) * steps + i % steps)

    def held(at, i):
        return jnp.clip(i - at * steps, 0, steps - 1)

    out_specs = []
    for at in range(blocks):
        out_specs += [
            pl.BlockSpec((rows, QUAD), lambda i, m, at=at: (0, held(at, i))),
            pl.BlockSpec((rows, QUAD), lambda i, m, at=at: (0, held(at, i))),
            pl.BlockSpec(
                (pieces, None, QUAD // pieces, width), lambda i, m, at=at: (0, held(at, i), 0, 0)
            ),
            pl.BlockSpec((pieces, width // pieces, QUAD), lambda i, m, at=at: (0, 0, held(at, i))),
        ]
    return call(
        functools.partial(feed_body, steps),
        (blocks * steps,),
        (order, lifted, cotangent, grad_active, up),
        [
            far((rows, width)),
            far((rows, width)),
            shape((pieces, steps, QUAD // pieces, width)),
            shape((pieces, width // pieces, width)),
        ]
        * blocks,
        out_specs,
        [
            whole(rows, width),
            whole(rows, width),
            pl.BlockSpec((rows, QUAD), columns),
            pl.BlockSpec((width, QUAD), columns),
        ],
        [pltpu.VMEM((width, rows), LOW)],
        scalars=1,
        limit=20,
        cost=6 * blocks,
    )


def feed_back_body(
    order, hidden_1, hidden_2, hidden_3, hidden_4, up, cotangent, attended, inverse, gain, out_w,
    grad_attended, grad_branch, grad_mixed, norm_grads,
):
    width = cotangent.shape[1]

    @pl.when(pl.program_id(0) == 0)
    def _():
        norm_grads[...] = jnp.zeros_like(norm_grads)

    total = attended[...]
    scale = inverse[:, :1]
    unit = (total - jnp.mean(total, axis=-1, keepdims=True)) * scale
    grad = 0.0
    for at, hidden in enumerate((hidden_1, hidden_2, hidden_3, hidden_4)):
        start = pl.multiple_of(block_at(at, order) * width, width)
        grad += nt(hidden[...], up[:, pl.ds(start, width)])
    norm_grads[0:1, :] += jnp.sum(grad * unit, axis=0, keepdims=True)
    norm_grads[1:2, :] += jnp.sum(grad, axis=0, keepdims=True)
    whole_grad = cotangent[...].astype(F32) + normalize_back(grad, unit, scale, row(gain))
    grad_attended[...] = whole_grad
    branch = whole_grad.astype(LOW)
    grad_branch[...] = branch
    grad_mixed[...] = nt(branch, out_w[...]).astype(LOW)


def feed_back(order, hiddens, up, cotangent, attended, inverse, gain, out_w):
    seqs, span, width = cotangent.shape
    block = per_seq(span, width)
    lines = pl.BlockSpec((span, width), lambda s, *_: (s, 0))
    return call(
        feed_back_body,
        (seqs,),
        (
            order, *kept_far(*hiddens), up, *kept_far(cotangent, attended, inverse), gain, out_w,
        ),
        [
            far((seqs, span, width), F32),
            far((seqs, span, width)),
            far((seqs, span, width)),
            shape((8, width), F32),
        ],
        [block, block, block, result(8, width)],
        [
            *([lines] * len(hiddens)), whole(*up.shape), block, block, per_seq(span, 128),
            vector(width), whole(width, width),
        ],
        scalars=1,
        limit=24,
        cost=8,
    )


def attend_back_body(
    meta, grad_mixed, queries, keys, values, probs, key_w, value_w,
    grad_queries, grad_keys, grad_values, kept, sent, held,
):
    span, width = grad_mixed.shape
    rows = keys.shape[0]
    side = head_masks((rows, QUAD), 1)
    turned = head_masks((QUAD, rows), 0)
    for q in range(width // QUAD):
        cut = slice(q * QUAD, (q + 1) * QUAD)
        mixed_cut = grad_mixed[:, cut]
        tall = len(side) * rows
        low = probs[q * tall : (q + 1) * tall, :]
        grad_probs = nt(stack_heads(values[:, cut], side, 0), mixed_cut)
        lows = []
        for h in range(len(side)):
            part = low[h * rows : (h + 1) * rows].astype(F32)
            ours = grad_probs[h * rows : (h + 1) * rows]
            inner = jnp.sum(part * ours, axis=0, keepdims=True)
            lows.append((part * (ours - inner)).astype(LOW))
        grad_scores = jnp.concatenate(lows, axis=0)
        grad_values[:, cut] = own_heads(nn(low, mixed_cut), side, rows).astype(LOW)
        grad_keys[:, cut] = own_heads(nn(grad_scores, queries[:, cut]), side, rows).astype(LOW)
        keys_turned = stack_heads(keys[:, cut].astype(F32).T, turned, 1)
        grad_queries[:, cut] = (nn(keys_turned, grad_scores) * SCALE).T.astype(LOW)
    grad_summary = nt(grad_keys[...], key_w[...]) + nt(grad_values[...], value_w[...])
    send_by_distance(meta[0], grad_summary, held, kept, sent)


def attend_back(pairs, meta, grad_mixed, queries, keys, values, probs, key_w, value_w):
    seqs, span, width = grad_mixed.shape
    rows = keys.shape[1]
    tall = probs.shape[1]
    weight = whole(width, width)
    block, rows_block = per_seq(span, width), per_seq(rows, width)
    distance = distance_spec(pairs, rows, width)
    return call(
        attend_back_body,
        (seqs,),
        (meta, *kept_far(grad_mixed, queries, keys, values, probs), key_w, value_w),
        [
            far((seqs, span, width)),
            far((seqs, rows, width)),
            far((seqs, rows, width)),
            distance_rows(pairs, seqs, rows, width),
            distance_rows(pairs, seqs, rows, width),
        ],
        [block, rows_block, rows_block, distance, distance],
        [block, block, rows_block, rows_block, per_seq(tall, span), weight, weight],
        [pltpu.VMEM((rows, width), F32)],
        scalars=1,
        limit=24,
        cost=14,
    )


def squares_body(
    order, normed, summary, mixed, grad_queries, grad_keys, grad_values, grad_branch,
    sent_1, sent_2, kept_1, kept_2, normed_t, summary_t, mixed_t,
):
    @pl.when(pl.program_id(0) == 0)
    def _():
        normed_t[...] = normed[...].T
        summary_t[...] = summary[...].T
        mixed_t[...] = mixed[...].T

    pieces = sent_1.shape[0]
    half = normed_t.shape[0] // 2
    members = (
        (normed_t, grad_queries, (sent_1, kept_1), 0, order[1]),
        (summary_t, grad_keys, (sent_1, kept_1), 1, order[1]),
        (summary_t, grad_values, (sent_2, kept_2), 0, order[2]),
        (mixed_t, grad_branch, (sent_2, kept_2), 1, order[2]),
    )
    for left, right, outs, at, mask in members:
        for out, side in zip(outs, (1 - order[0], order[0])):
            start = pl.multiple_of(side * half, half)
            value = nn(left[pl.ds(start, half), :], right[...])
            cut = half // pieces
            for piece in range(pieces):
                out[piece ^ mask, at] = value[piece * cut : (piece + 1) * cut].astype(LOW)


def squares(
    pieces, order, normed, summary, mixed, grad_queries, grad_keys, grad_values, grad_branch
):
    rows, width = normed.shape
    tall = summary.shape[0]
    cut = QUAD
    line = width // 2 // pieces
    return call(
        squares_body,
        (width // cut,),
        (
            order, normed, summary, mixed,
            *kept_far(grad_queries, grad_keys, grad_values, grad_branch),
        ),
        [shape((pieces, 2, line, width))] * 4,
        [pl.BlockSpec((pieces, 2, line, cut), lambda i, m: (0, 0, 0, i))] * 4,
        [
            whole(rows, width),
            whole(tall, width),
            whole(rows, width),
            pl.BlockSpec((rows, cut), lambda i, m: (0, i)),
            pl.BlockSpec((tall, cut), lambda i, m: (0, i)),
            pl.BlockSpec((tall, cut), lambda i, m: (0, i)),
            pl.BlockSpec((rows, cut), lambda i, m: (0, i)),
        ],
        [
            pltpu.VMEM((width, rows), LOW),
            pltpu.VMEM((width, tall), LOW),
            pltpu.VMEM((width, rows), LOW),
        ],
        scalars=1,
        limit=24,
        cost=7,
    )


def place_feed_body(order, *refs):
    inputs, (down, up, total) = refs[:8], refs[8:]
    share, side = pl.program_id(0), pl.program_id(1)
    ours = (side ^ order[0]) == 0

    @pl.when((share == 0) & (side == 0))
    def _():
        total[...] = jnp.zeros_like(total)

    def place(down_in, up_in):
        pieces, steps, line, _ = down_in.shape
        tall = up_in.shape[1]

        def one(piece, square):
            for step in range(steps):
                value = down_in[piece ^ order[1], step].astype(F32)
                start = pl.multiple_of(step * pieces * line + piece * line, line)
                down[pl.ds(start, line), :] = value
                square += jnp.sum(value * value, axis=0, keepdims=True)
            value = up_in[piece ^ order[2]].astype(F32)
            up[pl.ds(pl.multiple_of(piece * tall, tall), tall), :] = value
            return square + jnp.sum(value * value, axis=0, keepdims=True)

        total[0:1, :] += lax.fori_loop(0, pieces, one, jnp.zeros((1, down.shape[1]), F32))

    for at in range(4):
        chosen = (share == at // 2) & (ours if at % 2 == 0 else jnp.logical_not(ours))
        pl.when(chosen)(
            functools.partial(place, inputs[4 * (at // 2) + at % 2], inputs[4 * (at // 2) + 2 + at % 2])
        )


def place_feed(order, down_shape, up_shape, *arrays):
    width = down_shape[1]
    return call(
        place_feed_body,
        (2, 2),
        (order, *arrays),
        [shape(down_shape, F32), shape(up_shape, F32), shape((8, width), F32)],
        [
            pl.BlockSpec((width, width), lambda h, i, m: (2 * h + i, 0)),
            pl.BlockSpec((width, width), lambda h, i, m: (0, 2 * h + i)),
            result(8, width),
        ],
        [whole(*x.shape) for x in arrays],
        scalars=1,
        limit=28,
        cost=8,
    )


def place_squares_body(order, own_1, other_1, own_2, other_2, others, norms, *refs):
    *outs, norm, total = refs
    side = pl.program_id(0)
    ours = (side ^ order[0]) == 0

    @pl.when(side == 0)
    def _():
        total[...] = others[...]

    def place(first, second):
        pieces, _, line, _ = first.shape

        def one(piece, square):
            for source, mask, pair in ((first, order[1], outs[:2]), (second, order[2], outs[2:])):
                for at, out in enumerate(pair):
                    value = source[piece ^ mask, at].astype(F32)
                    out[pl.ds(pl.multiple_of(piece * line, line), line), :] = value
                    square += jnp.sum(value * value, axis=0, keepdims=True)
            return square

        total[0:1, :] += lax.fori_loop(0, pieces, one, jnp.zeros((1, outs[0].shape[1]), F32))

    pl.when(ours)(lambda: place(own_1, own_2))
    pl.when(jnp.logical_not(ours))(lambda: place(other_1, other_2))

    @pl.when(side == 1)
    def _():
        square = jnp.sum(total[0:1, :], keepdims=True) + jnp.sum(
            norms[...] * norms[...], keepdims=True
        )
        norm[...] = jnp.sqrt(square)


def place_squares(order, own_1, other_1, own_2, other_2, others, norms):
    pieces, _, line, width = own_1.shape
    arrays = (own_1, other_1, own_2, other_2, others, norms)
    return call(
        place_squares_body,
        (2,),
        (order, *arrays),
        [shape((2 * pieces * line, width), F32)] * 4 + [shape((1, 1), F32)],
        [pl.BlockSpec((pieces * line, width), lambda i, m: (i, 0))] * 4 + [result(1, 1)],
        [whole(*x.shape) for x in arrays],
        [pltpu.VMEM(others.shape, F32)],
        scalars=1,
        limit=24,
        cost=5,
    )


def leave_body(
    meta, own, other, columns, normed, tokens, gain, grad_queries, query_w, grad_attended,
    tokens_grad, terms, norm_grads, columns_t, terms_sum, grad_summary,
):
    seq = pl.program_id(0)
    rows, span = columns.shape

    @pl.when(seq == 0)
    def _():
        columns_t[...] = columns[...].T
        terms_sum[...] = jnp.zeros_like(terms_sum)
        norm_grads[...] = jnp.zeros_like(norm_grads)

    take_by_distance(meta[0], own, other, grad_summary)
    length = meta[1 + seq] - meta[0] * span
    lane = lax.broadcasted_iota(jnp.int32, (rows, span), 1) < length
    line = lax.broadcasted_iota(jnp.int32, (span, 1), 0) < length
    summed = grad_summary[...]
    terms_sum[...] += jnp.where(lane, nt(summed, normed[...]), 0.0)
    grad = nt(grad_queries[...], query_w[...]) + jnp.where(line, nn(columns_t[...], summed), 0.0)
    unit, inverse = centre(tokens[...].astype(F32))
    norm_grads[0:1, :] += jnp.sum(grad * unit, axis=0, keepdims=True)
    norm_grads[1:2, :] += jnp.sum(grad, axis=0, keepdims=True)
    tokens_grad[...] = (
        grad_attended[...] + normalize_back(grad, unit, inverse, row(gain))
    ).astype(LOW)

    @pl.when(seq == pl.num_programs(0) - 1)
    def _():
        terms[...] = terms_sum[...].astype(LOW)


def leave(
    meta, own, other, columns, normed, tokens, gain, grad_queries, query_w, grad_attended
):
    seqs, span, width = tokens.shape
    rows = columns.shape[0]
    distance = distance_spec(own.shape[0], rows, width)
    block = per_seq(span, width)
    return call(
        leave_body,
        (seqs,),
        (
            meta, own, other, columns, *kept_far(normed, tokens), gain, *kept_far(grad_queries), query_w,
            *kept_far(grad_attended),
        ),
        [shape(tokens.shape), shape((rows, span)), shape((8, width), F32)],
        [block, result(rows, span), result(8, width)],
        [
            distance, distance, whole(rows, span), block, block, vector(width), block,
            whole(width, width), block,
        ],
        [
            pltpu.VMEM((span, rows), LOW),
            pltpu.VMEM((rows, span), F32),
            pltpu.VMEM((rows, width), LOW),
        ],
        scalars=1,
        limit=20,
        cost=5,
    )


def swap(value, axis, mask):
    size = lax.axis_size(axis)
    return lax.ppermute(value, axis, [(i, i ^ mask) for i in range(size)])


def pick(value, at):
    return lax.dynamic_index_in_dim(value, at, 0, keepdims=False)


def bits_of(axis):
    return (lax.axis_size(axis) - 1).bit_length()


def bit(axis, at):
    return (lax.axis_index(axis) >> at) & 1


def after(values, ticket):
    return lax.optimization_barrier((values, ticket))[0]


def in_order(mine, other, at):
    return jnp.where(at == 0, jnp.stack([mine, other]), jnp.stack([other, mine]))


def krow_orders():
    count = bits_of("krow")
    return [list(range(1, count)), list(range(count - 1, 0, -1))]


def distance_masks():
    count = bits_of("krow")
    masks = [bit("krow", 0)]
    for order in krow_orders():
        masks.append(sum(bit("krow", at) << (count - 2 - d) for d, at in enumerate(order)))
    return jnp.stack(masks).astype(jnp.int32)


def sum_everywhere(sent, halved):
    orders = krow_orders()
    flight = [swap(x, "krow", 1) for x in sent]
    kept = yield sent
    ticket = yield kept
    for digit in range(len(orders[0])):
        flight, kept = after((flight, kept), ticket)
        half = kept[0].shape[0] // 2
        sent = [k[half:] + f[half:] for k, f in zip(kept, flight)]
        kept = [k[:half] + f[:half] for k, f in zip(kept, flight)]
        flight = [swap(x, "krow", 1 << o[digit]) for x, o in zip(sent, orders)]
        ticket = yield (sent, kept)
    flight, kept = after((flight, kept), ticket)
    value = jnp.concatenate([k + f for k, f in zip(kept, flight)])
    split = []
    for at in range(bits_of("dp")):
        if at < halved:
            half = value.reshape(2, -1, value.shape[-1])
            mine = bit("dp", at)
            sent, kept = pick(half, 1 - mine), pick(half, mine)
            split.append((at, mine))
        else:
            sent = kept = value
        flight = swap(sent, "dp", 1 << at)
        ticket = yield (sent, kept)
        flight, kept = after((flight, kept), ticket)
        value = kept + flight
    for at, mine in reversed(split):
        flight = swap(value, "dp", 1 << at)
        ticket = yield value
        flight, value = after((flight, value), ticket)
        value = in_order(value, flight, mine).reshape(-1, value.shape[-1])
    values = list(value.reshape(2, 1, -1, value.shape[-1]))
    for digit in reversed(range(len(orders[0]))):
        flight = [swap(v, "krow", 1 << o[digit]) for v, o in zip(values, orders)]
        ticket = yield values
        flight, values = after((flight, values), ticket)
        values = [jnp.concatenate([v, f]) for v, f in zip(values, flight)]
    flight = [swap(v, "krow", 1) for v in values]
    ticket = yield values
    yield after([x for pair in zip(values, flight) for x in pair], ticket)


def sum_krow(sent, kept):
    pairs = kept.shape[0]
    flight = swap(sent, "krow", 1)
    ticket = yield kept
    kept, flight = after((kept, flight), ticket)
    half = [k.astype(F32) + f.astype(F32) for k, f in zip(kept, flight)]
    sent = [h.astype(LOW) for h in half[1:]]
    flight = [swap(x, "krow", 2 * pair) for pair, x in enumerate(sent, 1)]
    kept = half[0]
    ticket = yield (kept, sent)
    kept, flight = after((kept, flight), ticket)
    total = sum([f.astype(F32) for f in flight], kept).astype(LOW)
    flight = [swap(total, "krow", 2 * pair) for pair in range(1, pairs)]
    ticket = yield total
    total, flight = after((total, flight), ticket)
    own = jnp.stack([total, *flight])
    flight = swap(own, "krow", 1)
    ticket = yield own
    yield after((own, flight), ticket)


def sum_small(value):
    for axis in ("krow", "dp"):
        for at in range(bits_of(axis)):
            flight = swap(value, axis, 1 << at)
            ticket = yield value
            flight, value = after((flight, value), ticket)
            value = value + flight
    yield value


def sum_terms(terms, ring):
    rows, span = terms.shape
    value = lax.all_to_all(
        terms.reshape(ring, rows // ring, span), "krow", 0, 1, tiled=False
    ).reshape(rows // ring, ring * span)
    ticket = yield terms
    value = after(value, ticket)
    for at in range(bits_of("dp")):
        flight = swap(value, "dp", 1 << at)
        ticket = yield value
        flight, value = after((flight, value), ticket)
        value = value + flight
    yield value


class Line:
    def __init__(self, ticket):
        self.ticket = ticket

    def step(self, *sums):
        for each in sums:
            self.ticket = each.send(self.ticket)

    def run(self, kernel, *values):
        self.ticket = kernel(*after(values, self.ticket))
        return self.ticket


    def start(self, steps, *first):
        self.ticket = (self.ticket, next(steps))
        for value in first:
            self.ticket = (self.ticket, steps.send(value))
        return steps


PLAN = "S1KF212A1Bg1Q3g12312g1O32g1gL2312c32c3n2n31c32n132nP3ncn3"
HALVED = {"1": 2, "2": 2, "3": 2}


def local(
    tokens,
    lengths,
    attn_gain,
    attn_bias,
    query_weight,
    key_weight,
    value_weight,
    out_weight,
    compress,
    ffn_gain,
    ffn_bias,
    up_weight,
    down_weight,
    cotangent,
):
    seqs, span, width = tokens.shape
    ring = lax.axis_size("krow")
    rows = compress.shape[0] * ring
    pairs = pieces = ring // 2
    flat, tall = (seqs * span, width), (seqs * rows, width)
    order = distance_masks()
    meta = jnp.concatenate([lax.axis_index("krow")[None].astype(jnp.int32), lengths])
    columns = lax.all_to_all(
        compress.reshape(compress.shape[0], ring, span), "krow", 1, 0, tiled=False
    ).reshape(rows, span)
    cotangent_flat = cotangent.reshape(flat)
    normed = enter(tokens, attn_gain, attn_bias)
    kept, sent = summarize(pairs, meta, columns, normed)
    line = Line((kept, sent))
    summing = line.start(sum_krow(sent, kept))
    line.step(summing)
    grad_active = line.run(grad_active_of, cotangent_flat, down_weight)
    line.step(summing)
    queries = line.run(project, normed, query_weight)
    line.step(summing, summing)
    summary, keys, values, probs, mixed, attended, lifted, inverse = attend(
        meta, tokens, queries, *line.ticket, key_weight, value_weight, out_weight, ffn_gain,
        ffn_bias,
    )
    line.ticket = lifted

    def as_pieces(arrays):
        return [x.reshape(pieces, -1, width) for x in arrays]

    known, sums, results = {}, {}, {}

    def feed_blocks(first, blocks):
        return line.run(
            lambda lifted: feed(
                first, blocks, pieces, order, lifted.reshape(flat), cotangent_flat, grad_active,
                up_weight,
            ),
            lifted,
        )

    def run_s():
        known["active_1"], known["hidden_1"], *known["sent_1"] = feed_blocks(0, 1)

    def run_k():
        known["active_2"], known["hidden_2"], *known["kept_1"] = feed_blocks(1, 1)

    def run_f():
        out = feed_blocks(2, 2)
        known["active_3"], known["hidden_3"], *known["sent_2"] = out[:4]
        known["active_4"], known["hidden_4"], *known["kept_2"] = out[4:]

    def run_a():
        known["grad_attended"], known["grad_branch"], known["grad_mixed"], known["ffn_norms"] = (
            line.run(
                lambda *hiddens: feed_back(
                    order, hiddens, up_weight, cotangent, attended, inverse, ffn_gain, out_weight
                ),
                *(known[f"hidden_{at}"] for at in range(1, 5)),
            )
        )

    def run_b():
        *known["grads"], known["kept_g"], known["sent_g"] = line.run(
            lambda grad_mixed: attend_back(
                pairs, meta, grad_mixed, queries, keys, values, probs, key_weight, value_weight
            ),
            known["grad_mixed"],
        )

    def run_q():
        out = line.run(
            lambda branch, grad_queries, grad_keys, grad_values: squares(
                pieces, order, normed.reshape(flat), summary.reshape(tall), mixed.reshape(flat),
                grad_queries.reshape(flat), grad_keys.reshape(tall), grad_values.reshape(tall),
                branch.reshape(flat),
            ),
            known["grad_branch"],
            *known["grads"],
        )
        known["sent_3"], known["kept_3"] = out[:2], out[2:]

    def run_o():
        known["block_out"] = line.run(
            lambda *actives: block_out_of(order, down_weight, attended, *actives),
            *(known[f"active_{at}"] for at in range(1, 5)),
        )

    def run_l():
        finish("g")
        known["tokens_grad"], known["terms"], attn_norms = line.run(
            lambda own, other: leave(
                meta, own, other, columns, normed, tokens, attn_gain, known["grads"][0],
                query_weight, known["grad_attended"],
            ),
            *results["g"],
        )
        known["norms"] = jnp.concatenate([attn_norms[:2], known["ffn_norms"][:2]])

    def run_p():
        finish("1")
        finish("2")
        form = (pieces, width // QUAD, QUAD // pieces, width)
        arrays = [
            x.reshape(form) if at % 4 < 2 else x
            for at, x in enumerate((*results["1"], *results["2"]))
        ]
        known["feed"] = line.run(
            lambda *arrays: place_feed(order, down_weight.shape, up_weight.shape, *arrays),
            *arrays,
        )

    def begin(name):
        if name == "g":
            return sum_krow(known["sent_g"], known["kept_g"])
        if name == "n":
            return sum_small(known["norms"])
        if name == "c":
            return sum_terms(known["terms"], ring)
        return sum_everywhere(as_pieces(known[f"sent_{name}"]), HALVED[name])

    def advance(name):
        if name not in sums:
            sums[name] = [begin(name), 0]
            line.start(sums[name][0])
        else:
            if sums[name][1] == 1 and name in HALVED:
                sums[name][0].send(as_pieces(known[f"kept_{name}"]))
            try:
                line.step(sums[name][0])
                results[name] = line.ticket
            except StopIteration:
                return False
        sums[name][1] += 1
        return True

    def finish(name):
        while advance(name):
            pass

    kernels = {
        "S": run_s, "K": run_k, "F": run_f, "A": run_a, "B": run_b, "Q": run_q, "O": run_o,
        "L": run_l, "P": run_p,
    }
    for name in PLAN:
        if name in kernels:
            kernels[name]()
        else:
            advance(name)
    for name in "nc3":
        finish(name)
    down_grad, up_grad, others = known["feed"]
    arrays = [x.reshape(pieces, 2, -1, width) for x in results["3"]]
    norms, compress_grad = results["n"], results["c"]
    *attn_grads, grad_norm = place_squares(order, *arrays, others, norms)
    block_out, tokens_grad = known["block_out"], known["tokens_grad"]
    return (
        block_out,
        tokens_grad,
        norms[0],
        norms[1],
        *attn_grads,
        compress_grad.astype(F32),
        norms[2],
        norms[3],
        up_grad,
        down_grad,
        grad_norm.reshape(()),
    )


def solution(mesh):
    rows, held = P("dp", "krow", None), P("krow", None)
    in_specs = (rows, P("dp"), P(), P(), P(), P(), P(), P(), held, P(), P(), P(), P(), rows)
    out_specs = (rows, rows, P(), P(), P(), P(), P(), P(), held, P(), P(), P(), P(), P())
    return jax.shard_map(local, mesh=mesh, in_specs=in_specs, out_specs=out_specs, check_vma=False)
```

profile of v0, /device:TPU:0, one launch (start us, length us, event | category | flops | bytes accessed | tf_op | source)
XLA Modules:
  0.0 300.9 jit_solution(6402819495301055465)
XLA Ops:
  2.3 5.2 %all-to-all-start = ((bf16[1,32,8,256]{3,1,0,2:T(8,128)(2,1)}), bf16[1,32,8,256]{3,1,0,2:T(8,128)(2,1)S(1)}, u32[]{:S(2)}, u32[]{:S(2)}) async-start(bf16[1,32,8,256]{3,1,0,2:T(8,128)(2,1)} %copy.31), calls=%async_computation | async-start | bytes 262144 | tf_op jit(solution)/shard_map/all_to_all | solution.py:927
  10.1 2.1 shard_map.245.normed
  16.1 2.0 collective-permute-done
  21.8 5.9 %shard_map.247.grad_active = bf16[768,3072]{1,0:T(8,128)(2,1)} custom-call(bf16[768,768]{1,0:T(8,128)(2,1)S(1)} %bitcast.134, bf16[3072,768]{1,0:T(8,128)(2,1)S(1)} %bitcast.131), custom_call_target="tpu_custom_call" | custom-call | flops 5000000000 | bytes 1 | tf_op jit(solution)/shard_map/pallas_call | solution.py:62
  32.1 2.5 shard_map.248.queries
  34.9 2.9 collective-permute-done.5
  38.1 1.9 collective-permute-done.7.other
  42.5 11.5 %shard_map.249 = (bf16[3,256,768]{2,1,0:T(8,128)(2,1)}, bf16[3,256,768]{2,1,0:T(8,128)(2,1)}, bf16[3,256,768]{2,1,0:T(8,128)(2,1)}, bf16[3,3072,256]{2,1,0:T(8,1...) custom-call(s32[4]{0:T(128)S(1)} %pad_add_fusion.1.meta, ...), custom_call_target="tpu_custom_call" | custom-call | flops 10000000000 | bytes 1 | tf_op jit(solution)/shard_map/pallas_call | solution.py:62
  54.1 6.7 %shard_map.250 = (bf16[768,768]{1,0:T(8,128)(2,1)}, bf16[768,768]{1,0:T(8,128)(2,1)}, bf16[4,3,64,768]{3,2,1,0:T(8,128)(2,1)}, bf16[4,192,768]{2,1,0:T(8,128)(2,1)}) custom-call(s32[3]{0:T(128)S(1)} %pad_add_fusion.order, bf16[768,768]{1,0:T(8,128)(2,1)S(1)} %bitcast.145, bf16[768,768]{1,0:T(8,128)(2,1)S(1)} %bitcast.135, bf16[768,3072]{1,0:T(8,128)(2,1)S(1)} %copy-done.25, ...), custom_call_target="tpu_custom_call" | custom-call | flops 6000000000 | bytes 1 | tf_op jit(solution)/shard_map/pallas_call | solution.py:62
  61.3 6.7 %shard_map.251 = (bf16[768,768]{1,0:T(8,128)(2,1)}, bf16[768,768]{1,0:T(8,128)(2,1)}, bf16[4,3,64,768]{3,2,1,0:T(8,128)(2,1)S(1)}, bf16[4,192,768]{2,1,0:T(8,128)(2,1)S(1)}) custom-call(s32[3]{0:T(128)S(1)} %pad_add_fusion.order, bf16[768,768]{1,0:T(8,128)(2,1)S(1)} %bitcast.146, bf16[768,768]{1,0:T(8,128)(2,1)S(1)} %bitcast.136, ...), custom_call_target="tpu_custom_call" | custom-call | flops 6000000000 | bytes 1 | tf_op jit(solution)/shard_map/pallas_call | solution.py:62
  69.0 12.1 %shard_map.252 = (bf16[768,768]{1,0:T(8,128)(2,1)}, bf16[768,768]{1,0:T(8,128)(2,1)}, bf16[4,3,64,768]{3,2,1,0:T(8,128)(2,1)}, bf16[4,192,768]{2,1,0:T(8,128)(2,...) custom-call(s32[3]{0:T(128)S(1)} %pad_add_fusion.order, ...), custom_call_target="tpu_custom_call" | custom-call | flops 12000000000 | bytes 1 | tf_op jit(solution)/shard_map/pallas_call | solution.py:62
  81.6 1.7 slice_add_fusion.8
  86.9 2.4 slice_add_fusion.4
  89.3 2.5 slice_add_fusion.5
  91.8 2.3 copy-done.3
  94.1 11.2 %shard_map.253 = (f32[3,256,768]{2,1,0:T(8,128)}, bf16[3,256,768]{2,1,0:T(8,128)(2,1)}, bf16[3,256,768]{2,1,0:T(8,128)(2,1)}, f32[8,768]{1,0:T(8,128)S(1)}) custom-call(s32[3]{0:T(128)S(1)} %pad_add_fusion.order, bf16[768,768]{1,0:T(8,128)(2,1)} %get-tuple-element.276.hidden_1, bf16[768,768]{1,0:T(8,128)(2,1)} %get-tuple-element.277.hidden_2, ...), custom_call_target="tpu_custom_call" | custom-call | flops 8000000000 | bytes 1 | tf_op jit(solution)/shard_map/pallas_call | solution.py:62
  107.7 11.8 %shard_map.254 = (bf16[3,256,768]{2,1,0:T(8,128)(2,1)}, bf16[3,256,768]{2,1,0:T(8,128)(2,1)}, bf16[3,256,768]{2,1,0:T(8,128)(2,1)}, bf16[4,3,32,768]{3,2,1,0:T(8,128)(2,1)S(1)}, bf16[4,3,32,768]{3,2,1,0:T(8,128)(2,1)S(1)}) custom-call(s32[4]{0:T(128)S(1)} %pad_add_fusion.1.meta, bf16[3,256,768]{2,1,0:T(8,128)(2,1)} %get-tuple-element.289.grad_mixed, ...), custom_call_target="tpu_custom_call" | custom-call | flops 14000000000 | bytes 1 | tf_op jit(solution)/shard_map/pallas_call | solution.py:62
  121.4 8.0 %shard_map.255 = (bf16[4,2,96,768]{3,2,1,0:T(8,128)(2,1)}, bf16[4,2,96,768]{3,2,1,0:T(8,128)(2,1)}, bf16[4,2,96,768]{3,2,1,0:T(8,128)(2,1)S(1)}, bf16[4,2,96,768]{3,2,1,0:T(8,128)(2,1)S(1)}) custom-call(s32[3]{0:T(128)S(1)} %pad_add_fusion.order, bf16[768,768]{1,0:T(8,128)(2,1)S(1)} %bitcast.142, bf16[768,768]{1,0:T(8,128)(2,1)S(1)} %bitcast.143, ...), custom_call_target="tpu_custom_call" | custom-call | flops 7000000000 | bytes 1 | tf_op jit(solution)/shard_map/pallas_call | solution.py:62
  134.8 6.3 %collective-permute-done.16 = bf16[192,768]{1,0:T(8,128)(2,1)} collective-permute-done((bf16[192,768]{1,0:T(8,128)(2,1)}, bf16[192,768]{1,0:T(8,128)(2,1)}, u32[]{:S(2)}, u32[]{:S(2)}) %collective-permute-start.16) | collective-permute-done | bytes 294944 | tf_op jit(solution)/shard_map/ppermute | solution.py:755
  143.3 2.6 collective-permute-done.22
  147.5 2.6 collective-permute-start.18
  158.9 2.6 collective-permute-done.28
  162.5 2.3 collective-permute-done.27
  169.3 3.2 %collective-permute-done.23 = bf16[96,768]{1,0:T(8,128)(2,1)S(1)} collective-permute-done((bf16[96,768]{1,0:T(8,128)(2,1)S(1)}, bf16[96,768]{1,0:T(8,128)(2,1)S(1)}, u32[]{:S(2)}, u32[]{:S(2)}) %collective-permute-start.23) | collective-permute-done | bytes 147488 | tf_op jit(solution)/shard_map/ppermute | solution.py:755
  173.3 7.4 %shard_map.256 = bf16[3,256,768]{2,1,0:T(8,128)(2,1)} custom-call(s32[3]{0:T(128)S(1)} %pad_add_fusion.order, bf16[3072,768]{1,0:T(8,128)(2,1)S(1)} %bitcast.133, f32[3,256,768]{2,1,0:T(8,128)} %get-tuple-element.247.attended, bf16[768,768]{1,0:T(8,128)(2,1)} %get-tuple-element.336.refs_0_, bf16[768,768]{1,0:T(8,128)(2,1)} %get-tuple-element.337.refs_1_, ...), custom_call_target="tpu_custom_call" | custom-call | flops 6000000000 | bytes 1 | tf_op jit(solution)/shard_map/pallas_call | solution.py:62
  180.7 2.5 collective-permute-start.31
  185.1 1.6 collective-permute-done.31
  193.4 6.7 %shard_map.257 = (bf16[3,256,768]{2,1,0:T(8,128)(2,1)}, bf16[256,256]{1,0:T(8,128)(2,1)}, f32[8,768]{1,0:T(8,128)S(1)}) custom-call(s32[4]{0:T(128)S(1)} %pad_add_fusion.1.meta, bf16[4,3,32,768]{3,2,1,0:T(8,128)(2,1)S(1)} %pad_maximum_fusion.1.own, bf16[4,3,32,768]{3,2,1,0:T(8,128)(2,1)S(1)} %collective-permute-done.35.other, ...), custom_call_target="tpu_custom_call" | custom-call | flops 5000000000 | bytes 1 | tf_op jit(solution)/shard_map/pallas_call | solution.py:62
  200.1 2.4 collective-permute-start.39
  204.7 4.5 %collective-permute-done.39 = bf16[96,768]{1,0:T(8,128)(2,1)S(1)} collective-permute-done((bf16[96,768]{1,0:T(8,128)(2,1)S(1)}, bf16[96,768]{1,0:T(8,128)(2,1)S(1)}, u32[]{:S(2)}, u32[]{:S(2)}) %collective-permute-start.39) | collective-permute-done | bytes 147488 | tf_op jit(solution)/shard_map/ppermute | solution.py:755
  209.2 5.2 %collective-permute-done.45 = bf16[192,768]{1,0:T(8,128)(2,1)S(1)} collective-permute-done((bf16[192,768]{1,0:T(8,128)(2,1)S(1)}, bf16[192,768]{1,0:T(8,128)(2,1)S(1)}, u32[]{:S(2)}, u32[]{:S(2)}) %collective-permute-start.45) | collective-permute-done | bytes 294944 | tf_op jit(solution)/shard_map/ppermute | solution.py:755
  214.6 4.8 %collective-permute-done.44 = bf16[192,768]{1,0:T(8,128)(2,1)S(1)} collective-permute-done((bf16[192,768]{1,0:T(8,128)(2,1)S(1)}, bf16[192,768]{1,0:T(8,128)(2,1)S(1)}, u32[]{:S(2)}, u32[]{:S(2)}) %collective-permute-start.44) | collective-permute-done | bytes 294944 | tf_op jit(solution)/shard_map/ppermute | solution.py:755
  222.8 3.4 %all-to-all-start.1 = ((bf16[8,32,1,256]{3,1,2,0:T(8,128)(2,1)}), bf16[8,32,1,256]{3,1,2,0:T(8,128)(2,1)S(1)}, u32[]{:S(2)}, u32[]{:S(2)}) async-start(bf16[8,32,1,256]{3,1,2,0:T(8,128)(2,1)} %bitcast.70), calls=%async_computation.1 | async-start | bytes 262144 | tf_op jit(solution)/shard_map/all_to_all | solution.py:867
  226.2 2.0 collective-permute-start.56
  229.7 2.4 all-to-all-done.1
  233.7 1.8 collective-permute-start.52
  237.9 5.9 %collective-permute-done.52 = bf16[96,768]{1,0:T(8,128)(2,1)S(1)} collective-permute-done((bf16[96,768]{1,0:T(8,128)(2,1)S(1)}, bf16[96,768]{1,0:T(8,128)(2,1)S(1)}, u32[]{:S(2)}, u32[]{:S(2)}) %collective-permute-start.52) | collective-permute-done | bytes 147488 | tf_op jit(solution)/shard_map/ppermute | solution.py:755
  247.3 4.7 %collective-permute-done.53 = bf16[192,768]{1,0:T(8,128)(2,1)S(1)} collective-permute-done((bf16[192,768]{1,0:T(8,128)(2,1)S(1)}, bf16[192,768]{1,0:T(8,128)(2,1)S(1)}, u32[]{:S(2)}, u32[]{:S(2)}) %collective-permute-start.53) | collective-permute-done | bytes 294944 | tf_op jit(solution)/shard_map/ppermute | solution.py:755
  252.2 3.8 %collective-permute-done.51 = bf16[2,192,768]{2,1,0:T(8,128)(2,1)S(1)} collective-permute-done((bf16[2,192,768]{2,1,0:T(8,128)(2,1)S(1)}, bf16[2,192,768]{2,1,0:T(8,128)(2,1)S(1)}, u32[]{:S(2)}, u32[]{:S(2)}) %collective-permute-start.51) | collective-permute-done | bytes 589856 | tf_op jit(solution)/shard_map/ppermute | solution.py:755
  258.3 2.2 collective-permute-done.49
  264.1 4.4 %collective-permute-done.60 = bf16[1,192,768]{2,1,0:T(8,128)(2,1)S(1)} collective-permute-done((bf16[1,192,768]{2,1,0:T(8,128)(2,1)S(1)}, bf16[1,192,768]{2,1,0:T(8,128)(2,1)S(1)}, u32[]{:S(2)}, u32[]{:S(2)}) %collective-permute-start.60) | collective-permute-done | bytes 294944 | tf_op jit(solution)/shard_map/ppermute | solution.py:755
  271.8 7.5 %shard_map.258 = (f32[3072,768]{1,0:T(8,128)}, f32[768,3072]{1,0:T(8,128)}, f32[8,768]{1,0:T(8,128)S(1)}) custom-call(s32[3]{0:T(128)S(1)} %pad_add_fusion.order, bf16[4,3,64,768]{3,2,1,0:T(8,128)(2,1)S(1)} %bitcast.122, bf16[4,3,64,768]{3,2,1,0:T(8,128)(2,1)S(1)} %bitcast.138, bf16[4,192,768]{2,1,0:T(8,128)(2,1)S(1)} %constant_dynamic-update-slice_fusion.10.refs_2_, ...), custom_call_target="tpu_custom_call" | custom-call | flops 8000000000 | bytes 1 | tf_op jit(solution)/shard_map/pallas_call | solution.py:62
  279.4 3.3 %collective-permute-done.66 = bf16[2,192,768]{2,1,0:T(8,128)(2,1)S(1)} collective-permute-done((bf16[2,192,768]{2,1,0:T(8,128)(2,1)S(1)}, bf16[2,192,768]{2,1,0:T(8,128)(2,1)S(1)}, u32[]{:S(2)}, u32[]{:S(2)}) %collective-permute-start.66) | collective-permute-done | bytes 589856 | tf_op jit(solution)/shard_map/ppermute | solution.py:755
  283.9 2.7 collective-permute-start.68
  286.5 2.8 collective-permute-start.64
  289.3 1.7 collective-permute-done.64
  291.0 2.4 collective-permute-start.67
  296.2 4.6 %shard_map.259 = (f32[768,768]{1,0:T(8,128)}, f32[768,768]{1,0:T(8,128)}, f32[768,768]{1,0:T(8,128)}, f32[768,768]{1,0:T(8,128)}, f32[1,1]{1,0:T(1,128)}) custom-call(s32[3]{0:T(128)S(1)} %pad_add_fusion.order, bf16[4,2,96,768]{3,2,1,0:T(8,128)(2,1)S(1)} %bitcast.125, bf16[4,2,96,768]{3,2,1,0:T(8,128)(2,1)S(1)} %bitcast.141, ...), custom_call_target="tpu_custom_call" | custom-call | flops 5000000000 | bytes 1 | tf_op jit(solution)/shard_map/pallas_call | solution.py:62
  (273 shorter events, 89.6 us)
Async XLA Ops:
  2.3 10.7 %all-to-all-start = ((bf16[1,32,8,256]{3,1,0,2:T(8,128)(2,1)}), bf16[1,32,8,256]{3,1,0,2:T(8,128)(2,1)S(1)}, u32[]{:S(2)}, u32[]{:S(2)}) async-start(bf16[1,32,8,256]{3,1,0,2:T(8,128)(2,1)} %copy.31), calls=%async_computation | async-start | bytes 262144 | tf_op jit(solution)/shard_map/all_to_all | solution.py:927
  18.2 9.5 %collective-permute-start.1 = (bf16[3,32,768]{2,1,0:T(8,128)(2,1)S(1)}, bf16[3,32,768]{2,1,0:T(8,128)(2,1)S(1)}, u32[]{:S(2)}, u32[]{:S(2)}) collective-permute-start(bf16[3,32,768]{2,1,0:T(8,128)(2,1)S(1)} %get-tuple-element.480), channel_id=1, source_target_pairs={{0,2},{1,3},{2,0},{3,1},{4,6},{5,7},{6,4},{7,5},{8,10},{9,11},{10,... | collective-permute-start | bytes 442376 | tf_op jit(solution)/shard_map/ppermute | solution.py:755
  60.8 20.8 %collective-permute-start.8 = (bf16[4,192,768]{2,1,0:T(8,128)(2,1)}, bf16[4,192,768]{2,1,0:T(8,128)(2,1)}, u32[]{:S(2)}, u32[]{:S(2)}) collective-permute-start(bf16[4,192,768]{2,1,0:T(8,128)(2,1)} %bitcast.17), channel_id=1, source_target_pairs={{0,1},{1,0},{2,3},{3,2},{4,5},{5,4},{6,7},{7,6},{8,9},{9,8},{10,11... | collective-permute-start | bytes 3538952 | tf_op jit(solution)/shard_map/ppermute | solution.py:755
  61.0 20.7 %collective-permute-start.9 = (bf16[4,192,768]{2,1,0:T(8,128)(2,1)}, bf16[4,192,768]{2,1,0:T(8,128)(2,1)}, u32[]{:S(2)}, u32[]{:S(2)}) collective-permute-start(bf16[4,192,768]{2,1,0:T(8,128)(2,1)} %get-tuple-element.253), channel_id=1, source_target_pairs={{0,1},{1,0},{2,3},{3,2},{4,5},{5,4},{6,7},{7,6},{8,9},{9,8},{10,11... | collective-permute-start | bytes 3538952 | tf_op jit(solution)/shard_map/ppermute | solution.py:755
  83.3 22.0 %collective-permute-start.11 = (bf16[2,192,768]{2,1,0:T(8,128)(2,1)S(1)}, bf16[2,192,768]{2,1,0:T(8,128)(2,1)S(1)}, u32[]{:S(2)}, u32[]{:S(2)}) collective-permute-start(bf16[2,192,768]{2,1,0:T(8,128)(2,1)S(1)} %get-tuple-element.459), channel_id=1, source_target_pairs={{0,4},{1,5},{2,6},{3,7},{4,0},{5,1},{6,2},{7,3},{8,12},{9,13},{10,... | collective-permute-start | bytes 1769480 | tf_op jit(solution)/shard_map/ppermute | solution.py:755
  85.8 19.5 %collective-permute-start.10 = (bf16[2,192,768]{2,1,0:T(8,128)(2,1)S(1)}, bf16[2,192,768]{2,1,0:T(8,128)(2,1)S(1)}, u32[]{:S(2)}, u32[]{:S(2)}) collective-permute-start(bf16[2,192,768]{2,1,0:T(8,128)(2,1)S(1)} %get-tuple-element.461), channel_id=1, source_target_pairs={{0,2},{1,3},{2,0},{3,1},{4,6},{5,7},{6,4},{7,5},{8,10},{9,11},{10,... | collective-permute-start | bytes 1769480 | tf_op jit(solution)/shard_map/ppermute | solution.py:755
  105.4 14.1 %collective-permute-start.15 = (bf16[1,192,768]{2,1,0:T(8,128)(2,1)S(1)}, bf16[1,192,768]{2,1,0:T(8,128)(2,1)S(1)}, u32[]{:S(2)}, u32[]{:S(2)}) collective-permute-start(bf16[1,192,768]{2,1,0:T(8,128)(2,1)S(1)} %get-tuple-element.475), channel_id=1, source_target_pairs={{0,2},{1,3},{2,0},{3,1},{4,6},{5,7},{6,4},{7,5},{8,10},{9,11},{10,... | collective-permute-start | bytes 884744 | tf_op jit(solution)/shard_map/ppermute | solution.py:755
  106.6 12.9 %collective-permute-start.14 = (bf16[1,192,768]{2,1,0:T(8,128)(2,1)S(1)}, bf16[1,192,768]{2,1,0:T(8,128)(2,1)S(1)}, u32[]{:S(2)}, u32[]{:S(2)}) collective-permute-start(bf16[1,192,768]{2,1,0:T(8,128)(2,1)S(1)} %get-tuple-element.477), channel_id=1, source_target_pairs={{0,4},{1,5},{2,6},{3,7},{4,0},{5,1},{6,2},{7,3},{8,12},{9,13},{10,... | collective-permute-start | bytes 884744 | tf_op jit(solution)/shard_map/ppermute | solution.py:755
  119.5 12.5 %collective-permute-start.17 = (bf16[4,3,32,768]{3,2,1,0:T(8,128)(2,1)S(1)}, bf16[4,3,32,768]{3,2,1,0:T(8,128)(2,1)}, u32[]{:S(2)}, u32[]{:S(2)}) collective-permute-start(bf16[4,3,32,768]{3,2,1,0:T(8,128)(2,1)S(1)} %get-tuple-element.297), channel_id=1, source_target_pairs={{0,1},{1,0},{2,3},{3,2},{4,5},{5,4},{6,7},{7,6},{8,9},{9,8},{10,11... | collective-permute-start | bytes 1769480 | tf_op jit(solution)/shard_map/ppermute | solution.py:755
  129.4 22.9 %collective-permute-start.19 = (bf16[4,192,768]{2,1,0:T(8,128)(2,1)}, bf16[4,192,768]{2,1,0:T(8,128)(2,1)}, u32[]{:S(2)}, u32[]{:S(2)}) collective-permute-start(bf16[4,192,768]{2,1,0:T(8,128)(2,1)} %bitcast.32), channel_id=1, source_target_pairs={{0,1},{1,0},{2,3},{3,2},{4,5},{5,4},{6,7},{7,6},{8,9},{9,8},{10,11... | collective-permute-start | bytes 3538952 | tf_op jit(solution)/shard_map/ppermute | solution.py:755
  129.9 23.5 %collective-permute-start.20 = (bf16[4,192,768]{2,1,0:T(8,128)(2,1)}, bf16[4,192,768]{2,1,0:T(8,128)(2,1)}, u32[]{:S(2)}, u32[]{:S(2)}) collective-permute-start(bf16[4,192,768]{2,1,0:T(8,128)(2,1)} %bitcast.33), channel_id=1, source_target_pairs={{0,1},{1,0},{2,3},{3,2},{4,5},{5,4},{6,7},{7,6},{8,9},{9,8},{10,11... | collective-permute-start | bytes 3538952 | tf_op jit(solution)/shard_map/ppermute | solution.py:755
  130.0 16.0 %collective-permute-start.22 = (bf16[2,192,768]{2,1,0:T(8,128)(2,1)}, bf16[2,192,768]{2,1,0:T(8,128)(2,1)}, u32[]{:S(2)}, u32[]{:S(2)}) collective-permute-start(bf16[2,192,768]{2,1,0:T(8,128)(2,1)} %get-tuple-element.455), channel_id=1, source_target_pairs={{0,4},{1,5},{2,6},{3,7},{4,0},{5,1},{6,2},{7,3},{8,12},{9,13},{10,... | collective-permute-start | bytes 1769480 | tf_op jit(solution)/shard_map/ppermute | solution.py:755
  131.0 16.5 %collective-permute-start.21 = (bf16[2,192,768]{2,1,0:T(8,128)(2,1)}, bf16[2,192,768]{2,1,0:T(8,128)(2,1)}, u32[]{:S(2)}, u32[]{:S(2)}) collective-permute-start(bf16[2,192,768]{2,1,0:T(8,128)(2,1)} %get-tuple-element.457), channel_id=1, source_target_pairs={{0,2},{1,3},{2,0},{3,1},{4,6},{5,7},{6,4},{7,5},{8,10},{9,11},{10,... | collective-permute-start | bytes 1769480 | tf_op jit(solution)/shard_map/ppermute | solution.py:755
  141.1 24.9 %collective-permute-start.24 = (bf16[3,32,768]{2,1,0:T(8,128)(2,1)S(1)}, bf16[3,32,768]{2,1,0:T(8,128)(2,1)S(1)}, u32[]{:S(2)}, u32[]{:S(2)}) collective-permute-start(bf16[3,32,768]{2,1,0:T(8,128)(2,1)S(1)} %get-tuple-element.472), channel_id=1, source_target_pairs={{0,2},{1,3},{2,0},{3,1},{4,6},{5,7},{6,4},{7,5},{8,10},{9,11},{10,... | collective-permute-start | bytes 442376 | tf_op jit(solution)/shard_map/ppermute | solution.py:755
  145.9 21.3 %collective-permute-start.25 = (bf16[3,32,768]{2,1,0:T(8,128)(2,1)S(1)}, bf16[3,32,768]{2,1,0:T(8,128)(2,1)S(1)}, u32[]{:S(2)}, u32[]{:S(2)}) collective-permute-start(bf16[3,32,768]{2,1,0:T(8,128)(2,1)S(1)} %get-tuple-element.471), channel_id=1, source_target_pairs={{0,4},{1,5},{2,6},{3,7},{4,0},{5,1},{6,2},{7,3},{8,12},{9,13},{10,... | collective-permute-start | bytes 442376 | tf_op jit(solution)/shard_map/ppermute | solution.py:755
  153.4 11.4 %collective-permute-start.27 = (bf16[1,192,768]{2,1,0:T(8,128)(2,1)S(1)}, bf16[1,192,768]{2,1,0:T(8,128)(2,1)S(1)}, u32[]{:S(2)}, u32[]{:S(2)}) collective-permute-start(bf16[1,192,768]{2,1,0:T(8,128)(2,1)S(1)} %get-tuple-element.469), channel_id=1, source_target_pairs={{0,4},{1,5},{2,6},{3,7},{4,0},{5,1},{6,2},{7,3},{8,12},{9,13},{10,... | collective-permute-start | bytes 884744 | tf_op jit(solution)/shard_map/ppermute | solution.py:755
  156.2 12.0 %collective-permute-start.26 = (bf16[3,32,768]{2,1,0:T(8,128)(2,1)S(1)}, bf16[3,32,768]{2,1,0:T(8,128)(2,1)S(1)}, u32[]{:S(2)}, u32[]{:S(2)}) collective-permute-start(bf16[3,32,768]{2,1,0:T(8,128)(2,1)S(1)} %get-tuple-element.470), channel_id=1, source_target_pairs={{0,6},{1,7},{2,4},{3,5},{4,2},{5,3},{6,0},{7,1},{8,14},{9,15},{10,... | collective-permute-start | bytes 442376 | tf_op jit(solution)/shard_map/ppermute | solution.py:755
  161.5 19.2 %collective-permute-start.34 = (bf16[2,192,768]{2,1,0:T(8,128)(2,1)S(1)}, bf16[2,192,768]{2,1,0:T(8,128)(2,1)S(1)}, u32[]{:S(2)}, u32[]{:S(2)}) collective-permute-start(bf16[2,192,768]{2,1,0:T(8,128)(2,1)S(1)} %get-tuple-element.451), channel_id=1, source_target_pairs={{0,4},{1,5},{2,6},{3,7},{4,0},{5,1},{6,2},{7,3},{8,12},{9,13},{10,... | collective-permute-start | bytes 1769480 | tf_op jit(solution)/shard_map/ppermute | solution.py:755
  166.0 17.2 %collective-permute-start.33 = (bf16[2,192,768]{2,1,0:T(8,128)(2,1)S(1)}, bf16[2,192,768]{2,1,0:T(8,128)(2,1)S(1)}, u32[]{:S(2)}, u32[]{:S(2)}) collective-permute-start(bf16[2,192,768]{2,1,0:T(8,128)(2,1)S(1)} %get-tuple-element.453), channel_id=1, source_target_pairs={{0,2},{1,3},{2,0},{3,1},{4,6},{5,7},{6,4},{7,5},{8,10},{9,11},{10,... | collective-permute-start | bytes 1769480 | tf_op jit(solution)/shard_map/ppermute | solution.py:755
  167.2 17.1 %collective-permute-start.32 = (bf16[192,768]{1,0:T(8,128)(2,1)S(1)}, bf16[192,768]{1,0:T(8,128)(2,1)S(1)}, u32[]{:S(2)}, u32[]{:S(2)}) collective-permute-start(bf16[192,768]{1,0:T(8,128)(2,1)S(1)} %get-tuple-element.491), channel_id=1, source_target_pairs={{0,8},{8,0},{16,24},{24,16},{1,9},{9,1},{17,25},{25,17},{2,10},{10... | collective-permute-start | bytes 884744 | tf_op jit(solution)/shard_map/ppermute | solution.py:755
  168.2 16.9 %collective-permute-start.29 = (bf16[3,32,768]{2,1,0:T(8,128)(2,1)S(1)}, bf16[3,32,768]{2,1,0:T(8,128)(2,1)S(1)}, u32[]{:S(2)}, u32[]{:S(2)}) collective-permute-start(bf16[3,32,768]{2,1,0:T(8,128)(2,1)S(1)} %add_convert_fusion), channel_id=1, source_target_pairs={{0,2},{1,3},{2,0},{3,1},{4,6},{5,7},{6,4},{7,5},{8,10},{9,11},{10,... | collective-permute-start | bytes 442376 | tf_op jit(solution)/shard_map/ppermute | solution.py:755
  172.5 12.6 %collective-permute-start.30 = (bf16[3,32,768]{2,1,0:T(8,128)(2,1)S(1)}, bf16[3,32,768]{2,1,0:T(8,128)(2,1)S(1)}, u32[]{:S(2)}, u32[]{:S(2)}) collective-permute-start(bf16[3,32,768]{2,1,0:T(8,128)(2,1)S(1)} %add_convert_fusion), channel_id=1, source_target_pairs={{0,4},{1,5},{2,6},{3,7},{4,0},{5,1},{6,2},{7,3},{8,12},{9,13},{10,... | collective-permute-start | bytes 442376 | tf_op jit(solution)/shard_map/ppermute | solution.py:755
  186.9 13.2 %collective-permute-start.38 = (bf16[96,768]{1,0:T(8,128)(2,1)}, bf16[96,768]{1,0:T(8,128)(2,1)S(1)}, u32[]{:S(2)}, u32[]{:S(2)}) collective-permute-start(bf16[96,768]{1,0:T(8,128)(2,1)} %get-tuple-element.497), channel_id=1, source_target_pairs={{0,16},{8,24},{16,0},{24,8},{1,17},{9,25},{17,1},{25,9},{2,18},{10... | collective-permute-start | bytes 442376 | tf_op jit(solution)/shard_map/ppermute | solution.py:755
  187.8 14.7 %collective-permute-start.43 = (bf16[1,192,768]{2,1,0:T(8,128)(2,1)S(1)}, bf16[1,192,768]{2,1,0:T(8,128)(2,1)S(1)}, u32[]{:S(2)}, u32[]{:S(2)}) collective-permute-start(bf16[1,192,768]{2,1,0:T(8,128)(2,1)S(1)} %copy-done.28), channel_id=1, source_target_pairs={{0,2},{1,3},{2,0},{3,1},{4,6},{5,7},{6,4},{7,5},{8,10},{9,11},{10,... | collective-permute-start | bytes 884744 | tf_op jit(solution)/shard_map/ppermute | solution.py:755
  189.2 13.3 %collective-permute-start.42 = (bf16[1,192,768]{2,1,0:T(8,128)(2,1)S(1)}, bf16[1,192,768]{2,1,0:T(8,128)(2,1)S(1)}, u32[]{:S(2)}, u32[]{:S(2)}) collective-permute-start(bf16[1,192,768]{2,1,0:T(8,128)(2,1)S(1)} %get-tuple-element.465), channel_id=1, source_target_pairs={{0,4},{1,5},{2,6},{3,7},{4,0},{5,1},{6,2},{7,3},{8,12},{9,13},{10,... | collective-permute-start | bytes 884744 | tf_op jit(solution)/shard_map/ppermute | solution.py:755
  191.8 12.8 %collective-permute-start.40 = (bf16[1,192,768]{2,1,0:T(8,128)(2,1)S(1)}, bf16[1,192,768]{2,1,0:T(8,128)(2,1)S(1)}, u32[]{:S(2)}, u32[]{:S(2)}) collective-permute-start(bf16[1,192,768]{2,1,0:T(8,128)(2,1)S(1)} %get-tuple-element.365), channel_id=1, source_target_pairs={{0,4},{1,5},{2,6},{3,7},{4,0},{5,1},{6,2},{7,3},{8,12},{9,13},{10,... | collective-permute-start | bytes 884744 | tf_op jit(solution)/shard_map/ppermute | solution.py:755
  193.0 11.6 %collective-permute-start.41 = (bf16[1,192,768]{2,1,0:T(8,128)(2,1)S(1)}, bf16[1,192,768]{2,1,0:T(8,128)(2,1)S(1)}, u32[]{:S(2)}, u32[]{:S(2)}) collective-permute-start(bf16[1,192,768]{2,1,0:T(8,128)(2,1)S(1)} %get-tuple-element.367), channel_id=1, source_target_pairs={{0,2},{1,3},{2,0},{3,1},{4,6},{5,7},{6,4},{7,5},{8,10},{9,11},{10,... | collective-permute-start | bytes 884744 | tf_op jit(solution)/shard_map/ppermute | solution.py:755
  202.9 11.5 %collective-permute-start.45 = (bf16[192,768]{1,0:T(8,128)(2,1)S(1)}, bf16[192,768]{1,0:T(8,128)(2,1)S(1)}, u32[]{:S(2)}, u32[]{:S(2)}) collective-permute-start(bf16[192,768]{1,0:T(8,128)(2,1)S(1)} %get-tuple-element.487), channel_id=1, source_target_pairs={{0,8},{8,0},{16,24},{24,16},{1,9},{9,1},{17,25},{25,17},{2,10},{10... | collective-permute-start | bytes 884744 | tf_op jit(solution)/shard_map/ppermute | solution.py:755
  209.2 10.3 %collective-permute-start.44 = (bf16[192,768]{1,0:T(8,128)(2,1)S(1)}, bf16[192,768]{1,0:T(8,128)(2,1)S(1)}, u32[]{:S(2)}, u32[]{:S(2)}) collective-permute-start(bf16[192,768]{1,0:T(8,128)(2,1)S(1)} %bitcast.153), channel_id=1, source_target_pairs={{0,8},{8,0},{16,24},{24,16},{1,9},{9,1},{17,25},{25,17},{2,10},{10... | collective-permute-start | bytes 884744 | tf_op jit(solution)/shard_map/ppermute | solution.py:755
  219.6 12.7 %collective-permute-start.46 = (bf16[1,192,768]{2,1,0:T(8,128)(2,1)S(1)}, bf16[1,192,768]{2,1,0:T(8,128)(2,1)}, u32[]{:S(2)}, u32[]{:S(2)}) collective-permute-start(bf16[1,192,768]{2,1,0:T(8,128)(2,1)S(1)} %get-tuple-element.378), channel_id=1, source_target_pairs={{0,4},{1,5},{2,6},{3,7},{4,0},{5,1},{6,2},{7,3},{8,12},{9,13},{10,... | collective-permute-start | bytes 884744 | tf_op jit(solution)/shard_map/ppermute | solution.py:755
  221.1 12.6 %collective-permute-start.47 = (bf16[1,192,768]{2,1,0:T(8,128)(2,1)S(1)}, bf16[1,192,768]{2,1,0:T(8,128)(2,1)}, u32[]{:S(2)}, u32[]{:S(2)}) collective-permute-start(bf16[1,192,768]{2,1,0:T(8,128)(2,1)S(1)} %get-tuple-element.380), channel_id=1, source_target_pairs={{0,2},{1,3},{2,0},{3,1},{4,6},{5,7},{6,4},{7,5},{8,10},{9,11},{10,... | collective-permute-start | bytes 884744 | tf_op jit(solution)/shard_map/ppermute | solution.py:755
  222.3 9.9 %collective-permute-start.48 = (bf16[96,768]{1,0:T(8,128)(2,1)S(1)}, bf16[96,768]{1,0:T(8,128)(2,1)S(1)}, u32[]{:S(2)}, u32[]{:S(2)}) collective-permute-start(bf16[96,768]{1,0:T(8,128)(2,1)S(1)} %get-tuple-element.495), channel_id=1, source_target_pairs={{0,16},{8,24},{16,0},{24,8},{1,17},{9,25},{17,1},{25,9},{2,18},{10... | collective-permute-start | bytes 442376 | tf_op jit(solution)/shard_map/ppermute | solution.py:755
  222.8 9.3 %all-to-all-start.1 = ((bf16[8,32,1,256]{3,1,2,0:T(8,128)(2,1)}), bf16[8,32,1,256]{3,1,2,0:T(8,128)(2,1)S(1)}, u32[]{:S(2)}, u32[]{:S(2)}) async-start(bf16[8,32,1,256]{3,1,2,0:T(8,128)(2,1)} %bitcast.70), calls=%async_computation.1 | async-start | bytes 262144 | tf_op jit(solution)/shard_map/all_to_all | solution.py:867
  226.2 17.9 %collective-permute-start.56 = (bf16[2,192,768]{2,1,0:T(8,128)(2,1)S(1)}, bf16[2,192,768]{2,1,0:T(8,128)(2,1)}, u32[]{:S(2)}, u32[]{:S(2)}) collective-permute-start(bf16[2,192,768]{2,1,0:T(8,128)(2,1)S(1)} %constant_dynamic-update-slice_fusion.2), channel_id=1, source_target_pairs={{0,4},{1,5},{2,6},{3,7},{4,0},{5,1},{6,2},{7,3},{8,12},{9,13},{10,... | collective-permute-start | bytes 1769480 | tf_op jit(solution)/shard_map/ppermute | solution.py:755
  228.2 17.2 %collective-permute-start.55 = (bf16[2,192,768]{2,1,0:T(8,128)(2,1)S(1)}, bf16[2,192,768]{2,1,0:T(8,128)(2,1)S(1)}, u32[]{:S(2)}, u32[]{:S(2)}) collective-permute-start(bf16[2,192,768]{2,1,0:T(8,128)(2,1)S(1)} %constant_dynamic-update-slice_fusion), channel_id=1, source_target_pairs={{0,2},{1,3},{2,0},{3,1},{4,6},{5,7},{6,4},{7,5},{8,10},{9,11},{10,... | collective-permute-start | bytes 1769480 | tf_op jit(solution)/shard_map/ppermute | solution.py:755
  232.3 14.4 %collective-permute-start.54 = (bf16[32,2048]{1,0:T(8,128)(2,1)S(1)}, bf16[32,2048]{1,0:T(8,128)(2,1)S(1)}, u32[]{:S(2)}, u32[]{:S(2)}) collective-permute-start(bf16[32,2048]{1,0:T(8,128)(2,1)S(1)} %bitcast.160), channel_id=1, source_target_pairs={{0,8},{8,0},{16,24},{24,16},{1,9},{9,1},{17,25},{25,17},{2,10},{10... | collective-permute-start | bytes 393224 | tf_op jit(solution)/shard_map/ppermute | solution.py:755
  233.7 10.1 %collective-permute-start.52 = (bf16[96,768]{1,0:T(8,128)(2,1)S(1)}, bf16[96,768]{1,0:T(8,128)(2,1)S(1)}, u32[]{:S(2)}, u32[]{:S(2)}) collective-permute-start(bf16[96,768]{1,0:T(8,128)(2,1)S(1)} %add.270), channel_id=1, source_target_pairs={{0,16},{8,24},{16,0},{24,8},{1,17},{9,25},{17,1},{25,9},{2,18},{10... | collective-permute-start | bytes 442376 | tf_op jit(solution)/shard_map/ppermute | solution.py:755
  237.6 18.4 %collective-permute-start.51 = (bf16[2,192,768]{2,1,0:T(8,128)(2,1)S(1)}, bf16[2,192,768]{2,1,0:T(8,128)(2,1)S(1)}, u32[]{:S(2)}, u32[]{:S(2)}) collective-permute-start(bf16[2,192,768]{2,1,0:T(8,128)(2,1)S(1)} %constant_dynamic-update-slice_fusion.6), channel_id=1, source_target_pairs={{0,4},{1,5},{2,6},{3,7},{4,0},{5,1},{6,2},{7,3},{8,12},{9,13},{10,... | collective-permute-start | bytes 1769480 | tf_op jit(solution)/shard_map/ppermute | solution.py:755
  243.8 12.2 %collective-permute-start.50 = (bf16[2,192,768]{2,1,0:T(8,128)(2,1)S(1)}, bf16[2,192,768]{2,1,0:T(8,128)(2,1)S(1)}, u32[]{:S(2)}, u32[]{:S(2)}) collective-permute-start(bf16[2,192,768]{2,1,0:T(8,128)(2,1)S(1)} %constant_dynamic-update-slice_fusion.4), channel_id=1, source_target_pairs={{0,2},{1,3},{2,0},{3,1},{4,6},{5,7},{6,4},{7,5},{8,10},{9,11},{10,... | collective-permute-start | bytes 1769480 | tf_op jit(solution)/shard_map/ppermute | solution.py:755
  246.5 15.5 %collective-permute-start.63 = (bf16[4,192,768]{2,1,0:T(8,128)(2,1)S(1)}, bf16[4,192,768]{2,1,0:T(8,128)(2,1)S(1)}, u32[]{:S(2)}, u32[]{:S(2)}) collective-permute-start(bf16[4,192,768]{2,1,0:T(8,128)(2,1)S(1)} %constant_dynamic-update-slice_fusion.10.refs_2_), channel_id=1, source_target_pairs={{0,1},{1,0},{2,3},{3,2},{4,5},{5,4},{6,7},{7,6},{8,9},{9,8},{10,11... | collective-permute-start | bytes 3538952 | tf_op jit(solution)/shard_map/ppermute | solution.py:755
  246.7 15.9 %collective-permute-start.62 = (bf16[4,192,768]{2,1,0:T(8,128)(2,1)S(1)}, bf16[4,192,768]{2,1,0:T(8,128)(2,1)S(1)}, u32[]{:S(2)}, u32[]{:S(2)}) collective-permute-start(bf16[4,192,768]{2,1,0:T(8,128)(2,1)S(1)} %constant_dynamic-update-slice_fusion.8), channel_id=1, source_target_pairs={{0,1},{1,0},{2,3},{3,2},{4,5},{5,4},{6,7},{7,6},{8,9},{9,8},{10,11... | collective-permute-start | bytes 3538952 | tf_op jit(solution)/shard_map/ppermute | solution.py:755
  256.1 15.7 %collective-permute-start.59 = (bf16[4,192,768]{2,1,0:T(8,128)(2,1)S(1)}, bf16[4,192,768]{2,1,0:T(8,128)(2,1)S(1)}, u32[]{:S(2)}, u32[]{:S(2)}) collective-permute-start(bf16[4,192,768]{2,1,0:T(8,128)(2,1)S(1)} %constant_dynamic-update-slice_fusion.14.refs_6_), channel_id=1, source_target_pairs={{0,1},{1,0},{2,3},{3,2},{4,5},{5,4},{6,7},{7,6},{8,9},{9,8},{10,11... | collective-permute-start | bytes 3538952 | tf_op jit(solution)/shard_map/ppermute | solution.py:755
  256.3 15.6 %collective-permute-start.58 = (bf16[4,192,768]{2,1,0:T(8,128)(2,1)S(1)}, bf16[4,192,768]{2,1,0:T(8,128)(2,1)S(1)}, u32[]{:S(2)}, u32[]{:S(2)}) collective-permute-start(bf16[4,192,768]{2,1,0:T(8,128)(2,1)S(1)} %constant_dynamic-update-slice_fusion.12), channel_id=1, source_target_pairs={{0,1},{1,0},{2,3},{3,2},{4,5},{5,4},{6,7},{7,6},{8,9},{9,8},{10,11... | collective-permute-start | bytes 3538952 | tf_op jit(solution)/shard_map/ppermute | solution.py:755
  269.6 13.0 %collective-permute-start.66 = (bf16[2,192,768]{2,1,0:T(8,128)(2,1)S(1)}, bf16[2,192,768]{2,1,0:T(8,128)(2,1)S(1)}, u32[]{:S(2)}, u32[]{:S(2)}) collective-permute-start(bf16[2,192,768]{2,1,0:T(8,128)(2,1)S(1)} %constant_dynamic-update-slice_fusion.18), channel_id=1, source_target_pairs={{0,4},{1,5},{2,6},{3,7},{4,0},{5,1},{6,2},{7,3},{8,12},{9,13},{10,... | collective-permute-start | bytes 1769480 | tf_op jit(solution)/shard_map/ppermute | solution.py:755
  270.3 12.7 %collective-permute-start.65 = (bf16[2,192,768]{2,1,0:T(8,128)(2,1)S(1)}, bf16[2,192,768]{2,1,0:T(8,128)(2,1)S(1)}, u32[]{:S(2)}, u32[]{:S(2)}) collective-permute-start(bf16[2,192,768]{2,1,0:T(8,128)(2,1)S(1)} %constant_dynamic-update-slice_fusion.16), channel_id=1, source_target_pairs={{0,2},{1,3},{2,0},{3,1},{4,6},{5,7},{6,4},{7,5},{8,10},{9,11},{10,... | collective-permute-start | bytes 1769480 | tf_op jit(solution)/shard_map/ppermute | solution.py:755
  283.1 13.1 %collective-permute-start.70 = (bf16[4,192,768]{2,1,0:T(8,128)(2,1)S(1)}, bf16[4,192,768]{2,1,0:T(8,128)(2,1)S(1)}, u32[]{:S(2)}, u32[]{:S(2)}) collective-permute-start(bf16[4,192,768]{2,1,0:T(8,128)(2,1)S(1)} %constant_dynamic-update-slice_fusion.22), channel_id=1, source_target_pairs={{0,1},{1,0},{2,3},{3,2},{4,5},{5,4},{6,7},{7,6},{8,9},{9,8},{10,11... | collective-permute-start | bytes 3538952 | tf_op jit(solution)/shard_map/ppermute | solution.py:755
  283.3 12.9 %collective-permute-start.69 = (bf16[4,192,768]{2,1,0:T(8,128)(2,1)S(1)}, bf16[4,192,768]{2,1,0:T(8,128)(2,1)S(1)}, u32[]{:S(2)}, u32[]{:S(2)}) collective-permute-start(bf16[4,192,768]{2,1,0:T(8,128)(2,1)S(1)} %constant_dynamic-update-slice_fusion.20), channel_id=1, source_target_pairs={{0,1},{1,0},{2,3},{3,2},{4,5},{5,4},{6,7},{7,6},{8,9},{9,8},{10,11... | collective-permute-start | bytes 3538952 | tf_op jit(solution)/shard_map/ppermute | solution.py:755
  283.9 9.5 %collective-permute-start.68 = (bf16[32,2048]{1,0:T(8,128)(2,1)S(1)}, bf16[32,2048]{1,0:T(8,128)(2,1)S(1)}, u32[]{:S(2)}, u32[]{:S(2)}) collective-permute-start(bf16[32,2048]{1,0:T(8,128)(2,1)S(1)} %add.272), channel_id=1, source_target_pairs={{0,16},{8,24},{16,0},{24,8},{1,17},{9,25},{17,1},{25,9},{2,18},{10... | collective-permute-start | bytes 393224 | tf_op jit(solution)/shard_map/ppermute | solution.py:755
  (61 other events, 388.0 us)
where the time goes:
time: 302 us; the launch traced here: 301 us
  Pallas kernels  106 us (35%)
  starting transfers between devices  77.5 us (26%)
  waiting for transfers between devices  75.5 us (25%)
  other arithmetic  22.4 us (7%)
  local copies, waits for them, and re-layouts  17.6 us (6%)
    pallas_call x15, Pallas kernels, call(): pl.pallas_call(body, grid_spec=pltpu.PrefetchScalarGridSpec(num_scalar_pr...  106 us
    ppermute x71, waiting for transfers between devices, swap(): return lax.ppermute(value, axis, [(i, i ^ mask) for i in range(size)])  72.4 us
    ppermute x71, starting transfers between devices, swap(): return lax.ppermute(value, axis, [(i, i ^ mask) for i in range(size)])  68.9 us
    add x12, other arithmetic, sum_everywhere(): kept = [k[:half] + f[:half] for k, f in zip(kept, flight)]  14 us
    unnamed x86, local copies, waits for them, and re-layouts  12 us
  transfers between devices with their start and end apart: 73, of which 30 were waited for; matrix products, arithmetic and copies ran while one was open for 9% of the time, Pallas kernels for 27%

commit v1 on v0

--- a/solution.py
+++ b/solution.py
@@ -13,7 +13,7 @@
 SCALE = HEAD_DIM ** (-0.5)
 LOW = jnp.bfloat16
 F32 = jnp.float32
-COST = 10**9
+COST = 4 * 10**9
 
 
 def dot(left_side, right_side, contract):
@@ -70,6 +70,7 @@
         ),
         out_shape=outs,
         compiler_params=pltpu.CompilerParams(vmem_limit_bytes=limit << 20),
+        name=getattr(body, "__name__", None) or body.func.__name__,
         cost_estimate=pl.CostEstimate(flops=cost * COST, bytes_accessed=1, transcendentals=0),
     )(*ins)
 
@@ -153,23 +154,23 @@
     )
 
 
-def block_at(step, order):
-    return step - step % 2 + (order[0] ^ 1 ^ (step % 2))
-
-
-def block_out_body(order, down, attended, *refs):
-    *actives, out = refs
+def block_at(pair, own, order):
+    return 2 * pair + (order[0] ^ 1 ^ own)
+
+
+def block_out_body(order, down, attended, sent, kept, out):
     width = attended.shape[1]
     total = attended[...]
-    for at, active in enumerate(actives):
-        start = pl.multiple_of(block_at(at, order) * width, width)
-        total += nn(active[...], down[pl.ds(start, width), :])
+    for own, actives in enumerate((sent, kept)):
+        for pair in range(actives.shape[0]):
+            start = pl.multiple_of(block_at(pair, own, order) * width, width)
+            total += nn(actives[pair], down[pl.ds(start, width), :])
     out[...] = total.astype(LOW)
 
 
 def block_out_of(order, down, attended, *actives):
     seqs, span, width = attended.shape
-    lines = pl.BlockSpec((span, width), lambda s, m: (s, 0))
+    lines = pl.BlockSpec((actives[0].shape[0], span, width), lambda s, m: (0, s, 0))
     return call(
         block_out_body,
         (seqs,),
@@ -179,7 +180,7 @@
         [whole(*down.shape), per_seq(span, width), *([lines] * len(actives))],
         scalars=1,
         limit=24,
-        cost=6,
+        cost=0,
     )
 
 
@@ -334,8 +335,13 @@
     )
 
 
-def feed_step(order, lifted, cotangent, grad_active, up, turned, outs):
-    active_out, grad_out, down_grad, up_grad = outs
+def feed_body(
+    order, lifted, cotangent, grad_active, up, active_out, grad_out, down_grad, up_grad, turned
+):
+    @pl.when(pl.program_id(0) == 0)
+    def _():
+        turned[...] = lifted[...].T
+
     hidden = nn(lifted[...], up[...])
     share = 0.5 * (1.0 + lax.erf(hidden * 0.5**0.5))
     slope = share + hidden * jnp.exp(-0.5 * hidden * hidden) * 0.3989422804014327
@@ -353,54 +359,38 @@
         up_grad[piece ^ order[2]] = value[piece * line : (piece + 1) * line].astype(LOW)
 
 
-def feed_body(steps, order, lifted, cotangent, grad_active, up, *refs):
-    *outs, turned = refs
-    step = pl.program_id(0)
-
-    @pl.when(step == 0)
-    def _():
-        turned[...] = lifted[...].T
-
-    for at in range(len(outs) // 4):
-        pl.when(step // steps == at)(
-            functools.partial(
-                feed_step, order, lifted, cotangent, grad_active, up, turned, outs[4 * at : 4 * at + 4]
-            )
-        )
-
-
-def feed(first, blocks, pieces, order, lifted, cotangent, grad_active, up):
+def feed(own, pieces, order, lifted, cotangent, grad_active, up):
     rows, width = lifted.shape
     steps = width // QUAD
+    pairs = up.shape[1] // width // 2
 
     def columns(i, m):
-        return (0, block_at(first + i // steps, m) * steps + i % steps)
-
-    def held(at, i):
-        return jnp.clip(i - at * steps, 0, steps - 1)
-
-    out_specs = []
-    for at in range(blocks):
-        out_specs += [
-            pl.BlockSpec((rows, QUAD), lambda i, m, at=at: (0, held(at, i))),
-            pl.BlockSpec((rows, QUAD), lambda i, m, at=at: (0, held(at, i))),
+        return (0, block_at(i // steps, own, m) * steps + i % steps)
+
+    def lines(i, m):
+        return (i // steps, 0, i % steps)
+
+    return call(
+        feed_body,
+        (pairs * steps,),
+        (order, lifted, cotangent, grad_active, up),
+        [
+            far((pairs, rows, width)),
+            far((pairs, rows, width)),
+            shape((pieces, pairs, steps, QUAD // pieces, width)),
+            shape((pieces, pairs, width // pieces, width)),
+        ],
+        [
+            pl.BlockSpec((None, rows, QUAD), lines),
+            pl.BlockSpec((None, rows, QUAD), lines),
             pl.BlockSpec(
-                (pieces, None, QUAD // pieces, width), lambda i, m, at=at: (0, held(at, i), 0, 0)
+                (pieces, None, None, QUAD // pieces, width),
+                lambda i, m: (0, i // steps, i % steps, 0, 0),
             ),
-            pl.BlockSpec((pieces, width // pieces, QUAD), lambda i, m, at=at: (0, 0, held(at, i))),
-        ]
-    return call(
-        functools.partial(feed_body, steps),
-        (blocks * steps,),
-        (order, lifted, cotangent, grad_active, up),
-        [
-            far((rows, width)),
-            far((rows, width)),
-            shape((pieces, steps, QUAD // pieces, width)),
-            shape((pieces, width // pieces, width)),
-        ]
-        * blocks,
-        out_specs,
+            pl.BlockSpec(
+                (pieces, None, width // pieces, QUAD), lambda i, m: (0, i // steps, 0, i % steps)
+            ),
+        ],
         [
             whole(rows, width),
             whole(rows, width),
@@ -410,12 +400,12 @@
         [pltpu.VMEM((width, rows), LOW)],
         scalars=1,
         limit=20,
-        cost=6 * blocks,
+        cost=6 * pairs,
     )
 
 
 def feed_back_body(
-    order, hidden_1, hidden_2, hidden_3, hidden_4, up, cotangent, attended, inverse, gain, out_w,
+    order, sent, kept, up, cotangent, attended, inverse, gain, out_w,
     grad_attended, grad_branch, grad_mixed, norm_grads,
 ):
     width = cotangent.shape[1]
@@ -428,9 +418,10 @@
     scale = inverse[:, :1]
     unit = (total - jnp.mean(total, axis=-1, keepdims=True)) * scale
     grad = 0.0
-    for at, hidden in enumerate((hidden_1, hidden_2, hidden_3, hidden_4)):
-        start = pl.multiple_of(block_at(at, order) * width, width)
-        grad += nt(hidden[...], up[:, pl.ds(start, width)])
+    for own, hiddens in enumerate((sent, kept)):
+        for pair in range(hiddens.shape[0]):
+            start = pl.multiple_of(block_at(pair, own, order) * width, width)
+            grad += nt(hiddens[pair], up[:, pl.ds(start, width)])
     norm_grads[0:1, :] += jnp.sum(grad * unit, axis=0, keepdims=True)
     norm_grads[1:2, :] += jnp.sum(grad, axis=0, keepdims=True)
     whole_grad = cotangent[...].astype(F32) + normalize_back(grad, unit, scale, row(gain))
@@ -443,7 +434,7 @@
 def feed_back(order, hiddens, up, cotangent, attended, inverse, gain, out_w):
     seqs, span, width = cotangent.shape
     block = per_seq(span, width)
-    lines = pl.BlockSpec((span, width), lambda s, *_: (s, 0))
+    lines = pl.BlockSpec((hiddens[0].shape[0], span, width), lambda s, *_: (0, s, 0))
     return call(
         feed_back_body,
         (seqs,),
@@ -586,43 +577,39 @@
     )
 
 
-def place_feed_body(order, *refs):
-    inputs, (down, up, total) = refs[:8], refs[8:]
-    share, side = pl.program_id(0), pl.program_id(1)
+def place_feed_body(order, own_down, other_down, own_up, other_up, down, up, total):
+    pair, side = pl.program_id(0), pl.program_id(1)
     ours = (side ^ order[0]) == 0
 
-    @pl.when((share == 0) & (side == 0))
+    @pl.when((pair == 0) & (side == 0))
     def _():
         total[...] = jnp.zeros_like(total)
 
     def place(down_in, up_in):
-        pieces, steps, line, _ = down_in.shape
-        tall = up_in.shape[1]
+        pieces, _, steps, line, _ = down_in.shape
+        tall = up_in.shape[2]
 
         def one(piece, square):
             for step in range(steps):
-                value = down_in[piece ^ order[1], step].astype(F32)
+                value = down_in[piece ^ order[1], pair, step].astype(F32)
                 start = pl.multiple_of(step * pieces * line + piece * line, line)
                 down[pl.ds(start, line), :] = value
                 square += jnp.sum(value * value, axis=0, keepdims=True)
-            value = up_in[piece ^ order[2]].astype(F32)
+            value = up_in[piece ^ order[2], pair].astype(F32)
             up[pl.ds(pl.multiple_of(piece * tall, tall), tall), :] = value
             return square + jnp.sum(value * value, axis=0, keepdims=True)
 
         total[0:1, :] += lax.fori_loop(0, pieces, one, jnp.zeros((1, down.shape[1]), F32))
 
-    for at in range(4):
-        chosen = (share == at // 2) & (ours if at % 2 == 0 else jnp.logical_not(ours))
-        pl.when(chosen)(
-            functools.partial(place, inputs[4 * (at // 2) + at % 2], inputs[4 * (at // 2) + 2 + at % 2])
-        )
+    pl.when(ours)(lambda: place(own_down, own_up))
+    pl.when(jnp.logical_not(ours))(lambda: place(other_down, other_up))
 
 
 def place_feed(order, down_shape, up_shape, *arrays):
     width = down_shape[1]
     return call(
         place_feed_body,
-        (2, 2),
+        (down_shape[0] // width // 2, 2),
         (order, *arrays),
         [shape(down_shape, F32), shape(up_shape, F32), shape((8, width), F32)],
         [
@@ -633,12 +620,12 @@
         [whole(*x.shape) for x in arrays],
         scalars=1,
         limit=28,
-        cost=8,
+        cost=0,
     )
 
 
 def place_squares_body(order, own_1, other_1, own_2, other_2, others, norms, *refs):
-    *outs, norm, total = refs
+    *outs, attn_gain, attn_bias, ffn_gain, ffn_bias, norm, total = refs
     side = pl.program_id(0)
     ours = (side ^ order[0]) == 0
 
@@ -664,9 +651,14 @@
 
     @pl.when(side == 1)
     def _():
-        square = jnp.sum(total[0:1, :], keepdims=True) + jnp.sum(
-            norms[...] * norms[...], keepdims=True
-        )
+        value = norms[...].astype(F32)
+        square = jnp.sum(total[0:1, :], keepdims=True) + jnp.sum(value * value, keepdims=True)
+        span = value.shape[1]
+        cuts = attn_gain.shape[0] // span
+        for at, out in enumerate((attn_gain, attn_bias, ffn_gain, ffn_bias)):
+            for cut in range(cuts):
+                line = value[at * cuts + cut : at * cuts + cut + 1]
+                out[cut * span : (cut + 1) * span] = line.reshape(span)
         norm[...] = jnp.sqrt(square)
 
 
@@ -677,8 +669,12 @@
         place_squares_body,
         (2,),
         (order, *arrays),
-        [shape((2 * pieces * line, width), F32)] * 4 + [shape((1, 1), F32)],
-        [pl.BlockSpec((pieces * line, width), lambda i, m: (i, 0))] * 4 + [result(1, 1)],
+        [shape((2 * pieces * line, width), F32)] * 4
+        + [shape((width,), F32)] * 4
+        + [shape((1, 1), F32)],
+        [pl.BlockSpec((pieces * line, width), lambda i, m: (i, 0))] * 4
+        + [result(width)] * 4
+        + [result(1, 1)],
         [whole(*x.shape) for x in arrays],
         [pltpu.VMEM(others.shape, F32)],
         scalars=1,
@@ -689,7 +685,7 @@
 
 def leave_body(
     meta, own, other, columns, normed, tokens, gain, grad_queries, query_w, grad_attended,
-    tokens_grad, terms, norm_grads, columns_t, terms_sum, grad_summary,
+    ffn_norms, tokens_grad, packed, columns_t, terms_sum, norm_grads, grad_summary,
 ):
     seq = pl.program_id(0)
     rows, span = columns.shape
@@ -716,37 +712,53 @@
 
     @pl.when(seq == pl.num_programs(0) - 1)
     def _():
-        terms[...] = terms_sum[...].astype(LOW)
+        total = terms_sum[...].astype(LOW)
+        width = norm_grads.shape[1]
+        lines = [
+            source[at : at + 1, cut : cut + span]
+            for source in (norm_grads, ffn_norms)
+            for at in range(2)
+            for cut in range(0, width, span)
+        ]
+        share, tall = rows // packed.shape[0], packed.shape[1]
+        lines.append(jnp.zeros((tall - share - len(lines), span), F32))
+        norms = jnp.concatenate(lines, axis=0).astype(LOW)
+        for at in range(packed.shape[0]):
+            packed[at, :share, :] = total[at * share : (at + 1) * share]
+            packed[at, share:, :] = norms
 
 
 def leave(
-    meta, own, other, columns, normed, tokens, gain, grad_queries, query_w, grad_attended
+    ring, meta, own, other, columns, normed, tokens, gain, grad_queries, query_w, grad_attended,
+    ffn_norms,
 ):
     seqs, span, width = tokens.shape
     rows = columns.shape[0]
     distance = distance_spec(own.shape[0], rows, width)
+    tall = rows // ring + -(-4 * width // span // 16) * 16
     block = per_seq(span, width)
     return call(
         leave_body,
         (seqs,),
         (
             meta, own, other, columns, *kept_far(normed, tokens), gain, *kept_far(grad_queries), query_w,
-            *kept_far(grad_attended),
+            *kept_far(grad_attended), ffn_norms,
         ),
-        [shape(tokens.shape), shape((rows, span)), shape((8, width), F32)],
-        [block, result(rows, span), result(8, width)],
+        [shape(tokens.shape), shape((ring, tall, span))],
+        [block, result(ring, tall, span)],
         [
             distance, distance, whole(rows, span), block, block, vector(width), block,
-            whole(width, width), block,
+            whole(width, width), block, whole(8, width),
         ],
         [
             pltpu.VMEM((span, rows), LOW),
             pltpu.VMEM((rows, span), F32),
+            pltpu.VMEM((8, width), F32),
             pltpu.VMEM((rows, width), LOW),
         ],
         scalars=1,
         limit=20,
-        cost=5,
+        cost=0,
     )
 
 
@@ -801,26 +813,29 @@
         flight = [swap(x, "krow", 1 << o[digit]) for x, o in zip(sent, orders)]
         ticket = yield (sent, kept)
     flight, kept = after((flight, kept), ticket)
-    value = jnp.concatenate([k + f for k, f in zip(kept, flight)])
-    split = []
-    for at in range(bits_of("dp")):
-        if at < halved:
-            half = value.reshape(2, -1, value.shape[-1])
-            mine = bit("dp", at)
-            sent, kept = pick(half, 1 - mine), pick(half, mine)
-            split.append((at, mine))
-        else:
-            sent = kept = value
-        flight = swap(sent, "dp", 1 << at)
+    values = [(k + f)[0] for k, f in zip(kept, flight)]
+    count = bits_of("dp")
+    strides = [list(range(count)), list(range(count - 1, -1, -1))]
+    sides = [bit("dp", stride[0]) for stride in strides]
+    for stage in range(count):
+        sent = kept = values
+        if stage < halved:
+            halves = [v.reshape(2, -1, v.shape[-1]) for v in values]
+            sent = [pick(h, 1 - side) for h, side in zip(halves, sides)]
+            kept = [pick(h, side) for h, side in zip(halves, sides)]
+        flight = [swap(x, "dp", 1 << o[stage]) for x, o in zip(sent, strides)]
         ticket = yield (sent, kept)
         flight, kept = after((flight, kept), ticket)
-        value = kept + flight
-    for at, mine in reversed(split):
-        flight = swap(value, "dp", 1 << at)
-        ticket = yield value
-        flight, value = after((flight, value), ticket)
-        value = in_order(value, flight, mine).reshape(-1, value.shape[-1])
-    values = list(value.reshape(2, 1, -1, value.shape[-1]))
+        values = [k + f for k, f in zip(kept, flight)]
+    if halved:
+        flight = [swap(x, "dp", 1 << o[0]) for x, o in zip(values, strides)]
+        ticket = yield values
+        flight, values = after((flight, values), ticket)
+        values = [
+            in_order(v, f, side).reshape(-1, v.shape[-1])
+            for v, f, side in zip(values, flight, sides)
+        ]
+    values = [v[None] for v in values]
     for digit in reversed(range(len(orders[0]))):
         flight = [swap(v, "krow", 1 << o[digit]) for v, o in zip(values, orders)]
         ticket = yield values
@@ -852,29 +867,23 @@
     yield after((own, flight), ticket)
 
 
-def sum_small(value):
-    for axis in ("krow", "dp"):
-        for at in range(bits_of(axis)):
-            flight = swap(value, axis, 1 << at)
-            ticket = yield value
-            flight, value = after((flight, value), ticket)
-            value = value + flight
-    yield value
-
-
-def sum_terms(terms, ring):
-    rows, span = terms.shape
-    value = lax.all_to_all(
-        terms.reshape(ring, rows // ring, span), "krow", 0, 1, tiled=False
-    ).reshape(rows // ring, ring * span)
-    ticket = yield terms
-    value = after(value, ticket)
+def sum_terms(packed, share):
+    span = packed.shape[2]
+    flight = lax.all_to_all(packed, "krow", 0, 0, tiled=True)
+    ticket = yield packed
+    flight = after(flight, ticket)
+    norms = jnp.sum(flight[:, share:].astype(F32), axis=0).astype(LOW)
+    value = jnp.concatenate([flight[:, :share].reshape(-1, span), norms])
     for at in range(bits_of("dp")):
         flight = swap(value, "dp", 1 << at)
         ticket = yield value
         flight, value = after((flight, value), ticket)
         value = value + flight
-    yield value
+    norms, value = value[packed.shape[0] * share :], value.astype(F32)
+    ring = packed.shape[0]
+    rows = ring * share
+    compress = value[:rows].reshape(ring, share, span).transpose(1, 0, 2).reshape(share, -1)
+    yield (compress, norms)
 
 
 class Line:
@@ -897,8 +906,8 @@
         return steps
 
 
-PLAN = "S1KF212A1Bg1Q3g12312g1O32g1gL2312c32c3n2n31c32n132nP3ncn3"
-HALVED = {"1": 2, "2": 2, "3": 2}
+PLAN = "S1K1AB1gQ1g3g13ggL31313c31c3Oc3c11P33"
+HALVED = {"1": 1, "3": 1}
 
 
 def local(
@@ -948,25 +957,14 @@
 
     known, sums, results = {}, {}, {}
 
-    def feed_blocks(first, blocks):
-        return line.run(
+    def run_feed(own):
+        name = ("sent", "kept")[own]
+        known[f"active_{name}"], known[f"hidden_{name}"], *known[f"{name}_1"] = line.run(
             lambda lifted: feed(
-                first, blocks, pieces, order, lifted.reshape(flat), cotangent_flat, grad_active,
-                up_weight,
+                own, pieces, order, lifted.reshape(flat), cotangent_flat, grad_active, up_weight
             ),
             lifted,
         )
-
-    def run_s():
-        known["active_1"], known["hidden_1"], *known["sent_1"] = feed_blocks(0, 1)
-
-    def run_k():
-        known["active_2"], known["hidden_2"], *known["kept_1"] = feed_blocks(1, 1)
-
-    def run_f():
-        out = feed_blocks(2, 2)
-        known["active_3"], known["hidden_3"], *known["sent_2"] = out[:4]
-        known["active_4"], known["hidden_4"], *known["kept_2"] = out[4:]
 
     def run_a():
         known["grad_attended"], known["grad_branch"], known["grad_mixed"], known["ffn_norms"] = (
@@ -974,7 +972,8 @@
                 lambda *hiddens: feed_back(
                     order, hiddens, up_weight, cotangent, attended, inverse, ffn_gain, out_weight
                 ),
-                *(known[f"hidden_{at}"] for at in range(1, 5)),
+                known["hidden_sent"],
+                known["hidden_kept"],
             )
         )
 
@@ -1001,28 +1000,26 @@
     def run_o():
         known["block_out"] = line.run(
             lambda *actives: block_out_of(order, down_weight, attended, *actives),
-            *(known[f"active_{at}"] for at in range(1, 5)),
+            known["active_sent"],
+            known["active_kept"],
         )
 
     def run_l():
         finish("g")
-        known["tokens_grad"], known["terms"], attn_norms = line.run(
+        known["tokens_grad"], known["terms"] = line.run(
             lambda own, other: leave(
-                meta, own, other, columns, normed, tokens, attn_gain, known["grads"][0],
-                query_weight, known["grad_attended"],
+                ring, meta, own, other, columns, normed, tokens, attn_gain, known["grads"][0],
+                query_weight, known["grad_attended"], known["ffn_norms"],
             ),
             *results["g"],
         )
-        known["norms"] = jnp.concatenate([attn_norms[:2], known["ffn_norms"][:2]])
 
     def run_p():
         finish("1")
-        finish("2")
-        form = (pieces, width // QUAD, QUAD // pieces, width)
-        arrays = [
-            x.reshape(form) if at % 4 < 2 else x
-            for at, x in enumerate((*results["1"], *results["2"]))
-        ]
+        pairs_held = down_weight.shape[0] // width // 2
+        steps = width // QUAD
+        forms = ((pieces, pairs_held, steps, QUAD // pieces, width), (pieces, pairs_held, -1, width))
+        arrays = [x.reshape(forms[at // 2]) for at, x in enumerate(results["1"])]
         known["feed"] = line.run(
             lambda *arrays: place_feed(order, down_weight.shape, up_weight.shape, *arrays),
             *arrays,
@@ -1031,21 +1028,21 @@
     def begin(name):
         if name == "g":
             return sum_krow(known["sent_g"], known["kept_g"])
-        if name == "n":
-            return sum_small(known["norms"])
         if name == "c":
-            return sum_terms(known["terms"], ring)
+            return sum_terms(known["terms"], rows // ring)
         return sum_everywhere(as_pieces(known[f"sent_{name}"]), HALVED[name])
 
     def advance(name):
         if name not in sums:
             sums[name] = [begin(name), 0]
-            line.start(sums[name][0])
+            with jax.named_scope(f"sum_{name}_0"):
+                line.start(sums[name][0])
         else:
             if sums[name][1] == 1 and name in HALVED:
                 sums[name][0].send(as_pieces(known[f"kept_{name}"]))
             try:
-                line.step(sums[name][0])
+                with jax.named_scope(f"sum_{name}_{sums[name][1]}"):
+                    line.step(sums[name][0])
                 results[name] = line.ticket
             except StopIteration:
                 return False
@@ -1057,30 +1054,30 @@
             pass
 
     kernels = {
-        "S": run_s, "K": run_k, "F": run_f, "A": run_a, "B": run_b, "Q": run_q, "O": run_o,
-        "L": run_l, "P": run_p,
+        "S": lambda: run_feed(0), "K": lambda: run_feed(1), "A": run_a, "B": run_b, "Q": run_q,
+        "O": run_o, "L": run_l, "P": run_p,
     }
     for name in PLAN:
         if name in kernels:
             kernels[name]()
         else:
             advance(name)
-    for name in "nc3":
+    for name in "c3":
         finish(name)
     down_grad, up_grad, others = known["feed"]
     arrays = [x.reshape(pieces, 2, -1, width) for x in results["3"]]
-    norms, compress_grad = results["n"], results["c"]
-    *attn_grads, grad_norm = place_squares(order, *arrays, others, norms)
+    compress_grad, norms = results["c"]
+    *attn_grads, gain_1, bias_1, gain_2, bias_2, grad_norm = place_squares(order, *arrays, others, norms)
     block_out, tokens_grad = known["block_out"], known["tokens_grad"]
     return (
         block_out,
         tokens_grad,
-        norms[0],
-        norms[1],
+        gain_1,
+        bias_1,
         *attn_grads,
-        compress_grad.astype(F32),
-        norms[2],
-        norms[3],
+        compress_grad,
+        gain_2,
+        bias_2,
         up_grad,
         down_grad,
         grad_norm.reshape(()),

time: 302 us -> 274 us (0.907)
  starting transfers between devices: 77.5 us -> 65.7 us
  other arithmetic: 22.4 us -> 12.8 us
    ppermute x71 -> x54, starting transfers between devices: 68.9 us -> 56.8 us  [swap(): return lax.ppermute(value, axis, [(i, i ^ mask) for i in range(size)])]
    add x12 -> x8, other arithmetic: 14 us -> 5.41 us  [sum_everywhere(): kept = [k[:half] + f[:half] for k, f in zip(kept, flight)]]
    pallas_call x15 -> x14, Pallas kernels: 106 us -> 104 us  [call(): pl.pallas_call(body, grid_spec=pltpu.PrefetchScalarGridSpec(num_scalar_pr...]
    unnamed x86 -> x77, local copies, waits for them, and re-layouts: 12 us -> 13 us
    ppermute x71 -> x54, waiting for transfers between devices: 72.4 us -> 72.6 us  [swap(): return lax.ppermute(value, axis, [(i, i ^ mask) for i in range(size)])]
  transfers between devices with their start and end apart: 73 -> 56, of which waited for: 30 -> 31; matrix products, arithmetic and copies ran while one was open for 9% -> 5% of each run, Pallas kernels for 27% -> 27%
where the time goes in v1:
time: 274 us; the launch traced here: 273 us
  Pallas kernels  104 us (38%)
  waiting for transfers between devices  73.3 us (27%)
  starting transfers between devices  65.7 us (24%)
  local copies, waits for them, and re-layouts  16.1 us (6%)
  other arithmetic  12.8 us (5%)
    pallas_call x14, Pallas kernels, call(): pl.pallas_call(body, grid_spec=pltpu.PrefetchScalarGridSpec(num_scalar_pr...  104 us
    ppermute x54, waiting for transfers between devices, swap(): return lax.ppermute(value, axis, [(i, i ^ mask) for i in range(size)])  72.6 us
    ppermute x54, starting transfers between devices, swap(): return lax.ppermute(value, axis, [(i, i ^ mask) for i in range(size)])  56.8 us
    unnamed x77, local copies, waits for them, and re-layouts  13 us
  transfers between devices with their start and end apart: 56, of which 31 were waited for; matrix products, arithmetic and copies ran while one was open for 5% of the time, Pallas kernels for 27%

profile of v1, /device:TPU:0, one launch (start us, length us, event | category | flops | bytes accessed | tf_op | source)
XLA Modules:
  0.0 273.1 jit_solution(10891445751270873337)
XLA Ops:
  2.3 5.2 %all-to-all-start = ((bf16[1,32,8,256]{3,1,0,2:T(8,128)(2,1)}), bf16[1,32,8,256]{3,1,0,2:T(8,128)(2,1)S(1)}, u32[]{:S(2)}, u32[]{:S(2)}) async-start(bf16[1,32,8,256]{3,1,0,2:T(8,128)(2,1)} %copy.31), calls=%async_computation | async-start | bytes 262144 | tf_op jit(solution)/shard_map/all_to_all | solution.py:936
  10.1 2.1 enter_body.1.normed
  14.4 1.6 summarize_body.1
  16.1 2.0 collective-permute-done
  21.8 5.9 %grad_active_body.1.grad_active = bf16[768,3072]{1,0:T(8,128)(2,1)} custom-call(bf16[768,768]{1,0:T(8,128)(2,1)S(1)} %bitcast.121, bf16[3072,768]{1,0:T(8,128)(2,1)S(1)} %bitcast.105), custom_call_target="tpu_custom_call" | custom-call | flops 20000000000 | bytes 1 | tf_op jit(solution)/shard_map/grad_active_body/pallas_call | solution.py:62
  32.1 2.5 project_body.1.queries
  34.9 2.9 %collective-permute-done.5 = bf16[3,32,768]{2,1,0:T(8,128)(2,1)S(1)} collective-permute-done((bf16[3,32,768]{2,1,0:T(8,128)(2,1)S(1)}, bf16[3,32,768]{2,1,0:T(8,128)(2,1)S(1)}, u32[]{:S(2)}, u32[]{:S(2)}) %collective-permute-start.5) | collective-permute-done | bytes 147488 | tf_op jit(solution)/shard_map/ppermute | solution.py:767
  38.1 1.9 collective-permute-done.7.other
  42.5 11.5 %attend_body.1 = (bf16[3,256,768]{2,1,0:T(8,128)(2,1)}, bf16[3,256,768]{2,1,0:T(8,128)(2,1)}, bf16[3,256,768]{2,1,0:T(8,128)(2,1)}, bf16[3,3072,256]{2,1,0:T(8,1...) custom-call(s32[4]{0:T(128)S(1)} %pad_add_fusion.1.meta, ...), custom_call_target="tpu_custom_call" | custom-call | flops 40000000000 | bytes 1 | tf_op jit(solution)/shard_map/attend_body/pallas_call | solution.py:62
  54.1 11.2 %feed_body.2 = (bf16[2,768,768]{2,1,0:T(8,128)(2,1)}, bf16[2,768,768]{2,1,0:T(8,128)(2,1)}, bf16[4,2,3,64,768]{4,3,2,1,0:T(8,128)(2,1)S(1)}, bf16[4,2,192,768]{3,2,1,0:T(8,128)(2,1)S(1)}) custom-call(s32[3]{0:T(128)S(1)} %pad_add_fusion.order, bf16[768,768]{1,0:T(8,128)(2,1)S(1)} %bitcast.128, bf16[768,768]{1,0:T(8,128)(2,1)S(1)} %bitcast.122, ...), custom_call_target="tpu_custom_call" | custom-call | flops 48000000000 | bytes 1 | tf_op jit(solution)/shard_map/feed_body/pallas_call | solution.py:62
  65.8 11.2 %feed_body.3 = (bf16[2,768,768]{2,1,0:T(8,128)(2,1)}, bf16[2,768,768]{2,1,0:T(8,128)(2,1)}, bf16[4,2,3,64,768]{4,3,2,1,0:T(8,128)(2,1)S(1)}, bf16[4,2,192,768]{3,2,1,0:T(8,128)(2,1)S(1)}) custom-call(s32[3]{0:T(128)S(1)} %pad_add_fusion.order, bf16[768,768]{1,0:T(8,128)(2,1)S(1)} %bitcast.129, bf16[768,768]{1,0:T(8,128)(2,1)S(1)} %bitcast.123, ...), custom_call_target="tpu_custom_call" | custom-call | flops 48000000000 | bytes 1 | tf_op jit(solution)/shard_map/feed_body/pallas_call | solution.py:62
  79.6 11.4 %feed_back_body.1 = (f32[3,256,768]{2,1,0:T(8,128)}, bf16[3,256,768]{2,1,0:T(8,128)(2,1)}, bf16[3,256,768]{2,1,0:T(8,128)(2,1)}, f32[8,768]{1,0:T(8,128)S(1)}) custom-call(s32[3]{0:T(128)S(1)} %pad_add_fusion.order, bf16[2,768,768]{2,1,0:T(8,128)(2,1)} %get-tuple-element.217.sent, bf16[2,768,768]{2,1,0:T(8,128)(2,1)} %get-tuple-element.218.kept, ...), custom_call_target="tpu_custom_call" | custom-call | flops 32000000000 | bytes 1 | tf_op jit(solution)/shard_map/feed_back_body/pallas_call | solution.py:62
  91.0 12.1 %attend_back_body.1 = (bf16[3,256,768]{2,1,0:T(8,128)(2,1)}, bf16[3,256,768]{2,1,0:T(8,128)(2,1)}, bf16[3,256,768]{2,1,0:T(8,128)(2,1)}, bf16[4,3,32,768]{3,2,1,0:T(8,128)(2,1)S(1)}, bf16[4,3,32,768]{3,2,1,0:T(8,128)(2,1)}) custom-call(s32[4]{0:T(128)S(1)} %pad_add_fusion.1.meta, bf16[3,256,768]{2,1,0:T(8,128)(2,1)} %get-tuple-element.224.grad_mixed, ...), custom_call_target="tpu_custom_call" | custom-call | flops 56000000000 | bytes 1 | tf_op jit(solution)/shard_map/attend_back_body/pallas_call | solution.py:62
  103.2 2.0 collective-permute-done.11
  110.0 8.1 %squares_body.1 = (bf16[4,2,96,768]{3,2,1,0:T(8,128)(2,1)}, bf16[4,2,96,768]{3,2,1,0:T(8,128)(2,1)}, bf16[4,2,96,768]{3,2,1,0:T(8,128)(2,1)S(1)}, bf16[4,2,96,768]{3,2,1,0:T(8,128)(2,1)S(1)}) custom-call(s32[3]{0:T(128)S(1)} %pad_add_fusion.order, bf16[768,768]{1,0:T(8,128)(2,1)S(1)} %bitcast.110, bf16[768,768]{1,0:T(8,128)(2,1)S(1)} %bitcast.126, ...), custom_call_target="tpu_custom_call" | custom-call | flops 28000000000 | bytes 1 | tf_op jit(solution)/shard_map/squares_body/pallas_call | solution.py:62
  118.6 3.3 %collective-permute-done.15 = bf16[1,384,768]{2,1,0:T(8,128)(2,1)} collective-permute-done((bf16[1,384,768]{2,1,0:T(8,128)(2,1)}, bf16[1,384,768]{2,1,0:T(8,128)(2,1)}, u32[]{:S(2)}, u32[]{:S(2)}) %collective-permute-start.15) | collective-permute-done | bytes 589856 | tf_op jit(solution)/shard_map/sum_1_2/ppermute | solution.py:767
  121.9 1.6 collective-permute-done.14
  131.9 2.0 collective-permute-done.19
  133.9 2.6 collective-permute-start.17
  136.5 1.5 collective-permute-start.16
  139.2 7.2 %collective-permute-done.17 = bf16[192,768]{1,0:T(8,128)(2,1)S(1)} collective-permute-done((bf16[192,768]{1,0:T(8,128)(2,1)S(1)}, bf16[192,768]{1,0:T(8,128)(2,1)S(1)}, u32[]{:S(2)}, u32[]{:S(2)}) %collective-permute-start.17) | collective-permute-done | bytes 294944 | tf_op jit(solution)/shard_map/sum_1_3/ppermute | solution.py:767
  147.2 1.8 collective-permute-start.26
  150.7 1.5 slice_add_fusion.5
  152.2 1.6 collective-permute-done.25
  156.9 3.4 %collective-permute-start.30 = (bf16[192,768]{1,0:T(8,128)(2,1)S(1)}, bf16[192,768]{1,0:T(8,128)(2,1)S(1)}, u32[]{:S(2)}, u32[]{:S(2)}) collective-permute-start(bf16[192,768]{1,0:T(8,128)(2,1)S(1)} %add.202), channel_id=1, source_target_pairs={{0,16},{8,24},{16,0},{24,8},{1,17},{9,25},{17,1},{25,9},{2,18},{10... | collective-permute-start | bytes 884744 | tf_op jit(solution)/shard_map/sum_1_4/ppermute | solution.py:767
  160.3 6.7 %leave_body.1 = (bf16[3,256,768]{2,1,0:T(8,128)(2,1)}, bf16[8,48,256]{2,1,0:T(8,128)(2,1)}) custom-call(s32[4]{0:T(128)S(1)} %pad_add_fusion.1.meta, bf16[4,3,32,768]{3,2,1,0:T(8,128)(2,1)S(1)} %pad_maximum_fusion.1.own, bf16[4,3,32,768]{3,2,1,0:T(8,128)(2,1)S(1)} %collective-permute-done.27.other, bf16[256,256]{1,0:T(8,128)(2,1)S(1)} %bitcast.114, ...), custom_call_target="tpu_custom_call" | custom-call | bytes 1 | tf_op jit(solution)/shard_map/leave_body/pallas_call | solution.py:62
  167.0 2.7 %collective-permute-done.23 = bf16[2,192,768]{2,1,0:T(8,128)(2,1)S(1)} collective-permute-done((bf16[2,192,768]{2,1,0:T(8,128)(2,1)S(1)}, bf16[2,192,768]{2,1,0:T(8,128)(2,1)S(1)}, u32[]{:S(2)}, u32[]{:S(2)}) %collective-permute-start.23) | collective-permute-done | bytes 589856 | tf_op jit(solution)/shard_map/sum_3_1/ppermute | solution.py:767
  174.9 2.5 collective-permute-start.34
  177.4 1.5 collective-permute-done.29
  180.2 8.0 %collective-permute-done.35 = bf16[192,768]{1,0:T(8,128)(2,1)S(1)} collective-permute-done((bf16[192,768]{1,0:T(8,128)(2,1)S(1)}, bf16[192,768]{1,0:T(8,128)(2,1)S(1)}, u32[]{:S(2)}, u32[]{:S(2)}) %collective-permute-start.35) | collective-permute-done | bytes 294944 | tf_op jit(solution)/shard_map/sum_1_5/ppermute | solution.py:767
  191.6 1.9 collective-permute-start.32
  193.5 5.2 %collective-permute-done.33 = bf16[96,768]{1,0:T(8,128)(2,1)S(1)} collective-permute-done((bf16[96,768]{1,0:T(8,128)(2,1)S(1)}, bf16[96,768]{1,0:T(8,128)(2,1)S(1)}, u32[]{:S(2)}, u32[]{:S(2)}) %collective-permute-start.33) | collective-permute-done | bytes 147488 | tf_op jit(solution)/shard_map/sum_3_3/ppermute | solution.py:767
  199.1 2.0 collective-permute-start.36
  201.2 3.7 %all-to-all-start.1 = ((bf16[8,48,256]{2,1,0:T(8,128)(2,1)}), bf16[8,48,256]{2,1,0:T(8,128)(2,1)S(1)}, u32[]{:S(2)}, u32[]{:S(2)}) async-start(bf16[8,48,256]{2,1,0:T(8,128)(2,1)} %get-tuple-element.272), calls=%async_computation.1 | async-start | bytes 393216 | tf_op jit(solution)/shard_map/sum_c_0/all_to_all | solution.py:872
  205.9 2.0 collective-permute-done.36
  208.1 1.8 collective-permute-start.38
  219.2 1.6 collective-permute-start.42
  221.0 2.3 copy-done
  223.3 7.5 %block_out_body.1 = bf16[3,256,768]{2,1,0:T(8,128)(2,1)} custom-call(s32[3]{0:T(128)S(1)} %pad_add_fusion.order, bf16[3072,768]{1,0:T(8,128)(2,1)S(1)} %copy-done, f32[3,256,768]{2,1,0:T(8,128)} %get-tuple-element.199.attended, bf16[2,768,768]{2,1,0:T(8,128)(2,1)} %get-tuple-element.306.sent, bf16[2,768,768]{2,1,0:T(8,128)(2,1)} %get-tuple-element.307.kept), custom_call_target="tpu_custom_call" | custom-call | bytes 1 | tf_op jit(solution)/shard_map/block_out_body/pallas_call | solution.py:62
  230.9 2.5 collective-permute-start.49
  233.4 12.9 %collective-permute-done.43 = bf16[1,192,768]{2,1,0:T(8,128)(2,1)S(1)} collective-permute-done((bf16[1,192,768]{2,1,0:T(8,128)(2,1)S(1)}, bf16[1,192,768]{2,1,0:T(8,128)(2,1)S(1)}, u32[]{:S(2)}, u32[]{:S(2)}) %collective-permute-start.43) | collective-permute-done | bytes 294944 | tf_op jit(solution)/shard_map/sum_3_6/ppermute | solution.py:767
  248.6 1.6 collective-permute-start.45
  250.2 1.8 collective-permute-done.51
  252.0 3.4 %collective-permute-done.50 = bf16[4,384,768]{2,1,0:T(8,128)(2,1)S(1)} collective-permute-done((bf16[4,384,768]{2,1,0:T(8,128)(2,1)S(1)}, bf16[4,384,768]{2,1,0:T(8,128)(2,1)S(1)}, u32[]{:S(2)}, u32[]{:S(2)}) %collective-permute-start.50) | collective-permute-done | bytes 2359328 | tf_op jit(solution)/shard_map/sum_1_8/ppermute | solution.py:767
  255.4 7.5 %place_feed_body.1 = (f32[3072,768]{1,0:T(8,128)}, f32[768,3072]{1,0:T(8,128)}, f32[8,768]{1,0:T(8,128)S(1)}) custom-call(s32[3]{0:T(128)S(1)} %pad_add_fusion.order, bf16[4,2,3,64,768]{4,3,2,1,0:T(8,128)(2,1)S(1)} %bitcast.103, bf16[4,2,3,64,768]{4,3,2,1,0:T(8,128)(2,1)S(1)} %bitcast.109, bf16[4,2,192,768]{3,2,1,0:T(8,128)(2,1)S(1)} %bitcast.102, ...), custom_call_target="tpu_custom_call" | custom-call | bytes 1 | tf_op jit(solution)/shard_map/place_feed_body/pallas_call | solution.py:62
  264.5 2.2 collective-permute-done.53
  266.7 1.7 collective-permute-done.52
  268.3 4.6 %place_squares_body.1 = (f32[768,768]{1,0:T(8,128)}, f32[768,768]{1,0:T(8,128)}, f32[768,768]{1,0:T(8,128)}, f32[768,768]{1,0:T(8,128)}, f32[768]{0:T(1024)}, /*...) custom-call(s32[3]{0:T(128)S(1)} %pad_add_fusion.order, bf16[4,2,96,768]{3,2,1,0:T(8,128)(2,1)S(1)} %bitcast.116, ...), custom_call_target="tpu_custom_call" | custom-call | flops 20000000000 | bytes 1 | tf_op jit(solution)/shard_map/place_squares_body/pallas_call | solution.py:62
  (211 shorter events, 65.9 us)
Async XLA Ops:
  2.3 10.7 %all-to-all-start = ((bf16[1,32,8,256]{3,1,0,2:T(8,128)(2,1)}), bf16[1,32,8,256]{3,1,0,2:T(8,128)(2,1)S(1)}, u32[]{:S(2)}, u32[]{:S(2)}) async-start(bf16[1,32,8,256]{3,1,0,2:T(8,128)(2,1)} %copy.31), calls=%async_computation | async-start | bytes 262144 | tf_op jit(solution)/shard_map/all_to_all | solution.py:936
  18.2 9.5 %collective-permute-start.1 = (bf16[3,32,768]{2,1,0:T(8,128)(2,1)S(1)}, bf16[3,32,768]{2,1,0:T(8,128)(2,1)S(1)}, u32[]{:S(2)}, u32[]{:S(2)}) collective-permute-start(bf16[3,32,768]{2,1,0:T(8,128)(2,1)S(1)} %get-tuple-element.370), channel_id=1, source_target_pairs={{0,2},{1,3},{2,0},{3,1},{4,6},{5,7},{6,4},{7,5},{8,10},{9,11},{10,... | collective-permute-start | bytes 442376 | tf_op jit(solution)/shard_map/ppermute | solution.py:767
  19.6 8.8 %collective-permute-start.2 = (bf16[3,32,768]{2,1,0:T(8,128)(2,1)S(1)}, bf16[3,32,768]{2,1,0:T(8,128)(2,1)S(1)}, u32[]{:S(2)}, u32[]{:S(2)}) collective-permute-start(bf16[3,32,768]{2,1,0:T(8,128)(2,1)S(1)} %get-tuple-element.369), channel_id=1, source_target_pairs={{0,4},{1,5},{2,6},{3,7},{4,0},{5,1},{6,2},{7,3},{8,12},{9,13},{10,... | collective-permute-start | bytes 442376 | tf_op jit(solution)/shard_map/ppermute | solution.py:767
  21.1 7.3 %collective-permute-start.3 = (bf16[3,32,768]{2,1,0:T(8,128)(2,1)S(1)}, bf16[3,32,768]{2,1,0:T(8,128)(2,1)S(1)}, u32[]{:S(2)}, u32[]{:S(2)}) collective-permute-start(bf16[3,32,768]{2,1,0:T(8,128)(2,1)S(1)} %get-tuple-element.368), channel_id=1, source_target_pairs={{0,6},{1,7},{2,4},{3,5},{4,2},{5,3},{6,0},{7,1},{8,14},{9,15},{10,... | collective-permute-start | bytes 442376 | tf_op jit(solution)/shard_map/ppermute | solution.py:767
  29.8 8.1 %collective-permute-start.5 = (bf16[3,32,768]{2,1,0:T(8,128)(2,1)S(1)}, bf16[3,32,768]{2,1,0:T(8,128)(2,1)S(1)}, u32[]{:S(2)}, u32[]{:S(2)}) collective-permute-start(bf16[3,32,768]{2,1,0:T(8,128)(2,1)S(1)} %add_convert_fusion.4), channel_id=1, source_target_pairs={{0,4},{1,5},{2,6},{3,7},{4,0},{5,1},{6,2},{7,3},{8,12},{9,13},{10,... | collective-permute-start | bytes 442376 | tf_op jit(solution)/shard_map/ppermute | solution.py:767
  30.7 7.1 %collective-permute-start.6 = (bf16[3,32,768]{2,1,0:T(8,128)(2,1)S(1)}, bf16[3,32,768]{2,1,0:T(8,128)(2,1)S(1)}, u32[]{:S(2)}, u32[]{:S(2)}) collective-permute-start(bf16[3,32,768]{2,1,0:T(8,128)(2,1)S(1)} %add_convert_fusion.4), channel_id=1, source_target_pairs={{0,6},{1,7},{2,4},{3,5},{4,2},{5,3},{6,0},{7,1},{8,14},{9,15},{10,... | collective-permute-start | bytes 442376 | tf_op jit(solution)/shard_map/ppermute | solution.py:767
  65.3 11.7 %collective-permute-start.8 = (bf16[4,384,768]{2,1,0:T(8,128)(2,1)S(1)}, bf16[4,384,768]{2,1,0:T(8,128)(2,1)S(1)}, u32[]{:S(2)}, u32[]{:S(2)}) collective-permute-start(bf16[4,384,768]{2,1,0:T(8,128)(2,1)S(1)} %bitcast.120), channel_id=1, source_target_pairs={{0,1},{1,0},{2,3},{3,2},{4,5},{5,4},{6,7},{7,6},{8,9},{9,8},{10,11... | collective-permute-start | bytes 7077896 | tf_op jit(solution)/shard_map/sum_1_0/ppermute | solution.py:767
  65.4 11.5 %collective-permute-start.9 = (bf16[4,384,768]{2,1,0:T(8,128)(2,1)S(1)}, bf16[4,384,768]{2,1,0:T(8,128)(2,1)S(1)}, u32[]{:S(2)}, u32[]{:S(2)}) collective-permute-start(bf16[4,384,768]{2,1,0:T(8,128)(2,1)S(1)} %bitcast.119), channel_id=1, source_target_pairs={{0,1},{1,0},{2,3},{3,2},{4,5},{5,4},{6,7},{7,6},{8,9},{9,8},{10,11... | collective-permute-start | bytes 7077896 | tf_op jit(solution)/shard_map/sum_1_0/ppermute | solution.py:767
  77.2 28.1 %collective-permute-start.11 = (bf16[2,384,768]{2,1,0:T(8,128)(2,1)S(1)}, bf16[2,384,768]{2,1,0:T(8,128)(2,1)S(1)}, u32[]{:S(2)}, u32[]{:S(2)}) collective-permute-start(bf16[2,384,768]{2,1,0:T(8,128)(2,1)S(1)} %get-tuple-element.349), channel_id=1, source_target_pairs={{0,4},{1,5},{2,6},{3,7},{4,0},{5,1},{6,2},{7,3},{8,12},{9,13},{10,... | collective-permute-start | bytes 3538952 | tf_op jit(solution)/shard_map/sum_1_1/ppermute | solution.py:767
  78.5 27.8 %collective-permute-start.10 = (bf16[2,384,768]{2,1,0:T(8,128)(2,1)S(1)}, bf16[2,384,768]{2,1,0:T(8,128)(2,1)S(1)}, u32[]{:S(2)}, u32[]{:S(2)}) collective-permute-start(bf16[2,384,768]{2,1,0:T(8,128)(2,1)S(1)} %get-tuple-element.351), channel_id=1, source_target_pairs={{0,2},{1,3},{2,0},{3,1},{4,6},{5,7},{6,4},{7,5},{8,10},{9,11},{10,... | collective-permute-start | bytes 3538952 | tf_op jit(solution)/shard_map/sum_1_1/ppermute | solution.py:767
  103.1 23.0 %collective-permute-start.18 = (bf16[4,3,32,768]{3,2,1,0:T(8,128)(2,1)}, bf16[4,3,32,768]{3,2,1,0:T(8,128)(2,1)}, u32[]{:S(2)}, u32[]{:S(2)}) collective-permute-start(bf16[4,3,32,768]{3,2,1,0:T(8,128)(2,1)} %get-tuple-element.232), channel_id=1, source_target_pairs={{0,1},{1,0},{2,3},{3,2},{4,5},{5,4},{6,7},{7,6},{8,9},{9,8},{10,11... | collective-permute-start | bytes 1769480 | tf_op jit(solution)/shard_map/sum_g_0/ppermute | solution.py:767
  107.3 14.6 %collective-permute-start.15 = (bf16[1,384,768]{2,1,0:T(8,128)(2,1)}, bf16[1,384,768]{2,1,0:T(8,128)(2,1)}, u32[]{:S(2)}, u32[]{:S(2)}) collective-permute-start(bf16[1,384,768]{2,1,0:T(8,128)(2,1)} %get-tuple-element.357), channel_id=1, source_target_pairs={{0,2},{1,3},{2,0},{3,1},{4,6},{5,7},{6,4},{7,5},{8,10},{9,11},{10,... | collective-permute-start | bytes 1769480 | tf_op jit(solution)/shard_map/sum_1_2/ppermute | solution.py:767
  109.3 14.2 %collective-permute-start.14 = (bf16[1,384,768]{2,1,0:T(8,128)(2,1)}, bf16[1,384,768]{2,1,0:T(8,128)(2,1)}, u32[]{:S(2)}, u32[]{:S(2)}) collective-permute-start(bf16[1,384,768]{2,1,0:T(8,128)(2,1)} %get-tuple-element.359), channel_id=1, source_target_pairs={{0,4},{1,5},{2,6},{3,7},{4,0},{5,1},{6,2},{7,3},{8,12},{9,13},{10,... | collective-permute-start | bytes 1769480 | tf_op jit(solution)/shard_map/sum_1_2/ppermute | solution.py:767
  118.1 31.1 %collective-permute-start.12 = (bf16[4,192,768]{2,1,0:T(8,128)(2,1)}, bf16[4,192,768]{2,1,0:T(8,128)(2,1)}, u32[]{:S(2)}, u32[]{:S(2)}) collective-permute-start(bf16[4,192,768]{2,1,0:T(8,128)(2,1)} %bitcast.29), channel_id=1, source_target_pairs={{0,1},{1,0},{2,3},{3,2},{4,5},{5,4},{6,7},{7,6},{8,9},{9,8},{10,11... | collective-permute-start | bytes 3538952 | tf_op jit(solution)/shard_map/sum_3_0/ppermute | solution.py:767
  118.1 31.1 %collective-permute-start.13 = (bf16[4,192,768]{2,1,0:T(8,128)(2,1)}, bf16[4,192,768]{2,1,0:T(8,128)(2,1)}, u32[]{:S(2)}, u32[]{:S(2)}) collective-permute-start(bf16[4,192,768]{2,1,0:T(8,128)(2,1)} %bitcast.30), channel_id=1, source_target_pairs={{0,1},{1,0},{2,3},{3,2},{4,5},{5,4},{6,7},{7,6},{8,9},{9,8},{10,11... | collective-permute-start | bytes 3538952 | tf_op jit(solution)/shard_map/sum_3_0/ppermute | solution.py:767
  129.5 7.0 %collective-permute-start.20 = (bf16[3,32,768]{2,1,0:T(8,128)(2,1)S(1)}, bf16[3,32,768]{2,1,0:T(8,128)(2,1)S(1)}, u32[]{:S(2)}, u32[]{:S(2)}) collective-permute-start(bf16[3,32,768]{2,1,0:T(8,128)(2,1)S(1)} %get-tuple-element.365), channel_id=1, source_target_pairs={{0,4},{1,5},{2,6},{3,7},{4,0},{5,1},{6,2},{7,3},{8,12},{9,13},{10,... | collective-permute-start | bytes 442376 | tf_op jit(solution)/shard_map/sum_g_1/ppermute | solution.py:767
  130.5 7.6 %collective-permute-start.21 = (bf16[3,32,768]{2,1,0:T(8,128)(2,1)S(1)}, bf16[3,32,768]{2,1,0:T(8,128)(2,1)S(1)}, u32[]{:S(2)}, u32[]{:S(2)}) collective-permute-start(bf16[3,32,768]{2,1,0:T(8,128)(2,1)S(1)} %get-tuple-element.364), channel_id=1, source_target_pairs={{0,6},{1,7},{2,4},{3,5},{4,2},{5,3},{6,0},{7,1},{8,14},{9,15},{10,... | collective-permute-start | bytes 442376 | tf_op jit(solution)/shard_map/sum_g_1/ppermute | solution.py:767
  133.9 12.6 %collective-permute-start.17 = (bf16[192,768]{1,0:T(8,128)(2,1)S(1)}, bf16[192,768]{1,0:T(8,128)(2,1)S(1)}, u32[]{:S(2)}, u32[]{:S(2)}) collective-permute-start(bf16[192,768]{1,0:T(8,128)(2,1)S(1)} %get-tuple-element.373), channel_id=1, source_target_pairs={{0,16},{8,24},{16,0},{24,8},{1,17},{9,25},{17,1},{25,9},{2,18},{10... | collective-permute-start | bytes 884744 | tf_op jit(solution)/shard_map/sum_1_3/ppermute | solution.py:767
  136.5 10.7 %collective-permute-start.16 = (bf16[192,768]{1,0:T(8,128)(2,1)S(1)}, bf16[192,768]{1,0:T(8,128)(2,1)S(1)}, u32[]{:S(2)}, u32[]{:S(2)}) collective-permute-start(bf16[192,768]{1,0:T(8,128)(2,1)S(1)} %get-tuple-element.375), channel_id=1, source_target_pairs={{0,8},{8,0},{16,24},{24,16},{1,9},{9,1},{17,25},{25,17},{2,10},{10... | collective-permute-start | bytes 884744 | tf_op jit(solution)/shard_map/sum_1_3/ppermute | solution.py:767
  138.1 14.0 %collective-permute-start.24 = (bf16[3,32,768]{2,1,0:T(8,128)(2,1)S(1)}, bf16[3,32,768]{2,1,0:T(8,128)(2,1)S(1)}, u32[]{:S(2)}, u32[]{:S(2)}) collective-permute-start(bf16[3,32,768]{2,1,0:T(8,128)(2,1)S(1)} %add_convert_fusion), channel_id=1, source_target_pairs={{0,2},{1,3},{2,0},{3,1},{4,6},{5,7},{6,4},{7,5},{8,10},{9,11},{10,... | collective-permute-start | bytes 442376 | tf_op jit(solution)/shard_map/sum_g_2/ppermute | solution.py:767
  146.5 7.3 %collective-permute-start.25 = (bf16[3,32,768]{2,1,0:T(8,128)(2,1)S(1)}, bf16[3,32,768]{2,1,0:T(8,128)(2,1)S(1)}, u32[]{:S(2)}, u32[]{:S(2)}) collective-permute-start(bf16[3,32,768]{2,1,0:T(8,128)(2,1)S(1)} %add_convert_fusion), channel_id=1, source_target_pairs={{0,4},{1,5},{2,6},{3,7},{4,0},{5,1},{6,2},{7,3},{8,12},{9,13},{10,... | collective-permute-start | bytes 442376 | tf_op jit(solution)/shard_map/sum_g_2/ppermute | solution.py:767
  147.2 6.6 %collective-permute-start.26 = (bf16[3,32,768]{2,1,0:T(8,128)(2,1)S(1)}, bf16[3,32,768]{2,1,0:T(8,128)(2,1)S(1)}, u32[]{:S(2)}, u32[]{:S(2)}) collective-permute-start(bf16[3,32,768]{2,1,0:T(8,128)(2,1)S(1)} %add_convert_fusion), channel_id=1, source_target_pairs={{0,6},{1,7},{2,4},{3,5},{4,2},{5,3},{6,0},{7,1},{8,14},{9,15},{10,... | collective-permute-start | bytes 442376 | tf_op jit(solution)/shard_map/sum_g_2/ppermute | solution.py:767
  154.0 15.7 %collective-permute-start.23 = (bf16[2,192,768]{2,1,0:T(8,128)(2,1)S(1)}, bf16[2,192,768]{2,1,0:T(8,128)(2,1)S(1)}, u32[]{:S(2)}, u32[]{:S(2)}) collective-permute-start(bf16[2,192,768]{2,1,0:T(8,128)(2,1)S(1)} %get-tuple-element.353), channel_id=1, source_target_pairs={{0,4},{1,5},{2,6},{3,7},{4,0},{5,1},{6,2},{7,3},{8,12},{9,13},{10,... | collective-permute-start | bytes 1769480 | tf_op jit(solution)/shard_map/sum_3_1/ppermute | solution.py:767
  155.1 15.4 %collective-permute-start.22 = (bf16[2,192,768]{2,1,0:T(8,128)(2,1)S(1)}, bf16[2,192,768]{2,1,0:T(8,128)(2,1)S(1)}, u32[]{:S(2)}, u32[]{:S(2)}) collective-permute-start(bf16[2,192,768]{2,1,0:T(8,128)(2,1)S(1)} %get-tuple-element.355), channel_id=1, source_target_pairs={{0,2},{1,3},{2,0},{3,1},{4,6},{5,7},{6,4},{7,5},{8,10},{9,11},{10,... | collective-permute-start | bytes 1769480 | tf_op jit(solution)/shard_map/sum_3_1/ppermute | solution.py:767
  156.3 16.7 %collective-permute-start.31 = (bf16[192,768]{1,0:T(8,128)(2,1)S(1)}, bf16[192,768]{1,0:T(8,128)(2,1)S(1)}, u32[]{:S(2)}, u32[]{:S(2)}) collective-permute-start(bf16[192,768]{1,0:T(8,128)(2,1)S(1)} %add.203), channel_id=1, source_target_pairs={{0,8},{8,0},{16,24},{24,16},{1,9},{9,1},{17,25},{25,17},{2,10},{10... | collective-permute-start | bytes 884744 | tf_op jit(solution)/shard_map/sum_1_4/ppermute | solution.py:767
  156.9 16.5 %collective-permute-start.30 = (bf16[192,768]{1,0:T(8,128)(2,1)S(1)}, bf16[192,768]{1,0:T(8,128)(2,1)S(1)}, u32[]{:S(2)}, u32[]{:S(2)}) collective-permute-start(bf16[192,768]{1,0:T(8,128)(2,1)S(1)} %add.202), channel_id=1, source_target_pairs={{0,16},{8,24},{16,0},{24,8},{1,17},{9,25},{17,1},{25,9},{2,18},{10... | collective-permute-start | bytes 884744 | tf_op jit(solution)/shard_map/sum_1_4/ppermute | solution.py:767
  170.6 8.3 %collective-permute-start.29 = (bf16[1,192,768]{2,1,0:T(8,128)(2,1)S(1)}, bf16[1,192,768]{2,1,0:T(8,128)(2,1)S(1)}, u32[]{:S(2)}, u32[]{:S(2)}) collective-permute-start(bf16[1,192,768]{2,1,0:T(8,128)(2,1)S(1)} %get-tuple-element.361), channel_id=1, source_target_pairs={{0,2},{1,3},{2,0},{3,1},{4,6},{5,7},{6,4},{7,5},{8,10},{9,11},{10,... | collective-permute-start | bytes 884744 | tf_op jit(solution)/shard_map/sum_3_2/ppermute | solution.py:767
  171.9 8.0 %collective-permute-start.28 = (bf16[1,192,768]{2,1,0:T(8,128)(2,1)S(1)}, bf16[1,192,768]{2,1,0:T(8,128)(2,1)S(1)}, u32[]{:S(2)}, u32[]{:S(2)}) collective-permute-start(bf16[1,192,768]{2,1,0:T(8,128)(2,1)S(1)} %get-tuple-element.363), channel_id=1, source_target_pairs={{0,4},{1,5},{2,6},{3,7},{4,0},{5,1},{6,2},{7,3},{8,12},{9,13},{10,... | collective-permute-start | bytes 884744 | tf_op jit(solution)/shard_map/sum_3_2/ppermute | solution.py:767
  173.5 14.7 %collective-permute-start.35 = (bf16[192,768]{1,0:T(8,128)(2,1)S(1)}, bf16[192,768]{1,0:T(8,128)(2,1)S(1)}, u32[]{:S(2)}, u32[]{:S(2)}) collective-permute-start(bf16[192,768]{1,0:T(8,128)(2,1)S(1)} %add.213), channel_id=1, source_target_pairs={{0,16},{8,24},{16,0},{24,8},{1,17},{9,25},{17,1},{25,9},{2,18},{10... | collective-permute-start | bytes 884744 | tf_op jit(solution)/shard_map/sum_1_5/ppermute | solution.py:767
  174.9 13.6 %collective-permute-start.34 = (bf16[192,768]{1,0:T(8,128)(2,1)S(1)}, bf16[192,768]{1,0:T(8,128)(2,1)S(1)}, u32[]{:S(2)}, u32[]{:S(2)}) collective-permute-start(bf16[192,768]{1,0:T(8,128)(2,1)S(1)} %add.212), channel_id=1, source_target_pairs={{0,8},{8,0},{16,24},{24,16},{1,9},{9,1},{17,25},{25,17},{2,10},{10... | collective-permute-start | bytes 884744 | tf_op jit(solution)/shard_map/sum_1_5/ppermute | solution.py:767
  188.5 21.4 %collective-permute-start.41 = (bf16[1,384,768]{2,1,0:T(8,128)(2,1)S(1)}, bf16[1,384,768]{2,1,0:T(8,128)(2,1)S(1)}, u32[]{:S(2)}, u32[]{:S(2)}) collective-permute-start(bf16[1,384,768]{2,1,0:T(8,128)(2,1)S(1)} %bitcast.132), channel_id=1, source_target_pairs={{0,2},{1,3},{2,0},{3,1},{4,6},{5,7},{6,4},{7,5},{8,10},{9,11},{10,... | collective-permute-start | bytes 1769480 | tf_op jit(solution)/shard_map/sum_1_6/ppermute | solution.py:767
  189.4 21.4 %collective-permute-start.40 = (bf16[1,384,768]{2,1,0:T(8,128)(2,1)S(1)}, bf16[1,384,768]{2,1,0:T(8,128)(2,1)}, u32[]{:S(2)}, u32[]{:S(2)}) collective-permute-start(bf16[1,384,768]{2,1,0:T(8,128)(2,1)S(1)} %bitcast.134), channel_id=1, source_target_pairs={{0,4},{1,5},{2,6},{3,7},{4,0},{5,1},{6,2},{7,3},{8,12},{9,13},{10,... | collective-permute-start | bytes 1769480 | tf_op jit(solution)/shard_map/sum_1_6/ppermute | solution.py:767
  190.5 8.1 %collective-permute-start.33 = (bf16[96,768]{1,0:T(8,128)(2,1)S(1)}, bf16[96,768]{1,0:T(8,128)(2,1)S(1)}, u32[]{:S(2)}, u32[]{:S(2)}) collective-permute-start(bf16[96,768]{1,0:T(8,128)(2,1)S(1)} %get-tuple-element.377), channel_id=1, source_target_pairs={{0,16},{8,24},{16,0},{24,8},{1,17},{9,25},{17,1},{25,9},{2,18},{10... | collective-permute-start | bytes 442376 | tf_op jit(solution)/shard_map/sum_3_3/ppermute | solution.py:767
  191.6 7.3 %collective-permute-start.32 = (bf16[96,768]{1,0:T(8,128)(2,1)S(1)}, bf16[96,768]{1,0:T(8,128)(2,1)S(1)}, u32[]{:S(2)}, u32[]{:S(2)}) collective-permute-start(bf16[96,768]{1,0:T(8,128)(2,1)S(1)} %get-tuple-element.379), channel_id=1, source_target_pairs={{0,8},{8,0},{16,24},{24,16},{1,9},{9,1},{17,25},{25,17},{2,10},{10... | collective-permute-start | bytes 442376 | tf_op jit(solution)/shard_map/sum_3_3/ppermute | solution.py:767
  198.9 7.0 %collective-permute-start.37 = (bf16[96,768]{1,0:T(8,128)(2,1)S(1)}, bf16[96,768]{1,0:T(8,128)(2,1)S(1)}, u32[]{:S(2)}, u32[]{:S(2)}) collective-permute-start(bf16[96,768]{1,0:T(8,128)(2,1)S(1)} %add.217), channel_id=1, source_target_pairs={{0,8},{8,0},{16,24},{24,16},{1,9},{9,1},{17,25},{25,17},{2,10},{10... | collective-permute-start | bytes 442376 | tf_op jit(solution)/shard_map/sum_3_4/ppermute | solution.py:767
  199.1 8.7 %collective-permute-start.36 = (bf16[96,768]{1,0:T(8,128)(2,1)S(1)}, bf16[96,768]{1,0:T(8,128)(2,1)S(1)}, u32[]{:S(2)}, u32[]{:S(2)}) collective-permute-start(bf16[96,768]{1,0:T(8,128)(2,1)S(1)} %add.216), channel_id=1, source_target_pairs={{0,16},{8,24},{16,0},{24,8},{1,17},{9,25},{17,1},{25,9},{2,18},{10... | collective-permute-start | bytes 442376 | tf_op jit(solution)/shard_map/sum_3_4/ppermute | solution.py:767
  201.2 11.8 %all-to-all-start.1 = ((bf16[8,48,256]{2,1,0:T(8,128)(2,1)}), bf16[8,48,256]{2,1,0:T(8,128)(2,1)S(1)}, u32[]{:S(2)}, u32[]{:S(2)}) async-start(bf16[8,48,256]{2,1,0:T(8,128)(2,1)} %get-tuple-element.272), calls=%async_computation.1 | async-start | bytes 393216 | tf_op jit(solution)/shard_map/sum_c_0/all_to_all | solution.py:872
  207.9 8.0 %collective-permute-start.39 = (bf16[96,768]{1,0:T(8,128)(2,1)S(1)}, bf16[96,768]{1,0:T(8,128)(2,1)}, u32[]{:S(2)}, u32[]{:S(2)}) collective-permute-start(bf16[96,768]{1,0:T(8,128)(2,1)S(1)} %add.219), channel_id=1, source_target_pairs={{0,16},{8,24},{16,0},{24,8},{1,17},{9,25},{17,1},{25,9},{2,18},{10... | collective-permute-start | bytes 442376 | tf_op jit(solution)/shard_map/sum_3_5/ppermute | solution.py:767
  208.1 7.8 %collective-permute-start.38 = (bf16[96,768]{1,0:T(8,128)(2,1)S(1)}, bf16[96,768]{1,0:T(8,128)(2,1)}, u32[]{:S(2)}, u32[]{:S(2)}) collective-permute-start(bf16[96,768]{1,0:T(8,128)(2,1)S(1)} %add.218), channel_id=1, source_target_pairs={{0,8},{8,0},{16,24},{24,16},{1,9},{9,1},{17,25},{25,17},{2,10},{10... | collective-permute-start | bytes 442376 | tf_op jit(solution)/shard_map/sum_3_5/ppermute | solution.py:767
  213.0 34.2 %collective-permute-start.48 = (bf16[2,384,768]{2,1,0:T(8,128)(2,1)S(1)}, bf16[2,384,768]{2,1,0:T(8,128)(2,1)S(1)}, u32[]{:S(2)}, u32[]{:S(2)}) collective-permute-start(bf16[2,384,768]{2,1,0:T(8,128)(2,1)S(1)} %constant_dynamic-update-slice_fusion.2), channel_id=1, source_target_pairs={{0,4},{1,5},{2,6},{3,7},{4,0},{5,1},{6,2},{7,3},{8,12},{9,13},{10,... | collective-permute-start | bytes 3538952 | tf_op jit(solution)/shard_map/sum_1_7/ppermute | solution.py:767
  214.5 32.8 %collective-permute-start.47 = (bf16[2,384,768]{2,1,0:T(8,128)(2,1)S(1)}, bf16[2,384,768]{2,1,0:T(8,128)(2,1)S(1)}, u32[]{:S(2)}, u32[]{:S(2)}) collective-permute-start(bf16[2,384,768]{2,1,0:T(8,128)(2,1)S(1)} %constant_dynamic-update-slice_fusion), channel_id=1, source_target_pairs={{0,2},{1,3},{2,0},{3,1},{4,6},{5,7},{6,4},{7,5},{8,10},{9,11},{10,... | collective-permute-start | bytes 3538952 | tf_op jit(solution)/shard_map/sum_1_7/ppermute | solution.py:767
  216.9 29.3 %collective-permute-start.43 = (bf16[1,192,768]{2,1,0:T(8,128)(2,1)S(1)}, bf16[1,192,768]{2,1,0:T(8,128)(2,1)S(1)}, u32[]{:S(2)}, u32[]{:S(2)}) collective-permute-start(bf16[1,192,768]{2,1,0:T(8,128)(2,1)S(1)} %bitcast.141), channel_id=1, source_target_pairs={{0,2},{1,3},{2,0},{3,1},{4,6},{5,7},{6,4},{7,5},{8,10},{9,11},{10,... | collective-permute-start | bytes 884744 | tf_op jit(solution)/shard_map/sum_3_6/ppermute | solution.py:767
  219.2 27.1 %collective-permute-start.42 = (bf16[1,192,768]{2,1,0:T(8,128)(2,1)S(1)}, bf16[1,192,768]{2,1,0:T(8,128)(2,1)S(1)}, u32[]{:S(2)}, u32[]{:S(2)}) collective-permute-start(bf16[1,192,768]{2,1,0:T(8,128)(2,1)S(1)} %bitcast.143), channel_id=1, source_target_pairs={{0,4},{1,5},{2,6},{3,7},{4,0},{5,1},{6,2},{7,3},{8,12},{9,13},{10,... | collective-permute-start | bytes 884744 | tf_op jit(solution)/shard_map/sum_3_6/ppermute | solution.py:767
  220.8 10.0 %collective-permute-start.44 = (bf16[272,256]{1,0:T(8,128)(2,1)S(1)}, bf16[272,256]{1,0:T(8,128)(2,1)S(1)}, u32[]{:S(2)}, u32[]{:S(2)}) collective-permute-start(bf16[272,256]{1,0:T(8,128)(2,1)S(1)} %pad_maximum_fusion.2), channel_id=1, source_target_pairs={{0,8},{8,0},{16,24},{24,16},{1,9},{9,1},{17,25},{25,17},{2,10},{10... | collective-permute-start | bytes 417800 | tf_op jit(solution)/shard_map/sum_c_1/ppermute | solution.py:767
  230.9 15.5 %collective-permute-start.49 = (bf16[272,256]{1,0:T(8,128)(2,1)S(1)}, bf16[272,256]{1,0:T(8,128)(2,1)S(1)}, u32[]{:S(2)}, u32[]{:S(2)}) collective-permute-start(bf16[272,256]{1,0:T(8,128)(2,1)S(1)} %add.220), channel_id=1, source_target_pairs={{0,16},{8,24},{16,0},{24,8},{1,17},{9,25},{17,1},{25,9},{2,18},{10... | collective-permute-start | bytes 417800 | tf_op jit(solution)/shard_map/sum_c_2/ppermute | solution.py:767
  247.7 7.7 %collective-permute-start.50 = (bf16[4,384,768]{2,1,0:T(8,128)(2,1)S(1)}, bf16[4,384,768]{2,1,0:T(8,128)(2,1)S(1)}, u32[]{:S(2)}, u32[]{:S(2)}) collective-permute-start(bf16[4,384,768]{2,1,0:T(8,128)(2,1)S(1)} %constant_dynamic-update-slice_fusion.8), channel_id=1, source_target_pairs={{0,1},{1,0},{2,3},{3,2},{4,5},{5,4},{6,7},{7,6},{8,9},{9,8},{10,11... | collective-permute-start | bytes 7077896 | tf_op jit(solution)/shard_map/sum_1_8/ppermute | solution.py:767
  248.2 15.3 %collective-permute-start.46 = (bf16[2,192,768]{2,1,0:T(8,128)(2,1)S(1)}, bf16[2,192,768]{2,1,0:T(8,128)(2,1)S(1)}, u32[]{:S(2)}, u32[]{:S(2)}) collective-permute-start(bf16[2,192,768]{2,1,0:T(8,128)(2,1)S(1)} %constant_dynamic-update-slice_fusion.6), channel_id=1, source_target_pairs={{0,4},{1,5},{2,6},{3,7},{4,0},{5,1},{6,2},{7,3},{8,12},{9,13},{10,... | collective-permute-start | bytes 1769480 | tf_op jit(solution)/shard_map/sum_3_7/ppermute | solution.py:767
  248.6 15.0 %collective-permute-start.45 = (bf16[2,192,768]{2,1,0:T(8,128)(2,1)S(1)}, bf16[2,192,768]{2,1,0:T(8,128)(2,1)S(1)}, u32[]{:S(2)}, u32[]{:S(2)}) collective-permute-start(bf16[2,192,768]{2,1,0:T(8,128)(2,1)S(1)} %constant_dynamic-update-slice_fusion.4), channel_id=1, source_target_pairs={{0,2},{1,3},{2,0},{3,1},{4,6},{5,7},{6,4},{7,5},{8,10},{9,11},{10,... | collective-permute-start | bytes 1769480 | tf_op jit(solution)/shard_map/sum_3_7/ppermute | solution.py:767
  (42 other events, 236.8 us)

commit v2 on v1

--- a/solution.py
+++ b/solution.py
@@ -13,7 +13,7 @@
 SCALE = HEAD_DIM ** (-0.5)
 LOW = jnp.bfloat16
 F32 = jnp.float32
-COST = 4 * 10**9
+COST = 3 * 10**9
 
 
 def dot(left_side, right_side, contract):
@@ -180,7 +180,7 @@
         [whole(*down.shape), per_seq(span, width), *([lines] * len(actives))],
         scalars=1,
         limit=24,
-        cost=0,
+        cost=6,
     )
 
 
@@ -620,12 +620,13 @@
         [whole(*x.shape) for x in arrays],
         scalars=1,
         limit=28,
-        cost=0,
-    )
-
-
-def place_squares_body(order, own_1, other_1, own_2, other_2, others, norms, *refs):
-    *outs, attn_gain, attn_bias, ffn_gain, ffn_bias, norm, total = refs
+        cost=8,
+    )
+
+
+def place_squares_body(order, *refs):
+    inputs, (others, norms, *outs), total = refs[:8], refs[8:-1], refs[-1]
+    *outs, attn_gain, attn_bias, ffn_gain, ffn_bias, norm = outs
     side = pl.program_id(0)
     ours = (side ^ order[0]) == 0
 
@@ -634,20 +635,19 @@
         total[...] = others[...]
 
     def place(first, second):
-        pieces, _, line, _ = first.shape
-
-        def one(piece, square):
+        count, _, line, width = first[0].shape
+        square = jnp.zeros((1, width), F32)
+        for at in range(2 * count):
             for source, mask, pair in ((first, order[1], outs[:2]), (second, order[2], outs[2:])):
-                for at, out in enumerate(pair):
-                    value = source[piece ^ mask, at].astype(F32)
-                    out[pl.ds(pl.multiple_of(piece * line, line), line), :] = value
+                start = pl.multiple_of((at ^ mask) * line, line)
+                for member, out in enumerate(pair):
+                    value = source[at // count][at % count, member].astype(F32)
+                    out[pl.ds(start, line), :] = value
                     square += jnp.sum(value * value, axis=0, keepdims=True)
-            return square
-
-        total[0:1, :] += lax.fori_loop(0, pieces, one, jnp.zeros((1, outs[0].shape[1]), F32))
-
-    pl.when(ours)(lambda: place(own_1, own_2))
-    pl.when(jnp.logical_not(ours))(lambda: place(other_1, other_2))
+        total[0:1, :] += square
+
+    pl.when(ours)(lambda: place(inputs[:2], inputs[4:6]))
+    pl.when(jnp.logical_not(ours))(lambda: place(inputs[2:4], inputs[6:]))
 
     @pl.when(side == 1)
     def _():
@@ -662,20 +662,19 @@
         norm[...] = jnp.sqrt(square)
 
 
-def place_squares(order, own_1, other_1, own_2, other_2, others, norms):
-    pieces, _, line, width = own_1.shape
-    arrays = (own_1, other_1, own_2, other_2, others, norms)
+def place_squares(order, others, norms, *arrays):
+    count, _, line, width = arrays[0].shape
     return call(
         place_squares_body,
         (2,),
-        (order, *arrays),
-        [shape((2 * pieces * line, width), F32)] * 4
+        (order, *arrays, others, norms),
+        [shape((4 * count * line, width), F32)] * 4
         + [shape((width,), F32)] * 4
         + [shape((1, 1), F32)],
-        [pl.BlockSpec((pieces * line, width), lambda i, m: (i, 0))] * 4
+        [pl.BlockSpec((2 * count * line, width), lambda i, m: (i, 0))] * 4
         + [result(width)] * 4
         + [result(1, 1)],
-        [whole(*x.shape) for x in arrays],
+        [whole(*x.shape) for x in (*arrays, others, norms)],
         [pltpu.VMEM(others.shape, F32)],
         scalars=1,
         limit=24,
@@ -758,7 +757,7 @@
         ],
         scalars=1,
         limit=20,
-        cost=0,
+        cost=5,
     )
 
 
@@ -800,7 +799,7 @@
     return jnp.stack(masks).astype(jnp.int32)
 
 
-def sum_everywhere(sent, halved):
+def sum_everywhere(sent, halved, parted):
     orders = krow_orders()
     flight = [swap(x, "krow", 1) for x in sent]
     kept = yield sent
@@ -836,14 +835,24 @@
             for v, f, side in zip(values, flight, sides)
         ]
     values = [v[None] for v in values]
-    for digit in reversed(range(len(orders[0]))):
+    for digit in reversed(range(1, len(orders[0]))):
         flight = [swap(v, "krow", 1 << o[digit]) for v, o in zip(values, orders)]
         ticket = yield values
         flight, values = after((flight, values), ticket)
         values = [jnp.concatenate([v, f]) for v, f in zip(values, flight)]
-    flight = [swap(v, "krow", 1) for v in values]
+    early = [swap(v, "krow", 1) for v in values] if parted else []
+    flight = [swap(v, "krow", 1 << o[0]) for v, o in zip(values, orders)]
     ticket = yield values
-    yield after([x for pair in zip(values, flight) for x in pair], ticket)
+    flight, values, early = after((flight, values, early), ticket)
+    if parted:
+        late = [swap(f, "krow", 1) for f in flight]
+        ticket = yield (flight, values, early)
+        yield after([x for color in zip(values, flight, early, late) for x in color], ticket)
+    else:
+        values = [jnp.concatenate([v, f]) for v, f in zip(values, flight)]
+        flight = [swap(v, "krow", 1) for v in values]
+        ticket = yield values
+        yield after([x for color in zip(values, flight) for x in color], ticket)
 
 
 def sum_krow(sent, kept):
@@ -906,7 +915,7 @@
         return steps
 
 
-PLAN = "S1K1AB1gQ1g3g13ggL31313c31c3Oc3c11P33"
+PLAN = "S1K1AB1gQ1gg31O13gL313c31c3c3c311P33"
 HALVED = {"1": 1, "3": 1}
 
 
@@ -1030,7 +1039,7 @@
             return sum_krow(known["sent_g"], known["kept_g"])
         if name == "c":
             return sum_terms(known["terms"], rows // ring)
-        return sum_everywhere(as_pieces(known[f"sent_{name}"]), HALVED[name])
+        return sum_everywhere(as_pieces(known[f"sent_{name}"]), HALVED[name], name == "3")
 
     def advance(name):
         if name not in sums:
@@ -1065,9 +1074,11 @@
     for name in "c3":
         finish(name)
     down_grad, up_grad, others = known["feed"]
-    arrays = [x.reshape(pieces, 2, -1, width) for x in results["3"]]
+    arrays = [x.reshape(pieces // 2, 2, -1, width) for x in results["3"]]
     compress_grad, norms = results["c"]
-    *attn_grads, gain_1, bias_1, gain_2, bias_2, grad_norm = place_squares(order, *arrays, others, norms)
+    *attn_grads, gain_1, bias_1, gain_2, bias_2, grad_norm = place_squares(
+        order, others, norms, *arrays
+    )
     block_out, tokens_grad = known["block_out"], known["tokens_grad"]
     return (
         block_out,

time: 274 us -> 264 us (0.964)
  other arithmetic: 12.8 us -> 6.91 us
  local copies, waits for them, and re-layouts: 16.1 us -> 12.6 us
    unnamed x77 -> x73, local copies, waits for them, and re-layouts: 13 us -> 9.7 us
    ppermute x54 -> x56, starting transfers between devices: 56.8 us -> 55.8 us  [swap(): return lax.ppermute(value, axis, [(i, i ^ mask) for i in range(size)])]
    ppermute x54 -> x56, waiting for transfers between devices: 72.6 us -> 73.3 us  [swap(): return lax.ppermute(value, axis, [(i, i ^ mask) for i in range(size)])]
  transfers between devices with their start and end apart: 56 -> 58, of which waited for: 31 -> 32; matrix products, arithmetic and copies ran while one was open for 5% -> 3% of each run, Pallas kernels for 27% -> 28%
where the time goes in v2:
time: 264 us; the launch traced here: 263 us
  Pallas kernels  104 us (39%)
  waiting for transfers between devices  74 us (28%)
  starting transfers between devices  64.5 us (24%)
  local copies, waits for them, and re-layouts  12.6 us (5%)
  other arithmetic  6.91 us (3%)
    pallas_call x14, Pallas kernels, call(): pl.pallas_call(body, grid_spec=pltpu.PrefetchScalarGridSpec(num_scalar_pr...  104 us
    ppermute x56, waiting for transfers between devices, swap(): return lax.ppermute(value, axis, [(i, i ^ mask) for i in range(size)])  73.3 us
    ppermute x56, starting transfers between devices, swap(): return lax.ppermute(value, axis, [(i, i ^ mask) for i in range(size)])  55.8 us
    unnamed x73, local copies, waits for them, and re-layouts  9.7 us
  transfers between devices with their start and end apart: 58, of which 32 were waited for; matrix products, arithmetic and copies ran while one was open for 3% of the time, Pallas kernels for 28%

profile of v2, /device:TPU:0, one launch (start us, length us, event | category | flops | bytes accessed | tf_op | source)
XLA Modules:
  0.0 263.3 jit_solution(16762544254364648235)
XLA Ops:
  2.3 5.2 %all-to-all-start = ((bf16[1,32,8,256]{3,1,0,2:T(8,128)(2,1)}), bf16[1,32,8,256]{3,1,0,2:T(8,128)(2,1)S(1)}, u32[]{:S(2)}, u32[]{:S(2)}) async-start(bf16[1,32,8,256]{3,1,0,2:T(8,128)(2,1)} %copy.31), calls=%async_computation | async-start | bytes 262144 | tf_op jit(solution)/shard_map/all_to_all | solution.py:945
  10.1 2.1 enter_body.1.normed
  14.4 1.6 summarize_body.1
  16.1 2.0 collective-permute-done
  19.7 1.5 collective-permute-start.2
  21.8 5.9 %grad_active_body.1.grad_active = bf16[768,3072]{1,0:T(8,128)(2,1)} custom-call(bf16[768,768]{1,0:T(8,128)(2,1)S(1)} %bitcast.126, bf16[3072,768]{1,0:T(8,128)(2,1)S(1)} %bitcast.119), custom_call_target="tpu_custom_call" | custom-call | flops 15000000512 | bytes 1 | tf_op jit(solution)/shard_map/grad_active_body/pallas_call | solution.py:62
  32.1 2.5 project_body.1.queries
  35.0 2.9 %collective-permute-done.5 = bf16[3,32,768]{2,1,0:T(8,128)(2,1)S(1)} collective-permute-done((bf16[3,32,768]{2,1,0:T(8,128)(2,1)S(1)}, bf16[3,32,768]{2,1,0:T(8,128)(2,1)S(1)}, u32[]{:S(2)}, u32[]{:S(2)}) %collective-permute-start.5) | collective-permute-done | bytes 147488 | tf_op jit(solution)/shard_map/ppermute | solution.py:766
  38.1 2.0 collective-permute-done.7.other
  42.7 12.1 %attend_body.1 = (bf16[3,256,768]{2,1,0:T(8,128)(2,1)}, bf16[3,256,768]{2,1,0:T(8,128)(2,1)}, bf16[3,256,768]{2,1,0:T(8,128)(2,1)}, bf16[3,3072,256]{2,1,0:T(8,1...) custom-call(s32[4]{0:T(128)S(1)} %pad_add_fusion.1.meta, ...), custom_call_target="tpu_custom_call" | custom-call | flops 30000001024 | bytes 1 | tf_op jit(solution)/shard_map/attend_body/pallas_call | solution.py:62
  54.8 11.2 %feed_body.2 = (bf16[2,768,768]{2,1,0:T(8,128)(2,1)}, bf16[2,768,768]{2,1,0:T(8,128)(2,1)}, bf16[4,2,3,64,768]{4,3,2,1,0:T(8,128)(2,1)S(1)}, bf16[4,2,192,768]{3,2,1,0:T(8,128)(2,1)S(1)}) custom-call(s32[3]{0:T(128)S(1)} %pad_add_fusion.order, bf16[768,768]{1,0:T(8,128)(2,1)S(1)} %bitcast.140, bf16[768,768]{1,0:T(8,128)(2,1)S(1)} %bitcast.127, ...), custom_call_target="tpu_custom_call" | custom-call | flops 35999997952 | bytes 1 | tf_op jit(solution)/shard_map/feed_body/pallas_call | solution.py:62
  66.5 11.2 %feed_body.3 = (bf16[2,768,768]{2,1,0:T(8,128)(2,1)}, bf16[2,768,768]{2,1,0:T(8,128)(2,1)}, bf16[4,2,3,64,768]{4,3,2,1,0:T(8,128)(2,1)S(1)}, bf16[4,2,192,768]{3,2,1,0:T(8,128)(2,1)S(1)}) custom-call(s32[3]{0:T(128)S(1)} %pad_add_fusion.order, bf16[768,768]{1,0:T(8,128)(2,1)S(1)} %bitcast.141, bf16[768,768]{1,0:T(8,128)(2,1)S(1)} %bitcast.128, ...), custom_call_target="tpu_custom_call" | custom-call | flops 35999997952 | bytes 1 | tf_op jit(solution)/shard_map/feed_body/pallas_call | solution.py:62
  80.3 11.4 %feed_back_body.1 = (f32[3,256,768]{2,1,0:T(8,128)}, bf16[3,256,768]{2,1,0:T(8,128)(2,1)}, bf16[3,256,768]{2,1,0:T(8,128)(2,1)}, f32[8,768]{1,0:T(8,128)S(1)}) custom-call(s32[3]{0:T(128)S(1)} %pad_add_fusion.order, bf16[2,768,768]{2,1,0:T(8,128)(2,1)} %get-tuple-element.221.sent, bf16[2,768,768]{2,1,0:T(8,128)(2,1)} %get-tuple-element.222.kept, ...), custom_call_target="tpu_custom_call" | custom-call | flops 24000000000 | bytes 1 | tf_op jit(solution)/shard_map/feed_back_body/pallas_call | solution.py:62
  91.8 12.0 %attend_back_body.1 = (bf16[3,256,768]{2,1,0:T(8,128)(2,1)}, bf16[3,256,768]{2,1,0:T(8,128)(2,1)}, bf16[3,256,768]{2,1,0:T(8,128)(2,1)}, bf16[4,3,32,768]{3,2,1,0:T(8,128)(2,1)S(1)}, bf16[4,3,32,768]{3,2,1,0:T(8,128)(2,1)S(1)}) custom-call(s32[4]{0:T(128)S(1)} %pad_add_fusion.1.meta, bf16[3,256,768]{2,1,0:T(8,128)(2,1)} %get-tuple-element.228.grad_mixed, ...), custom_call_target="tpu_custom_call" | custom-call | flops 41999998976 | bytes 1 | tf_op jit(solution)/shard_map/attend_back_body/pallas_call | solution.py:62
  103.8 2.2 collective-permute-done.11
  109.2 7.5 %squares_body.1 = (bf16[4,2,96,768]{3,2,1,0:T(8,128)(2,1)S(1)}, bf16[4,2,96,768]{3,2,1,0:T(8,128)(2,1)S(1)}, bf16[4,2,96,768]{3,2,1,0:T(8,128)(2,1)S(1)}, bf16[4,2,96,768]{3,2,1,0:T(8,128)(2,1)S(1)}) custom-call(s32[3]{0:T(128)S(1)} %pad_add_fusion.order, bf16[768,768]{1,0:T(8,128)(2,1)S(1)} %bitcast.137, bf16[768,768]{1,0:T(8,128)(2,1)S(1)} %bitcast.138, ...), custom_call_target="tpu_custom_call" | custom-call | flops 20999999488 | bytes 1 | tf_op jit(solution)/shard_map/squares_body/pallas_call | solution.py:62
  116.6 4.8 %collective-permute-done.13 = bf16[1,384,768]{2,1,0:T(8,128)(2,1)S(1)} collective-permute-done((bf16[1,384,768]{2,1,0:T(8,128)(2,1)S(1)}, bf16[1,384,768]{2,1,0:T(8,128)(2,1)S(1)}, u32[]{:S(2)}, u32[]{:S(2)}) %collective-permute-start.13) | collective-permute-done | bytes 589856 | tf_op jit(solution)/shard_map/sum_1_2/ppermute | solution.py:766
  125.0 1.5 collective-permute-start.19
  126.5 2.6 collective-permute-start.15
  129.1 1.6 collective-permute-start.14
  132.3 7.4 %collective-permute-done.15 = bf16[192,768]{1,0:T(8,128)(2,1)S(1)} collective-permute-done((bf16[192,768]{1,0:T(8,128)(2,1)S(1)}, bf16[192,768]{1,0:T(8,128)(2,1)S(1)}, u32[]{:S(2)}, u32[]{:S(2)}) %collective-permute-start.15) | collective-permute-done | bytes 294944 | tf_op jit(solution)/shard_map/sum_1_3/ppermute | solution.py:766
  140.0 1.5 collective-permute-start.26
  141.5 2.4 collective-permute-start.25
  143.9 7.5 %block_out_body.1 = bf16[3,256,768]{2,1,0:T(8,128)(2,1)} custom-call(s32[3]{0:T(128)S(1)} %pad_add_fusion.order, bf16[3072,768]{1,0:T(8,128)(2,1)S(1)} %bitcast.121, f32[3,256,768]{2,1,0:T(8,128)} %get-tuple-element.205.attended, bf16[2,768,768]{2,1,0:T(8,128)(2,1)} %get-tuple-element.265.sent, bf16[2,768,768]{2,1,0:T(8,128)(2,1)} %get-tuple-element.266.kept), custom_call_target="tpu_custom_call" | custom-call | flops 17999998976 | bytes 1 | tf_op jit(solution)/shard_map/block_out_body/pallas_call | solution.py:62
  151.4 2.1 collective-permute-done.26
  154.2 2.0 collective-permute-done.25
  156.2 1.5 collective-permute-start.22
  160.2 2.1 collective-permute-done.22
  164.6 2.9 %collective-permute-start.32 = (bf16[192,768]{1,0:T(8,128)(2,1)S(1)}, bf16[192,768]{1,0:T(8,128)(2,1)S(1)}, u32[]{:S(2)}, u32[]{:S(2)}) collective-permute-start(bf16[192,768]{1,0:T(8,128)(2,1)S(1)} %add.204), channel_id=1, source_target_pairs={{0,8},{8,0},{16,24},{24,16},{1,9},{9,1},{17,25},{25,17},{2,10},{10... | collective-permute-start | bytes 884744 | tf_op jit(solution)/shard_map/sum_1_5/ppermute | solution.py:766
  167.5 6.7 %leave_body.1 = (bf16[3,256,768]{2,1,0:T(8,128)(2,1)}, bf16[8,48,256]{2,1,0:T(8,128)(2,1)}) custom-call(s32[4]{0:T(128)S(1)} %pad_add_fusion.1.meta, bf16[4,3,32,768]{3,2,1,0:T(8,128)(2,1)S(1)} %pad_maximum_fusion.1.own, bf16[4,3,32,768]{3,2,1,0:T(8,128)(2,1)S(1)} %collective-permute-done.27.other, bf16[256,256]{1,0:T(8,128)(2,1)S(1)} %bitcast.115, ...), custom_call_target="tpu_custom_call" | custom-call | flops 15000000512 | bytes 1 | tf_op jit(solution)/shard_map/leave_body/pallas_call | solution.py:62
  174.3 4.1 %collective-permute-done.29 = bf16[2,192,768]{2,1,0:T(8,128)(2,1)S(1)} collective-permute-done((bf16[2,192,768]{2,1,0:T(8,128)(2,1)}, bf16[2,192,768]{2,1,0:T(8,128)(2,1)S(1)}, u32[]{:S(2)}, u32[]{:S(2)}) %collective-permute-start.29) | collective-permute-done | bytes 589856 | tf_op jit(solution)/shard_map/sum_3_1/ppermute | solution.py:766
  183.5 5.4 %collective-permute-done.31 = bf16[1,192,768]{2,1,0:T(8,128)(2,1)S(1)} collective-permute-done((bf16[1,192,768]{2,1,0:T(8,128)(2,1)S(1)}, bf16[1,192,768]{2,1,0:T(8,128)(2,1)S(1)}, u32[]{:S(2)}, u32[]{:S(2)}) %collective-permute-start.31) | collective-permute-done | bytes 294944 | tf_op jit(solution)/shard_map/sum_3_2/ppermute | solution.py:766
  188.9 1.5 collective-permute-done.30
  190.7 3.0 %collective-permute-start.34 = (bf16[96,768]{1,0:T(8,128)(2,1)S(1)}, bf16[96,768]{1,0:T(8,128)(2,1)S(1)}, u32[]{:S(2)}, u32[]{:S(2)}) collective-permute-start(bf16[96,768]{1,0:T(8,128)(2,1)S(1)} %get-tuple-element.391), channel_id=1, source_target_pairs={{0,8},{8,0},{16,24},{24,16},{1,9},{9,1},{17,25},{25,17},{2,10},{10... | collective-permute-start | bytes 442376 | tf_op jit(solution)/shard_map/sum_3_3/ppermute | solution.py:766
  193.7 3.6 %all-to-all-start.1 = ((bf16[8,48,256]{2,1,0:T(8,128)(2,1)}), bf16[8,48,256]{2,1,0:T(8,128)(2,1)S(1)}, u32[]{:S(2)}, u32[]{:S(2)}) async-start(bf16[8,48,256]{2,1,0:T(8,128)(2,1)} %get-tuple-element.284), calls=%async_computation.1 | async-start | bytes 393216 | tf_op jit(solution)/shard_map/sum_c_0/all_to_all | solution.py:881
  199.0 1.8 collective-permute-start.36
  204.2 1.6 collective-permute-start.51
  209.9 2.2 collective-permute-start.40
  212.1 6.9 %collective-permute-done.42 = bf16[272,256]{1,0:T(8,128)(2,1)S(1)} collective-permute-done((bf16[272,256]{1,0:T(8,128)(2,1)S(1)}, bf16[272,256]{1,0:T(8,128)(2,1)S(1)}, u32[]{:S(2)}, u32[]{:S(2)}) %collective-permute-start.42) | collective-permute-done | bytes 139296 | tf_op jit(solution)/shard_map/sum_c_1/ppermute | solution.py:766
  220.4 1.8 collective-permute-start.44
  222.2 2.1 collective-permute-start.43
  224.3 2.3 collective-permute-done.45
  227.4 10.5 %collective-permute-done.44 = bf16[1,192,768]{2,1,0:T(8,128)(2,1)S(1)} collective-permute-done((bf16[1,192,768]{2,1,0:T(8,128)(2,1)S(1)}, bf16[1,192,768]{2,1,0:T(8,128)(2,1)S(1)}, u32[]{:S(2)}, u32[]{:S(2)}) %collective-permute-start.44) | collective-permute-done | bytes 294944 | tf_op jit(solution)/shard_map/sum_3_6/ppermute | solution.py:766
  241.1 1.8 collective-permute-done.53
  243.0 3.2 %collective-permute-done.52 = bf16[4,384,768]{2,1,0:T(8,128)(2,1)S(1)} collective-permute-done((bf16[4,384,768]{2,1,0:T(8,128)(2,1)S(1)}, bf16[4,384,768]{2,1,0:T(8,128)(2,1)S(1)}, u32[]{:S(2)}, u32[]{:S(2)}) %collective-permute-start.52) | collective-permute-done | bytes 2359328 | tf_op jit(solution)/shard_map/sum_1_8/ppermute | solution.py:766
  246.2 7.5 %place_feed_body.1 = (f32[3072,768]{1,0:T(8,128)}, f32[768,3072]{1,0:T(8,128)}, f32[8,768]{1,0:T(8,128)S(1)}) custom-call(s32[3]{0:T(128)S(1)} %pad_add_fusion.order, bf16[4,2,3,64,768]{4,3,2,1,0:T(8,128)(2,1)S(1)} %bitcast.111, bf16[4,2,3,64,768]{4,3,2,1,0:T(8,128)(2,1)S(1)} %bitcast.123, bf16[4,2,192,768]{3,2,1,0:T(8,128)(2,1)S(1)} %bitcast.110, ...), custom_call_target="tpu_custom_call" | custom-call | flops 24000000000 | bytes 1 | tf_op jit(solution)/shard_map/place_feed_body/pallas_call | solution.py:62
  256.2 1.5 collective-permute-done.54
  258.5 4.6 %place_squares_body.1 = (f32[768,768]{1,0:T(8,128)}, f32[768,768]{1,0:T(8,128)}, f32[768,768]{1,0:T(8,128)}, f32[768,768]{1,0:T(8,128)}, f32[768]{0:T(1024)}, /*...) custom-call(s32[3]{0:T(128)S(1)} %pad_add_fusion.order, bf16[2,2,96,768]{3,2,1,0:T(8,128)(2,1)S(1)} %bitcast.112, ...), custom_call_target="tpu_custom_call" | custom-call | flops 15000000512 | bytes 1 | tf_op jit(solution)/shard_map/place_squares_body/pallas_call | solution.py:62
  (210 shorter events, 56.9 us)
Async XLA Ops:
  2.3 10.7 %all-to-all-start = ((bf16[1,32,8,256]{3,1,0,2:T(8,128)(2,1)}), bf16[1,32,8,256]{3,1,0,2:T(8,128)(2,1)S(1)}, u32[]{:S(2)}, u32[]{:S(2)}) async-start(bf16[1,32,8,256]{3,1,0,2:T(8,128)(2,1)} %copy.31), calls=%async_computation | async-start | bytes 262144 | tf_op jit(solution)/shard_map/all_to_all | solution.py:945
  18.2 9.5 %collective-permute-start.1 = (bf16[3,32,768]{2,1,0:T(8,128)(2,1)S(1)}, bf16[3,32,768]{2,1,0:T(8,128)(2,1)S(1)}, u32[]{:S(2)}, u32[]{:S(2)}) collective-permute-start(bf16[3,32,768]{2,1,0:T(8,128)(2,1)S(1)} %get-tuple-element.382), channel_id=1, source_target_pairs={{0,2},{1,3},{2,0},{3,1},{4,6},{5,7},{6,4},{7,5},{8,10},{9,11},{10,... | collective-permute-start | bytes 442376 | tf_op jit(solution)/shard_map/ppermute | solution.py:766
  19.7 8.8 %collective-permute-start.2 = (bf16[3,32,768]{2,1,0:T(8,128)(2,1)S(1)}, bf16[3,32,768]{2,1,0:T(8,128)(2,1)S(1)}, u32[]{:S(2)}, u32[]{:S(2)}) collective-permute-start(bf16[3,32,768]{2,1,0:T(8,128)(2,1)S(1)} %get-tuple-element.381), channel_id=1, source_target_pairs={{0,4},{1,5},{2,6},{3,7},{4,0},{5,1},{6,2},{7,3},{8,12},{9,13},{10,... | collective-permute-start | bytes 442376 | tf_op jit(solution)/shard_map/ppermute | solution.py:766
  21.1 7.3 %collective-permute-start.3 = (bf16[3,32,768]{2,1,0:T(8,128)(2,1)S(1)}, bf16[3,32,768]{2,1,0:T(8,128)(2,1)S(1)}, u32[]{:S(2)}, u32[]{:S(2)}) collective-permute-start(bf16[3,32,768]{2,1,0:T(8,128)(2,1)S(1)} %get-tuple-element.380), channel_id=1, source_target_pairs={{0,6},{1,7},{2,4},{3,5},{4,2},{5,3},{6,0},{7,1},{8,14},{9,15},{10,... | collective-permute-start | bytes 442376 | tf_op jit(solution)/shard_map/ppermute | solution.py:766
  29.8 8.1 %collective-permute-start.5 = (bf16[3,32,768]{2,1,0:T(8,128)(2,1)S(1)}, bf16[3,32,768]{2,1,0:T(8,128)(2,1)S(1)}, u32[]{:S(2)}, u32[]{:S(2)}) collective-permute-start(bf16[3,32,768]{2,1,0:T(8,128)(2,1)S(1)} %add_convert_fusion.4), channel_id=1, source_target_pairs={{0,4},{1,5},{2,6},{3,7},{4,0},{5,1},{6,2},{7,3},{8,12},{9,13},{10,... | collective-permute-start | bytes 442376 | tf_op jit(solution)/shard_map/ppermute | solution.py:766
  30.7 7.1 %collective-permute-start.6 = (bf16[3,32,768]{2,1,0:T(8,128)(2,1)S(1)}, bf16[3,32,768]{2,1,0:T(8,128)(2,1)S(1)}, u32[]{:S(2)}, u32[]{:S(2)}) collective-permute-start(bf16[3,32,768]{2,1,0:T(8,128)(2,1)S(1)} %add_convert_fusion.4), channel_id=1, source_target_pairs={{0,6},{1,7},{2,4},{3,5},{4,2},{5,3},{6,0},{7,1},{8,14},{9,15},{10,... | collective-permute-start | bytes 442376 | tf_op jit(solution)/shard_map/ppermute | solution.py:766
  66.0 11.7 %collective-permute-start.8 = (bf16[4,384,768]{2,1,0:T(8,128)(2,1)S(1)}, bf16[4,384,768]{2,1,0:T(8,128)(2,1)S(1)}, u32[]{:S(2)}, u32[]{:S(2)}) collective-permute-start(bf16[4,384,768]{2,1,0:T(8,128)(2,1)S(1)} %bitcast.125), channel_id=1, source_target_pairs={{0,1},{1,0},{2,3},{3,2},{4,5},{5,4},{6,7},{7,6},{8,9},{9,8},{10,11... | collective-permute-start | bytes 7077896 | tf_op jit(solution)/shard_map/sum_1_0/ppermute | solution.py:766
  66.1 11.5 %collective-permute-start.9 = (bf16[4,384,768]{2,1,0:T(8,128)(2,1)S(1)}, bf16[4,384,768]{2,1,0:T(8,128)(2,1)S(1)}, u32[]{:S(2)}, u32[]{:S(2)}) collective-permute-start(bf16[4,384,768]{2,1,0:T(8,128)(2,1)S(1)} %bitcast.124), channel_id=1, source_target_pairs={{0,1},{1,0},{2,3},{3,2},{4,5},{5,4},{6,7},{7,6},{8,9},{9,8},{10,11... | collective-permute-start | bytes 7077896 | tf_op jit(solution)/shard_map/sum_1_0/ppermute | solution.py:766
  77.9 28.1 %collective-permute-start.11 = (bf16[2,384,768]{2,1,0:T(8,128)(2,1)S(1)}, bf16[2,384,768]{2,1,0:T(8,128)(2,1)S(1)}, u32[]{:S(2)}, u32[]{:S(2)}) collective-permute-start(bf16[2,384,768]{2,1,0:T(8,128)(2,1)S(1)} %get-tuple-element.361), channel_id=1, source_target_pairs={{0,4},{1,5},{2,6},{3,7},{4,0},{5,1},{6,2},{7,3},{8,12},{9,13},{10,... | collective-permute-start | bytes 3538952 | tf_op jit(solution)/shard_map/sum_1_1/ppermute | solution.py:766
  79.2 27.8 %collective-permute-start.10 = (bf16[2,384,768]{2,1,0:T(8,128)(2,1)S(1)}, bf16[2,384,768]{2,1,0:T(8,128)(2,1)S(1)}, u32[]{:S(2)}, u32[]{:S(2)}) collective-permute-start(bf16[2,384,768]{2,1,0:T(8,128)(2,1)S(1)} %get-tuple-element.363), channel_id=1, source_target_pairs={{0,2},{1,3},{2,0},{3,1},{4,6},{5,7},{6,4},{7,5},{8,10},{9,11},{10,... | collective-permute-start | bytes 3538952 | tf_op jit(solution)/shard_map/sum_1_1/ppermute | solution.py:766
  103.8 19.0 %collective-permute-start.16 = (bf16[4,3,32,768]{3,2,1,0:T(8,128)(2,1)S(1)}, bf16[4,3,32,768]{3,2,1,0:T(8,128)(2,1)S(1)}, u32[]{:S(2)}, u32[]{:S(2)}) collective-permute-start(bf16[4,3,32,768]{3,2,1,0:T(8,128)(2,1)S(1)} %get-tuple-element.236), channel_id=1, source_target_pairs={{0,1},{1,0},{2,3},{3,2},{4,5},{5,4},{6,7},{7,6},{8,9},{9,8},{10,11... | collective-permute-start | bytes 1769480 | tf_op jit(solution)/shard_map/sum_g_0/ppermute | solution.py:766
  107.2 14.3 %collective-permute-start.13 = (bf16[1,384,768]{2,1,0:T(8,128)(2,1)S(1)}, bf16[1,384,768]{2,1,0:T(8,128)(2,1)S(1)}, u32[]{:S(2)}, u32[]{:S(2)}) collective-permute-start(bf16[1,384,768]{2,1,0:T(8,128)(2,1)S(1)} %get-tuple-element.369), channel_id=1, source_target_pairs={{0,2},{1,3},{2,0},{3,1},{4,6},{5,7},{6,4},{7,5},{8,10},{9,11},{10,... | collective-permute-start | bytes 1769480 | tf_op jit(solution)/shard_map/sum_1_2/ppermute | solution.py:766
  108.4 14.0 %collective-permute-start.12 = (bf16[1,384,768]{2,1,0:T(8,128)(2,1)S(1)}, bf16[1,384,768]{2,1,0:T(8,128)(2,1)S(1)}, u32[]{:S(2)}, u32[]{:S(2)}) collective-permute-start(bf16[1,384,768]{2,1,0:T(8,128)(2,1)S(1)} %get-tuple-element.371), channel_id=1, source_target_pairs={{0,4},{1,5},{2,6},{3,7},{4,0},{5,1},{6,2},{7,3},{8,12},{9,13},{10,... | collective-permute-start | bytes 1769480 | tf_op jit(solution)/shard_map/sum_1_2/ppermute | solution.py:766
  123.0 7.7 %collective-permute-start.17 = (bf16[3,32,768]{2,1,0:T(8,128)(2,1)S(1)}, bf16[3,32,768]{2,1,0:T(8,128)(2,1)S(1)}, u32[]{:S(2)}, u32[]{:S(2)}) collective-permute-start(bf16[3,32,768]{2,1,0:T(8,128)(2,1)S(1)} %get-tuple-element.378), channel_id=1, source_target_pairs={{0,2},{1,3},{2,0},{3,1},{4,6},{5,7},{6,4},{7,5},{8,10},{9,11},{10,... | collective-permute-start | bytes 442376 | tf_op jit(solution)/shard_map/sum_g_1/ppermute | solution.py:766
  124.0 6.7 %collective-permute-start.18 = (bf16[3,32,768]{2,1,0:T(8,128)(2,1)S(1)}, bf16[3,32,768]{2,1,0:T(8,128)(2,1)S(1)}, u32[]{:S(2)}, u32[]{:S(2)}) collective-permute-start(bf16[3,32,768]{2,1,0:T(8,128)(2,1)S(1)} %get-tuple-element.377), channel_id=1, source_target_pairs={{0,4},{1,5},{2,6},{3,7},{4,0},{5,1},{6,2},{7,3},{8,12},{9,13},{10,... | collective-permute-start | bytes 442376 | tf_op jit(solution)/shard_map/sum_g_1/ppermute | solution.py:766
  126.5 13.2 %collective-permute-start.15 = (bf16[192,768]{1,0:T(8,128)(2,1)S(1)}, bf16[192,768]{1,0:T(8,128)(2,1)S(1)}, u32[]{:S(2)}, u32[]{:S(2)}) collective-permute-start(bf16[192,768]{1,0:T(8,128)(2,1)S(1)} %get-tuple-element.385), channel_id=1, source_target_pairs={{0,16},{8,24},{16,0},{24,8},{1,17},{9,25},{17,1},{25,9},{2,18},{10... | collective-permute-start | bytes 884744 | tf_op jit(solution)/shard_map/sum_1_3/ppermute | solution.py:766
  129.1 10.8 %collective-permute-start.14 = (bf16[192,768]{1,0:T(8,128)(2,1)S(1)}, bf16[192,768]{1,0:T(8,128)(2,1)S(1)}, u32[]{:S(2)}, u32[]{:S(2)}) collective-permute-start(bf16[192,768]{1,0:T(8,128)(2,1)S(1)} %get-tuple-element.387), channel_id=1, source_target_pairs={{0,8},{8,0},{16,24},{24,16},{1,9},{9,1},{17,25},{25,17},{2,10},{10... | collective-permute-start | bytes 884744 | tf_op jit(solution)/shard_map/sum_1_3/ppermute | solution.py:766
  130.7 27.2 %collective-permute-start.23 = (bf16[4,192,768]{2,1,0:T(8,128)(2,1)S(1)}, bf16[4,192,768]{2,1,0:T(8,128)(2,1)S(1)}, u32[]{:S(2)}, u32[]{:S(2)}) collective-permute-start(bf16[4,192,768]{2,1,0:T(8,128)(2,1)S(1)} %bitcast.130), channel_id=1, source_target_pairs={{0,1},{1,0},{2,3},{3,2},{4,5},{5,4},{6,7},{7,6},{8,9},{9,8},{10,11... | collective-permute-start | bytes 3538952 | tf_op jit(solution)/shard_map/sum_3_0/ppermute | solution.py:766
  130.7 27.2 %collective-permute-start.24 = (bf16[4,192,768]{2,1,0:T(8,128)(2,1)S(1)}, bf16[4,192,768]{2,1,0:T(8,128)(2,1)S(1)}, u32[]{:S(2)}, u32[]{:S(2)}) collective-permute-start(bf16[4,192,768]{2,1,0:T(8,128)(2,1)S(1)} %bitcast.129), channel_id=1, source_target_pairs={{0,1},{1,0},{2,3},{3,2},{4,5},{5,4},{6,7},{7,6},{8,9},{9,8},{10,11... | collective-permute-start | bytes 3538952 | tf_op jit(solution)/shard_map/sum_3_0/ppermute | solution.py:766
  131.3 28.9 %collective-permute-start.20 = (bf16[3,32,768]{2,1,0:T(8,128)(2,1)S(1)}, bf16[3,32,768]{2,1,0:T(8,128)(2,1)S(1)}, u32[]{:S(2)}, u32[]{:S(2)}) collective-permute-start(bf16[3,32,768]{2,1,0:T(8,128)(2,1)S(1)} %add_convert_fusion), channel_id=1, source_target_pairs={{0,2},{1,3},{2,0},{3,1},{4,6},{5,7},{6,4},{7,5},{8,10},{9,11},{10,... | collective-permute-start | bytes 442376 | tf_op jit(solution)/shard_map/sum_g_2/ppermute | solution.py:766
  140.0 13.6 %collective-permute-start.26 = (bf16[192,768]{1,0:T(8,128)(2,1)S(1)}, bf16[192,768]{1,0:T(8,128)(2,1)S(1)}, u32[]{:S(2)}, u32[]{:S(2)}) collective-permute-start(bf16[192,768]{1,0:T(8,128)(2,1)S(1)} %add.203), channel_id=1, source_target_pairs={{0,8},{8,0},{16,24},{24,16},{1,9},{9,1},{17,25},{25,17},{2,10},{10... | collective-permute-start | bytes 884744 | tf_op jit(solution)/shard_map/sum_1_4/ppermute | solution.py:766
  141.5 14.7 %collective-permute-start.25 = (bf16[192,768]{1,0:T(8,128)(2,1)S(1)}, bf16[192,768]{1,0:T(8,128)(2,1)S(1)}, u32[]{:S(2)}, u32[]{:S(2)}) collective-permute-start(bf16[192,768]{1,0:T(8,128)(2,1)S(1)} %add.202), channel_id=1, source_target_pairs={{0,16},{8,24},{16,0},{24,8},{1,17},{9,25},{17,1},{25,9},{2,18},{10... | collective-permute-start | bytes 884744 | tf_op jit(solution)/shard_map/sum_1_4/ppermute | solution.py:766
  162.5 15.9 %collective-permute-start.29 = (bf16[2,192,768]{2,1,0:T(8,128)(2,1)}, bf16[2,192,768]{2,1,0:T(8,128)(2,1)S(1)}, u32[]{:S(2)}, u32[]{:S(2)}) collective-permute-start(bf16[2,192,768]{2,1,0:T(8,128)(2,1)} %get-tuple-element.365), channel_id=1, source_target_pairs={{0,4},{1,5},{2,6},{3,7},{4,0},{5,1},{6,2},{7,3},{8,12},{9,13},{10,... | collective-permute-start | bytes 1769480 | tf_op jit(solution)/shard_map/sum_3_1/ppermute | solution.py:766
  163.3 15.6 %collective-permute-start.28 = (bf16[2,192,768]{2,1,0:T(8,128)(2,1)}, bf16[2,192,768]{2,1,0:T(8,128)(2,1)S(1)}, u32[]{:S(2)}, u32[]{:S(2)}) collective-permute-start(bf16[2,192,768]{2,1,0:T(8,128)(2,1)} %get-tuple-element.367), channel_id=1, source_target_pairs={{0,2},{1,3},{2,0},{3,1},{4,6},{5,7},{6,4},{7,5},{8,10},{9,11},{10,... | collective-permute-start | bytes 1769480 | tf_op jit(solution)/shard_map/sum_3_1/ppermute | solution.py:766
  164.6 16.9 %collective-permute-start.33 = (bf16[192,768]{1,0:T(8,128)(2,1)S(1)}, bf16[192,768]{1,0:T(8,128)(2,1)S(1)}, u32[]{:S(2)}, u32[]{:S(2)}) collective-permute-start(bf16[192,768]{1,0:T(8,128)(2,1)S(1)} %add.205), channel_id=1, source_target_pairs={{0,16},{8,24},{16,0},{24,8},{1,17},{9,25},{17,1},{25,9},{2,18},{10... | collective-permute-start | bytes 884744 | tf_op jit(solution)/shard_map/sum_1_5/ppermute | solution.py:766
  164.6 16.9 %collective-permute-start.32 = (bf16[192,768]{1,0:T(8,128)(2,1)S(1)}, bf16[192,768]{1,0:T(8,128)(2,1)S(1)}, u32[]{:S(2)}, u32[]{:S(2)}) collective-permute-start(bf16[192,768]{1,0:T(8,128)(2,1)S(1)} %add.204), channel_id=1, source_target_pairs={{0,8},{8,0},{16,24},{24,16},{1,9},{9,1},{17,25},{25,17},{2,10},{10... | collective-permute-start | bytes 884744 | tf_op jit(solution)/shard_map/sum_1_5/ppermute | solution.py:766
  178.9 10.0 %collective-permute-start.31 = (bf16[1,192,768]{2,1,0:T(8,128)(2,1)S(1)}, bf16[1,192,768]{2,1,0:T(8,128)(2,1)S(1)}, u32[]{:S(2)}, u32[]{:S(2)}) collective-permute-start(bf16[1,192,768]{2,1,0:T(8,128)(2,1)S(1)} %get-tuple-element.373), channel_id=1, source_target_pairs={{0,2},{1,3},{2,0},{3,1},{4,6},{5,7},{6,4},{7,5},{8,10},{9,11},{10,... | collective-permute-start | bytes 884744 | tf_op jit(solution)/shard_map/sum_3_2/ppermute | solution.py:766
  180.4 10.0 %collective-permute-start.30 = (bf16[1,192,768]{2,1,0:T(8,128)(2,1)S(1)}, bf16[1,192,768]{2,1,0:T(8,128)(2,1)S(1)}, u32[]{:S(2)}, u32[]{:S(2)}) collective-permute-start(bf16[1,192,768]{2,1,0:T(8,128)(2,1)S(1)} %get-tuple-element.375), channel_id=1, source_target_pairs={{0,4},{1,5},{2,6},{3,7},{4,0},{5,1},{6,2},{7,3},{8,12},{9,13},{10,... | collective-permute-start | bytes 884744 | tf_op jit(solution)/shard_map/sum_3_2/ppermute | solution.py:766
  181.5 19.3 %collective-permute-start.39 = (bf16[1,384,768]{2,1,0:T(8,128)(2,1)S(1)}, bf16[1,384,768]{2,1,0:T(8,128)(2,1)S(1)}, u32[]{:S(2)}, u32[]{:S(2)}) collective-permute-start(bf16[1,384,768]{2,1,0:T(8,128)(2,1)S(1)} %bitcast.144), channel_id=1, source_target_pairs={{0,2},{1,3},{2,0},{3,1},{4,6},{5,7},{6,4},{7,5},{8,10},{9,11},{10,... | collective-permute-start | bytes 1769480 | tf_op jit(solution)/shard_map/sum_1_6/ppermute | solution.py:766
  182.7 19.2 %collective-permute-start.38 = (bf16[1,384,768]{2,1,0:T(8,128)(2,1)S(1)}, bf16[1,384,768]{2,1,0:T(8,128)(2,1)}, u32[]{:S(2)}, u32[]{:S(2)}) collective-permute-start(bf16[1,384,768]{2,1,0:T(8,128)(2,1)S(1)} %bitcast.146), channel_id=1, source_target_pairs={{0,4},{1,5},{2,6},{3,7},{4,0},{5,1},{6,2},{7,3},{8,12},{9,13},{10,... | collective-permute-start | bytes 1769480 | tf_op jit(solution)/shard_map/sum_1_6/ppermute | solution.py:766
  190.5 7.4 %collective-permute-start.35 = (bf16[96,768]{1,0:T(8,128)(2,1)S(1)}, bf16[96,768]{1,0:T(8,128)(2,1)S(1)}, u32[]{:S(2)}, u32[]{:S(2)}) collective-permute-start(bf16[96,768]{1,0:T(8,128)(2,1)S(1)} %get-tuple-element.389), channel_id=1, source_target_pairs={{0,16},{8,24},{16,0},{24,8},{1,17},{9,25},{17,1},{25,9},{2,18},{10... | collective-permute-start | bytes 442376 | tf_op jit(solution)/shard_map/sum_3_3/ppermute | solution.py:766
  190.7 7.7 %collective-permute-start.34 = (bf16[96,768]{1,0:T(8,128)(2,1)S(1)}, bf16[96,768]{1,0:T(8,128)(2,1)S(1)}, u32[]{:S(2)}, u32[]{:S(2)}) collective-permute-start(bf16[96,768]{1,0:T(8,128)(2,1)S(1)} %get-tuple-element.391), channel_id=1, source_target_pairs={{0,8},{8,0},{16,24},{24,16},{1,9},{9,1},{17,25},{25,17},{2,10},{10... | collective-permute-start | bytes 442376 | tf_op jit(solution)/shard_map/sum_3_3/ppermute | solution.py:766
  193.7 10.5 %all-to-all-start.1 = ((bf16[8,48,256]{2,1,0:T(8,128)(2,1)}), bf16[8,48,256]{2,1,0:T(8,128)(2,1)S(1)}, u32[]{:S(2)}, u32[]{:S(2)}) async-start(bf16[8,48,256]{2,1,0:T(8,128)(2,1)} %get-tuple-element.284), calls=%async_computation.1 | async-start | bytes 393216 | tf_op jit(solution)/shard_map/sum_c_0/all_to_all | solution.py:881
  198.4 8.7 %collective-permute-start.37 = (bf16[96,768]{1,0:T(8,128)(2,1)S(1)}, bf16[96,768]{1,0:T(8,128)(2,1)}, u32[]{:S(2)}, u32[]{:S(2)}) collective-permute-start(bf16[96,768]{1,0:T(8,128)(2,1)S(1)} %add.217), channel_id=1, source_target_pairs={{0,8},{8,0},{16,24},{24,16},{1,9},{9,1},{17,25},{25,17},{2,10},{10... | collective-permute-start | bytes 442376 | tf_op jit(solution)/shard_map/sum_3_4/ppermute | solution.py:766
  199.0 8.8 %collective-permute-start.36 = (bf16[96,768]{1,0:T(8,128)(2,1)S(1)}, bf16[96,768]{1,0:T(8,128)(2,1)}, u32[]{:S(2)}, u32[]{:S(2)}) collective-permute-start(bf16[96,768]{1,0:T(8,128)(2,1)S(1)} %add.216), channel_id=1, source_target_pairs={{0,16},{8,24},{16,0},{24,8},{1,17},{9,25},{17,1},{25,9},{2,18},{10... | collective-permute-start | bytes 442376 | tf_op jit(solution)/shard_map/sum_3_4/ppermute | solution.py:766
  204.2 33.8 %collective-permute-start.51 = (bf16[2,384,768]{2,1,0:T(8,128)(2,1)S(1)}, bf16[2,384,768]{2,1,0:T(8,128)(2,1)S(1)}, u32[]{:S(2)}, u32[]{:S(2)}) collective-permute-start(bf16[2,384,768]{2,1,0:T(8,128)(2,1)S(1)} %constant_dynamic-update-slice_fusion.2), channel_id=1, source_target_pairs={{0,4},{1,5},{2,6},{3,7},{4,0},{5,1},{6,2},{7,3},{8,12},{9,13},{10,... | collective-permute-start | bytes 3538952 | tf_op jit(solution)/shard_map/sum_1_7/ppermute | solution.py:766
  205.8 32.3 %collective-permute-start.50 = (bf16[2,384,768]{2,1,0:T(8,128)(2,1)S(1)}, bf16[2,384,768]{2,1,0:T(8,128)(2,1)S(1)}, u32[]{:S(2)}, u32[]{:S(2)}) collective-permute-start(bf16[2,384,768]{2,1,0:T(8,128)(2,1)S(1)} %constant_dynamic-update-slice_fusion), channel_id=1, source_target_pairs={{0,2},{1,3},{2,0},{3,1},{4,6},{5,7},{6,4},{7,5},{8,10},{9,11},{10,... | collective-permute-start | bytes 3538952 | tf_op jit(solution)/shard_map/sum_1_7/ppermute | solution.py:766
  208.7 11.7 %collective-permute-start.41 = (bf16[96,768]{1,0:T(8,128)(2,1)S(1)}, bf16[96,768]{1,0:T(8,128)(2,1)S(1)}, u32[]{:S(2)}, u32[]{:S(2)}) collective-permute-start(bf16[96,768]{1,0:T(8,128)(2,1)S(1)} %add.219), channel_id=1, source_target_pairs={{0,16},{8,24},{16,0},{24,8},{1,17},{9,25},{17,1},{25,9},{2,18},{10... | collective-permute-start | bytes 442376 | tf_op jit(solution)/shard_map/sum_3_5/ppermute | solution.py:766
  209.9 10.5 %collective-permute-start.40 = (bf16[96,768]{1,0:T(8,128)(2,1)S(1)}, bf16[96,768]{1,0:T(8,128)(2,1)S(1)}, u32[]{:S(2)}, u32[]{:S(2)}) collective-permute-start(bf16[96,768]{1,0:T(8,128)(2,1)S(1)} %add.218), channel_id=1, source_target_pairs={{0,8},{8,0},{16,24},{24,16},{1,9},{9,1},{17,25},{25,17},{2,10},{10... | collective-permute-start | bytes 442376 | tf_op jit(solution)/shard_map/sum_3_5/ppermute | solution.py:766
  212.1 6.9 %collective-permute-start.42 = (bf16[272,256]{1,0:T(8,128)(2,1)S(1)}, bf16[272,256]{1,0:T(8,128)(2,1)S(1)}, u32[]{:S(2)}, u32[]{:S(2)}) collective-permute-start(bf16[272,256]{1,0:T(8,128)(2,1)S(1)} %pad_maximum_fusion.2), channel_id=1, source_target_pairs={{0,8},{8,0},{16,24},{24,16},{1,9},{9,1},{17,25},{25,17},{2,10},{10... | collective-permute-start | bytes 417800 | tf_op jit(solution)/shard_map/sum_c_1/ppermute | solution.py:766
  219.0 7.6 %collective-permute-start.45 = (bf16[272,256]{1,0:T(8,128)(2,1)S(1)}, bf16[272,256]{1,0:T(8,128)(2,1)S(1)}, u32[]{:S(2)}, u32[]{:S(2)}) collective-permute-start(bf16[272,256]{1,0:T(8,128)(2,1)S(1)} %add.220), channel_id=1, source_target_pairs={{0,16},{8,24},{16,0},{24,8},{1,17},{9,25},{17,1},{25,9},{2,18},{10... | collective-permute-start | bytes 417800 | tf_op jit(solution)/shard_map/sum_c_2/ppermute | solution.py:766
  220.4 17.5 %collective-permute-start.44 = (bf16[1,192,768]{2,1,0:T(8,128)(2,1)S(1)}, bf16[1,192,768]{2,1,0:T(8,128)(2,1)S(1)}, u32[]{:S(2)}, u32[]{:S(2)}) collective-permute-start(bf16[1,192,768]{2,1,0:T(8,128)(2,1)S(1)} %bitcast.152), channel_id=1, source_target_pairs={{0,2},{1,3},{2,0},{3,1},{4,6},{5,7},{6,4},{7,5},{8,10},{9,11},{10,... | collective-permute-start | bytes 884744 | tf_op jit(solution)/shard_map/sum_3_6/ppermute | solution.py:766
  222.2 15.7 %collective-permute-start.43 = (bf16[1,192,768]{2,1,0:T(8,128)(2,1)S(1)}, bf16[1,192,768]{2,1,0:T(8,128)(2,1)S(1)}, u32[]{:S(2)}, u32[]{:S(2)}) collective-permute-start(bf16[1,192,768]{2,1,0:T(8,128)(2,1)S(1)} %bitcast.154), channel_id=1, source_target_pairs={{0,4},{1,5},{2,6},{3,7},{4,0},{5,1},{6,2},{7,3},{8,12},{9,13},{10,... | collective-permute-start | bytes 884744 | tf_op jit(solution)/shard_map/sum_3_6/ppermute | solution.py:766
  238.5 7.7 %collective-permute-start.52 = (bf16[4,384,768]{2,1,0:T(8,128)(2,1)S(1)}, bf16[4,384,768]{2,1,0:T(8,128)(2,1)S(1)}, u32[]{:S(2)}, u32[]{:S(2)}) collective-permute-start(bf16[4,384,768]{2,1,0:T(8,128)(2,1)S(1)} %constant_dynamic-update-slice_fusion.8), channel_id=1, source_target_pairs={{0,1},{1,0},{2,3},{3,2},{4,5},{5,4},{6,7},{7,6},{8,9},{9,8},{10,11... | collective-permute-start | bytes 7077896 | tf_op jit(solution)/shard_map/sum_1_8/ppermute | solution.py:766
  239.0 15.3 %collective-permute-start.47 = (bf16[2,192,768]{2,1,0:T(8,128)(2,1)S(1)}, bf16[2,192,768]{2,1,0:T(8,128)(2,1)S(1)}, u32[]{:S(2)}, u32[]{:S(2)}) collective-permute-start(bf16[2,192,768]{2,1,0:T(8,128)(2,1)S(1)} %constant_dynamic-update-slice_fusion.6), channel_id=1, source_target_pairs={{0,4},{1,5},{2,6},{3,7},{4,0},{5,1},{6,2},{7,3},{8,12},{9,13},{10,... | collective-permute-start | bytes 1769480 | tf_op jit(solution)/shard_map/sum_3_7/ppermute | solution.py:766
  239.9 14.4 %collective-permute-start.49 = (bf16[2,192,768]{2,1,0:T(8,128)(2,1)S(1)}, bf16[2,192,768]{2,1,0:T(8,128)(2,1)S(1)}, u32[]{:S(2)}, u32[]{:S(2)}) collective-permute-start(bf16[2,192,768]{2,1,0:T(8,128)(2,1)S(1)} %constant_dynamic-update-slice_fusion.6), channel_id=1, source_target_pairs={{0,1},{1,0},{2,3},{3,2},{4,5},{5,4},{6,7},{7,6},{8,9},{9,8},{10,11... | collective-permute-start | bytes 1769480 | tf_op jit(solution)/shard_map/sum_3_7/ppermute | solution.py:766
  239.9 15.7 %collective-permute-start.46 = (bf16[2,192,768]{2,1,0:T(8,128)(2,1)S(1)}, bf16[2,192,768]{2,1,0:T(8,128)(2,1)S(1)}, u32[]{:S(2)}, u32[]{:S(2)}) collective-permute-start(bf16[2,192,768]{2,1,0:T(8,128)(2,1)S(1)} %constant_dynamic-update-slice_fusion.4), channel_id=1, source_target_pairs={{0,2},{1,3},{2,0},{3,1},{4,6},{5,7},{6,4},{7,5},{8,10},{9,11},{10,... | collective-permute-start | bytes 1769480 | tf_op jit(solution)/shard_map/sum_3_7/ppermute | solution.py:766
  242.8 12.9 %collective-permute-start.48 = (bf16[2,192,768]{2,1,0:T(8,128)(2,1)S(1)}, bf16[2,192,768]{2,1,0:T(8,128)(2,1)S(1)}, u32[]{:S(2)}, u32[]{:S(2)}) collective-permute-start(bf16[2,192,768]{2,1,0:T(8,128)(2,1)S(1)} %constant_dynamic-update-slice_fusion.4), channel_id=1, source_target_pairs={{0,1},{1,0},{2,3},{3,2},{4,5},{5,4},{6,7},{7,6},{8,9},{9,8},{10,11... | collective-permute-start | bytes 1769480 | tf_op jit(solution)/shard_map/sum_3_7/ppermute | solution.py:766
  (43 other events, 324.3 us)

commit v3 on v2

--- a/solution.py
+++ b/solution.py
@@ -107,7 +107,7 @@
         enter_body,
         (seqs,),
         (tokens, gain, bias),
-        far(tokens.shape),
+        shape(tokens.shape),
         block,
         [block, vector(width), vector(width)],
         limit=10,
@@ -126,7 +126,7 @@
         project_body,
         (seqs,),
         (normed, weight),
-        far(normed.shape),
+        shape(normed.shape),
         block,
         [block, whole(width, width)],
         limit=10,

time: 264 us -> 262 us (level)
  transfers between devices with their start and end apart: 58 -> 58, of which waited for: 32 -> 31; matrix products, arithmetic and copies ran while one was open for 3% -> 3% of each run, Pallas kernels for 28% -> 28%
where the time goes in v3:
time: 262 us; the launch traced here: 261 us
  Pallas kernels  102 us (39%)
  waiting for transfers between devices  73.7 us (28%)
  starting transfers between devices  65.2 us (25%)
  local copies, waits for them, and re-layouts  12.2 us (5%)
  other arithmetic  6.91 us (3%)
    pallas_call x14, Pallas kernels, call(): pl.pallas_call(body, grid_spec=pltpu.PrefetchScalarGridSpec(num_scalar_pr...  102 us
    ppermute x56, waiting for transfers between devices, swap(): return lax.ppermute(value, axis, [(i, i ^ mask) for i in range(size)])  71.9 us
    ppermute x56, starting transfers between devices, swap(): return lax.ppermute(value, axis, [(i, i ^ mask) for i in range(size)])  56.4 us
    unnamed x73, local copies, waits for them, and re-layouts  9.29 us
  transfers between devices with their start and end apart: 58, of which 31 were waited for; matrix products, arithmetic and copies ran while one was open for 3% of the time, Pallas kernels for 28%

profile of v3, /device:TPU:0, one launch (start us, length us, event | category | flops | bytes accessed | tf_op | source)
XLA Modules:
  0.0 261.0 jit_solution(10966127364132512598)
XLA Ops:
  2.3 5.2 %all-to-all-start = ((bf16[1,32,8,256]{3,1,0,2:T(8,128)(2,1)}), bf16[1,32,8,256]{3,1,0,2:T(8,128)(2,1)S(1)}, u32[]{:S(2)}, u32[]{:S(2)}) async-start(bf16[1,32,8,256]{3,1,0,2:T(8,128)(2,1)} %copy.31), calls=%async_computation | async-start | bytes 262144 | tf_op jit(solution)/shard_map/all_to_all | solution.py:945
  11.2 1.8 all-to-all-done
  13.0 1.6 summarize_body.1
  14.7 2.0 collective-permute-done
  18.6 1.8 collective-permute-start.3
  20.4 5.9 %grad_active_body.1.grad_active = bf16[768,3072]{1,0:T(8,128)(2,1)} custom-call(bf16[768,768]{1,0:T(8,128)(2,1)S(1)} %bitcast.126, bf16[3072,768]{1,0:T(8,128)(2,1)S(1)} %bitcast.119), custom_call_target="tpu_custom_call" | custom-call | flops 15000000512 | bytes 1 | tf_op jit(solution)/shard_map/grad_active_body/pallas_call | solution.py:62
  28.4 1.6 collective-permute-start.6
  30.0 1.5 project_body.1.queries
  33.1 2.5 collective-permute-done.5
  35.9 2.0 collective-permute-done.7.other
  40.5 12.1 %attend_body.1 = (bf16[3,256,768]{2,1,0:T(8,128)(2,1)}, bf16[3,256,768]{2,1,0:T(8,128)(2,1)}, bf16[3,256,768]{2,1,0:T(8,128)(2,1)}, bf16[3,3072,256]{2,1,0:T(8,1...) custom-call(s32[4]{0:T(128)S(1)} %pad_add_fusion.1.meta, ...), custom_call_target="tpu_custom_call" | custom-call | flops 30000001024 | bytes 1 | tf_op jit(solution)/shard_map/attend_body/pallas_call | solution.py:62
  52.6 11.2 %feed_body.2 = (bf16[2,768,768]{2,1,0:T(8,128)(2,1)}, bf16[2,768,768]{2,1,0:T(8,128)(2,1)}, bf16[4,2,3,64,768]{4,3,2,1,0:T(8,128)(2,1)S(1)}, bf16[4,2,192,768]{3,2,1,0:T(8,128)(2,1)S(1)}) custom-call(s32[3]{0:T(128)S(1)} %pad_add_fusion.order, bf16[768,768]{1,0:T(8,128)(2,1)S(1)} %bitcast.140, bf16[768,768]{1,0:T(8,128)(2,1)S(1)} %bitcast.127, ...), custom_call_target="tpu_custom_call" | custom-call | flops 35999997952 | bytes 1 | tf_op jit(solution)/shard_map/feed_body/pallas_call | solution.py:62
  64.3 11.2 %feed_body.3 = (bf16[2,768,768]{2,1,0:T(8,128)(2,1)}, bf16[2,768,768]{2,1,0:T(8,128)(2,1)}, bf16[4,2,3,64,768]{4,3,2,1,0:T(8,128)(2,1)S(1)}, bf16[4,2,192,768]{3,2,1,0:T(8,128)(2,1)S(1)}) custom-call(s32[3]{0:T(128)S(1)} %pad_add_fusion.order, bf16[768,768]{1,0:T(8,128)(2,1)S(1)} %bitcast.141, bf16[768,768]{1,0:T(8,128)(2,1)S(1)} %bitcast.128, ...), custom_call_target="tpu_custom_call" | custom-call | flops 35999997952 | bytes 1 | tf_op jit(solution)/shard_map/feed_body/pallas_call | solution.py:62
  78.1 11.4 %feed_back_body.1 = (f32[3,256,768]{2,1,0:T(8,128)}, bf16[3,256,768]{2,1,0:T(8,128)(2,1)}, bf16[3,256,768]{2,1,0:T(8,128)(2,1)}, f32[8,768]{1,0:T(8,128)S(1)}) custom-call(s32[3]{0:T(128)S(1)} %pad_add_fusion.order, bf16[2,768,768]{2,1,0:T(8,128)(2,1)} %get-tuple-element.221.sent, bf16[2,768,768]{2,1,0:T(8,128)(2,1)} %get-tuple-element.222.kept, ...), custom_call_target="tpu_custom_call" | custom-call | flops 24000000000 | bytes 1 | tf_op jit(solution)/shard_map/feed_back_body/pallas_call | solution.py:62
  89.5 12.0 %attend_back_body.1 = (bf16[3,256,768]{2,1,0:T(8,128)(2,1)}, bf16[3,256,768]{2,1,0:T(8,128)(2,1)}, bf16[3,256,768]{2,1,0:T(8,128)(2,1)}, bf16[4,3,32,768]{3,2,1,0:T(8,128)(2,1)S(1)}, bf16[4,3,32,768]{3,2,1,0:T(8,128)(2,1)S(1)}) custom-call(s32[4]{0:T(128)S(1)} %pad_add_fusion.1.meta, bf16[3,256,768]{2,1,0:T(8,128)(2,1)} %get-tuple-element.228.grad_mixed, ...), custom_call_target="tpu_custom_call" | custom-call | flops 41999998976 | bytes 1 | tf_op jit(solution)/shard_map/attend_back_body/pallas_call | solution.py:62
  101.5 2.2 collective-permute-done.11
  107.2 7.5 %squares_body.1 = (bf16[4,2,96,768]{3,2,1,0:T(8,128)(2,1)S(1)}, bf16[4,2,96,768]{3,2,1,0:T(8,128)(2,1)S(1)}, bf16[4,2,96,768]{3,2,1,0:T(8,128)(2,1)S(1)}, bf16[4,2,96,768]{3,2,1,0:T(8,128)(2,1)S(1)}) custom-call(s32[3]{0:T(128)S(1)} %pad_add_fusion.order, bf16[768,768]{1,0:T(8,128)(2,1)S(1)} %bitcast.137, bf16[768,768]{1,0:T(8,128)(2,1)S(1)} %bitcast.138, ...), custom_call_target="tpu_custom_call" | custom-call | flops 20999999488 | bytes 1 | tf_op jit(solution)/shard_map/squares_body/pallas_call | solution.py:62
  114.7 4.4 %collective-permute-done.13 = bf16[1,384,768]{2,1,0:T(8,128)(2,1)S(1)} collective-permute-done((bf16[1,384,768]{2,1,0:T(8,128)(2,1)S(1)}, bf16[1,384,768]{2,1,0:T(8,128)(2,1)S(1)}, u32[]{:S(2)}, u32[]{:S(2)}) %collective-permute-start.13) | collective-permute-done | bytes 589856 | tf_op jit(solution)/shard_map/sum_1_2/ppermute | solution.py:766
  122.8 1.5 collective-permute-start.19
  124.3 2.6 collective-permute-start.15
  126.8 1.6 collective-permute-start.14
  130.0 7.5 %collective-permute-done.15 = bf16[192,768]{1,0:T(8,128)(2,1)S(1)} collective-permute-done((bf16[192,768]{1,0:T(8,128)(2,1)S(1)}, bf16[192,768]{1,0:T(8,128)(2,1)S(1)}, u32[]{:S(2)}, u32[]{:S(2)}) %collective-permute-start.15) | collective-permute-done | bytes 294944 | tf_op jit(solution)/shard_map/sum_1_3/ppermute | solution.py:766
  137.7 1.5 collective-permute-start.26
  139.3 2.4 collective-permute-start.25
  141.7 7.5 %block_out_body.1 = bf16[3,256,768]{2,1,0:T(8,128)(2,1)} custom-call(s32[3]{0:T(128)S(1)} %pad_add_fusion.order, bf16[3072,768]{1,0:T(8,128)(2,1)S(1)} %bitcast.121, f32[3,256,768]{2,1,0:T(8,128)} %get-tuple-element.205.attended, bf16[2,768,768]{2,1,0:T(8,128)(2,1)} %get-tuple-element.265.sent, bf16[2,768,768]{2,1,0:T(8,128)(2,1)} %get-tuple-element.266.kept), custom_call_target="tpu_custom_call" | custom-call | flops 17999998976 | bytes 1 | tf_op jit(solution)/shard_map/block_out_body/pallas_call | solution.py:62
  149.2 2.1 collective-permute-done.26
  152.3 1.7 collective-permute-done.25
  154.0 1.5 collective-permute-start.22
  158.0 2.1 collective-permute-done.22
  162.3 2.9 %collective-permute-start.32 = (bf16[192,768]{1,0:T(8,128)(2,1)S(1)}, bf16[192,768]{1,0:T(8,128)(2,1)S(1)}, u32[]{:S(2)}, u32[]{:S(2)}) collective-permute-start(bf16[192,768]{1,0:T(8,128)(2,1)S(1)} %add.204), channel_id=1, source_target_pairs={{0,8},{8,0},{16,24},{24,16},{1,9},{9,1},{17,25},{25,17},{2,10},{10... | collective-permute-start | bytes 884744 | tf_op jit(solution)/shard_map/sum_1_5/ppermute | solution.py:766
  165.3 6.7 %leave_body.1 = (bf16[3,256,768]{2,1,0:T(8,128)(2,1)}, bf16[8,48,256]{2,1,0:T(8,128)(2,1)}) custom-call(s32[4]{0:T(128)S(1)} %pad_add_fusion.1.meta, bf16[4,3,32,768]{3,2,1,0:T(8,128)(2,1)S(1)} %pad_maximum_fusion.1.own, bf16[4,3,32,768]{3,2,1,0:T(8,128)(2,1)S(1)} %collective-permute-done.27.other, bf16[256,256]{1,0:T(8,128)(2,1)S(1)} %bitcast.115, ...), custom_call_target="tpu_custom_call" | custom-call | flops 15000000512 | bytes 1 | tf_op jit(solution)/shard_map/leave_body/pallas_call | solution.py:62
  172.0 4.1 %collective-permute-done.29 = bf16[2,192,768]{2,1,0:T(8,128)(2,1)S(1)} collective-permute-done((bf16[2,192,768]{2,1,0:T(8,128)(2,1)}, bf16[2,192,768]{2,1,0:T(8,128)(2,1)S(1)}, u32[]{:S(2)}, u32[]{:S(2)}) %collective-permute-start.29) | collective-permute-done | bytes 589856 | tf_op jit(solution)/shard_map/sum_3_1/ppermute | solution.py:766
  181.6 5.4 %collective-permute-done.31 = bf16[1,192,768]{2,1,0:T(8,128)(2,1)S(1)} collective-permute-done((bf16[1,192,768]{2,1,0:T(8,128)(2,1)S(1)}, bf16[1,192,768]{2,1,0:T(8,128)(2,1)S(1)}, u32[]{:S(2)}, u32[]{:S(2)}) %collective-permute-start.31) | collective-permute-done | bytes 294944 | tf_op jit(solution)/shard_map/sum_3_2/ppermute | solution.py:766
  188.5 3.0 %collective-permute-start.34 = (bf16[96,768]{1,0:T(8,128)(2,1)S(1)}, bf16[96,768]{1,0:T(8,128)(2,1)S(1)}, u32[]{:S(2)}, u32[]{:S(2)}) collective-permute-start(bf16[96,768]{1,0:T(8,128)(2,1)S(1)} %get-tuple-element.391), channel_id=1, source_target_pairs={{0,8},{8,0},{16,24},{24,16},{1,9},{9,1},{17,25},{25,17},{2,10},{10... | collective-permute-start | bytes 442376 | tf_op jit(solution)/shard_map/sum_3_3/ppermute | solution.py:766
  191.4 3.6 %all-to-all-start.1 = ((bf16[8,48,256]{2,1,0:T(8,128)(2,1)}), bf16[8,48,256]{2,1,0:T(8,128)(2,1)S(1)}, u32[]{:S(2)}, u32[]{:S(2)}) async-start(bf16[8,48,256]{2,1,0:T(8,128)(2,1)} %get-tuple-element.284), calls=%async_computation.1 | async-start | bytes 393216 | tf_op jit(solution)/shard_map/sum_c_0/all_to_all | solution.py:881
  196.7 1.8 collective-permute-start.36
  202.9 1.9 collective-permute-start.50
  207.7 2.2 collective-permute-start.40
  209.9 6.9 %collective-permute-done.42 = bf16[272,256]{1,0:T(8,128)(2,1)S(1)} collective-permute-done((bf16[272,256]{1,0:T(8,128)(2,1)S(1)}, bf16[272,256]{1,0:T(8,128)(2,1)S(1)}, u32[]{:S(2)}, u32[]{:S(2)}) %collective-permute-start.42) | collective-permute-done | bytes 139296 | tf_op jit(solution)/shard_map/sum_c_1/ppermute | solution.py:766
  218.2 1.6 collective-permute-start.44
  219.8 2.3 collective-permute-start.43
  222.1 2.3 collective-permute-done.45
  225.2 10.5 %collective-permute-done.44 = bf16[1,192,768]{2,1,0:T(8,128)(2,1)S(1)} collective-permute-done((bf16[1,192,768]{2,1,0:T(8,128)(2,1)S(1)}, bf16[1,192,768]{2,1,0:T(8,128)(2,1)S(1)}, u32[]{:S(2)}, u32[]{:S(2)}) %collective-permute-start.44) | collective-permute-done | bytes 294944 | tf_op jit(solution)/shard_map/sum_3_6/ppermute | solution.py:766
  238.8 1.8 collective-permute-done.53
  240.7 3.2 %collective-permute-done.52 = bf16[4,384,768]{2,1,0:T(8,128)(2,1)S(1)} collective-permute-done((bf16[4,384,768]{2,1,0:T(8,128)(2,1)S(1)}, bf16[4,384,768]{2,1,0:T(8,128)(2,1)S(1)}, u32[]{:S(2)}, u32[]{:S(2)}) %collective-permute-start.52) | collective-permute-done | bytes 2359328 | tf_op jit(solution)/shard_map/sum_1_8/ppermute | solution.py:766
  244.0 7.5 %place_feed_body.1 = (f32[3072,768]{1,0:T(8,128)}, f32[768,3072]{1,0:T(8,128)}, f32[8,768]{1,0:T(8,128)S(1)}) custom-call(s32[3]{0:T(128)S(1)} %pad_add_fusion.order, bf16[4,2,3,64,768]{4,3,2,1,0:T(8,128)(2,1)S(1)} %bitcast.111, bf16[4,2,3,64,768]{4,3,2,1,0:T(8,128)(2,1)S(1)} %bitcast.123, bf16[4,2,192,768]{3,2,1,0:T(8,128)(2,1)S(1)} %bitcast.110, ...), custom_call_target="tpu_custom_call" | custom-call | flops 24000000000 | bytes 1 | tf_op jit(solution)/shard_map/place_feed_body/pallas_call | solution.py:62
  254.0 1.5 collective-permute-done.54
  256.3 4.6 %place_squares_body.1 = (f32[768,768]{1,0:T(8,128)}, f32[768,768]{1,0:T(8,128)}, f32[768,768]{1,0:T(8,128)}, f32[768,768]{1,0:T(8,128)}, f32[768]{0:T(1024)}, /*...) custom-call(s32[3]{0:T(128)S(1)} %pad_add_fusion.order, bf16[2,2,96,768]{3,2,1,0:T(8,128)(2,1)S(1)} %bitcast.112, ...), custom_call_target="tpu_custom_call" | custom-call | flops 15000000512 | bytes 1 | tf_op jit(solution)/shard_map/place_squares_body/pallas_call | solution.py:62
  (210 shorter events, 56.1 us)
Async XLA Ops:
  2.3 10.7 %all-to-all-start = ((bf16[1,32,8,256]{3,1,0,2:T(8,128)(2,1)}), bf16[1,32,8,256]{3,1,0,2:T(8,128)(2,1)S(1)}, u32[]{:S(2)}, u32[]{:S(2)}) async-start(bf16[1,32,8,256]{3,1,0,2:T(8,128)(2,1)} %copy.31), calls=%async_computation | async-start | bytes 262144 | tf_op jit(solution)/shard_map/all_to_all | solution.py:945
  16.8 9.5 %collective-permute-start.1 = (bf16[3,32,768]{2,1,0:T(8,128)(2,1)S(1)}, bf16[3,32,768]{2,1,0:T(8,128)(2,1)S(1)}, u32[]{:S(2)}, u32[]{:S(2)}) collective-permute-start(bf16[3,32,768]{2,1,0:T(8,128)(2,1)S(1)} %get-tuple-element.382), channel_id=1, source_target_pairs={{0,2},{1,3},{2,0},{3,1},{4,6},{5,7},{6,4},{7,5},{8,10},{9,11},{10,... | collective-permute-start | bytes 442376 | tf_op jit(solution)/shard_map/ppermute | solution.py:766
  17.5 8.9 %collective-permute-start.2 = (bf16[3,32,768]{2,1,0:T(8,128)(2,1)S(1)}, bf16[3,32,768]{2,1,0:T(8,128)(2,1)S(1)}, u32[]{:S(2)}, u32[]{:S(2)}) collective-permute-start(bf16[3,32,768]{2,1,0:T(8,128)(2,1)S(1)} %get-tuple-element.381), channel_id=1, source_target_pairs={{0,4},{1,5},{2,6},{3,7},{4,0},{5,1},{6,2},{7,3},{8,12},{9,13},{10,... | collective-permute-start | bytes 442376 | tf_op jit(solution)/shard_map/ppermute | solution.py:766
  18.6 7.7 %collective-permute-start.3 = (bf16[3,32,768]{2,1,0:T(8,128)(2,1)S(1)}, bf16[3,32,768]{2,1,0:T(8,128)(2,1)S(1)}, u32[]{:S(2)}, u32[]{:S(2)}) collective-permute-start(bf16[3,32,768]{2,1,0:T(8,128)(2,1)S(1)} %get-tuple-element.380), channel_id=1, source_target_pairs={{0,6},{1,7},{2,4},{3,5},{4,2},{5,3},{6,0},{7,1},{8,14},{9,15},{10,... | collective-permute-start | bytes 442376 | tf_op jit(solution)/shard_map/ppermute | solution.py:766
  27.8 7.8 %collective-permute-start.5 = (bf16[3,32,768]{2,1,0:T(8,128)(2,1)S(1)}, bf16[3,32,768]{2,1,0:T(8,128)(2,1)S(1)}, u32[]{:S(2)}, u32[]{:S(2)}) collective-permute-start(bf16[3,32,768]{2,1,0:T(8,128)(2,1)S(1)} %add_convert_fusion.4), channel_id=1, source_target_pairs={{0,4},{1,5},{2,6},{3,7},{4,0},{5,1},{6,2},{7,3},{8,12},{9,13},{10,... | collective-permute-start | bytes 442376 | tf_op jit(solution)/shard_map/ppermute | solution.py:766
  28.4 7.2 %collective-permute-start.6 = (bf16[3,32,768]{2,1,0:T(8,128)(2,1)S(1)}, bf16[3,32,768]{2,1,0:T(8,128)(2,1)S(1)}, u32[]{:S(2)}, u32[]{:S(2)}) collective-permute-start(bf16[3,32,768]{2,1,0:T(8,128)(2,1)S(1)} %add_convert_fusion.4), channel_id=1, source_target_pairs={{0,6},{1,7},{2,4},{3,5},{4,2},{5,3},{6,0},{7,1},{8,14},{9,15},{10,... | collective-permute-start | bytes 442376 | tf_op jit(solution)/shard_map/ppermute | solution.py:766
  63.8 11.7 %collective-permute-start.8 = (bf16[4,384,768]{2,1,0:T(8,128)(2,1)S(1)}, bf16[4,384,768]{2,1,0:T(8,128)(2,1)S(1)}, u32[]{:S(2)}, u32[]{:S(2)}) collective-permute-start(bf16[4,384,768]{2,1,0:T(8,128)(2,1)S(1)} %bitcast.125), channel_id=1, source_target_pairs={{0,1},{1,0},{2,3},{3,2},{4,5},{5,4},{6,7},{7,6},{8,9},{9,8},{10,11... | collective-permute-start | bytes 7077896 | tf_op jit(solution)/shard_map/sum_1_0/ppermute | solution.py:766
  63.9 11.5 %collective-permute-start.9 = (bf16[4,384,768]{2,1,0:T(8,128)(2,1)S(1)}, bf16[4,384,768]{2,1,0:T(8,128)(2,1)S(1)}, u32[]{:S(2)}, u32[]{:S(2)}) collective-permute-start(bf16[4,384,768]{2,1,0:T(8,128)(2,1)S(1)} %bitcast.124), channel_id=1, source_target_pairs={{0,1},{1,0},{2,3},{3,2},{4,5},{5,4},{6,7},{7,6},{8,9},{9,8},{10,11... | collective-permute-start | bytes 7077896 | tf_op jit(solution)/shard_map/sum_1_0/ppermute | solution.py:766
  75.7 28.1 %collective-permute-start.11 = (bf16[2,384,768]{2,1,0:T(8,128)(2,1)S(1)}, bf16[2,384,768]{2,1,0:T(8,128)(2,1)S(1)}, u32[]{:S(2)}, u32[]{:S(2)}) collective-permute-start(bf16[2,384,768]{2,1,0:T(8,128)(2,1)S(1)} %get-tuple-element.361), channel_id=1, source_target_pairs={{0,4},{1,5},{2,6},{3,7},{4,0},{5,1},{6,2},{7,3},{8,12},{9,13},{10,... | collective-permute-start | bytes 3538952 | tf_op jit(solution)/shard_map/sum_1_1/ppermute | solution.py:766
  76.8 27.8 %collective-permute-start.10 = (bf16[2,384,768]{2,1,0:T(8,128)(2,1)S(1)}, bf16[2,384,768]{2,1,0:T(8,128)(2,1)S(1)}, u32[]{:S(2)}, u32[]{:S(2)}) collective-permute-start(bf16[2,384,768]{2,1,0:T(8,128)(2,1)S(1)} %get-tuple-element.363), channel_id=1, source_target_pairs={{0,2},{1,3},{2,0},{3,1},{4,6},{5,7},{6,4},{7,5},{8,10},{9,11},{10,... | collective-permute-start | bytes 3538952 | tf_op jit(solution)/shard_map/sum_1_1/ppermute | solution.py:766
  101.5 19.0 %collective-permute-start.16 = (bf16[4,3,32,768]{3,2,1,0:T(8,128)(2,1)S(1)}, bf16[4,3,32,768]{3,2,1,0:T(8,128)(2,1)S(1)}, u32[]{:S(2)}, u32[]{:S(2)}) collective-permute-start(bf16[4,3,32,768]{3,2,1,0:T(8,128)(2,1)S(1)} %get-tuple-element.236), channel_id=1, source_target_pairs={{0,1},{1,0},{2,3},{3,2},{4,5},{5,4},{6,7},{7,6},{8,9},{9,8},{10,11... | collective-permute-start | bytes 1769480 | tf_op jit(solution)/shard_map/sum_g_0/ppermute | solution.py:766
  104.8 14.3 %collective-permute-start.13 = (bf16[1,384,768]{2,1,0:T(8,128)(2,1)S(1)}, bf16[1,384,768]{2,1,0:T(8,128)(2,1)S(1)}, u32[]{:S(2)}, u32[]{:S(2)}) collective-permute-start(bf16[1,384,768]{2,1,0:T(8,128)(2,1)S(1)} %get-tuple-element.369), channel_id=1, source_target_pairs={{0,2},{1,3},{2,0},{3,1},{4,6},{5,7},{6,4},{7,5},{8,10},{9,11},{10,... | collective-permute-start | bytes 1769480 | tf_op jit(solution)/shard_map/sum_1_2/ppermute | solution.py:766
  106.1 14.0 %collective-permute-start.12 = (bf16[1,384,768]{2,1,0:T(8,128)(2,1)S(1)}, bf16[1,384,768]{2,1,0:T(8,128)(2,1)S(1)}, u32[]{:S(2)}, u32[]{:S(2)}) collective-permute-start(bf16[1,384,768]{2,1,0:T(8,128)(2,1)S(1)} %get-tuple-element.371), channel_id=1, source_target_pairs={{0,4},{1,5},{2,6},{3,7},{4,0},{5,1},{6,2},{7,3},{8,12},{9,13},{10,... | collective-permute-start | bytes 1769480 | tf_op jit(solution)/shard_map/sum_1_2/ppermute | solution.py:766
  120.7 7.7 %collective-permute-start.17 = (bf16[3,32,768]{2,1,0:T(8,128)(2,1)S(1)}, bf16[3,32,768]{2,1,0:T(8,128)(2,1)S(1)}, u32[]{:S(2)}, u32[]{:S(2)}) collective-permute-start(bf16[3,32,768]{2,1,0:T(8,128)(2,1)S(1)} %get-tuple-element.378), channel_id=1, source_target_pairs={{0,2},{1,3},{2,0},{3,1},{4,6},{5,7},{6,4},{7,5},{8,10},{9,11},{10,... | collective-permute-start | bytes 442376 | tf_op jit(solution)/shard_map/sum_g_1/ppermute | solution.py:766
  121.7 6.8 %collective-permute-start.18 = (bf16[3,32,768]{2,1,0:T(8,128)(2,1)S(1)}, bf16[3,32,768]{2,1,0:T(8,128)(2,1)S(1)}, u32[]{:S(2)}, u32[]{:S(2)}) collective-permute-start(bf16[3,32,768]{2,1,0:T(8,128)(2,1)S(1)} %get-tuple-element.377), channel_id=1, source_target_pairs={{0,4},{1,5},{2,6},{3,7},{4,0},{5,1},{6,2},{7,3},{8,12},{9,13},{10,... | collective-permute-start | bytes 442376 | tf_op jit(solution)/shard_map/sum_g_1/ppermute | solution.py:766
  124.3 13.2 %collective-permute-start.15 = (bf16[192,768]{1,0:T(8,128)(2,1)S(1)}, bf16[192,768]{1,0:T(8,128)(2,1)S(1)}, u32[]{:S(2)}, u32[]{:S(2)}) collective-permute-start(bf16[192,768]{1,0:T(8,128)(2,1)S(1)} %get-tuple-element.385), channel_id=1, source_target_pairs={{0,16},{8,24},{16,0},{24,8},{1,17},{9,25},{17,1},{25,9},{2,18},{10... | collective-permute-start | bytes 884744 | tf_op jit(solution)/shard_map/sum_1_3/ppermute | solution.py:766
  126.8 10.8 %collective-permute-start.14 = (bf16[192,768]{1,0:T(8,128)(2,1)S(1)}, bf16[192,768]{1,0:T(8,128)(2,1)S(1)}, u32[]{:S(2)}, u32[]{:S(2)}) collective-permute-start(bf16[192,768]{1,0:T(8,128)(2,1)S(1)} %get-tuple-element.387), channel_id=1, source_target_pairs={{0,8},{8,0},{16,24},{24,16},{1,9},{9,1},{17,25},{25,17},{2,10},{10... | collective-permute-start | bytes 884744 | tf_op jit(solution)/shard_map/sum_1_3/ppermute | solution.py:766
  128.4 27.2 %collective-permute-start.23 = (bf16[4,192,768]{2,1,0:T(8,128)(2,1)S(1)}, bf16[4,192,768]{2,1,0:T(8,128)(2,1)S(1)}, u32[]{:S(2)}, u32[]{:S(2)}) collective-permute-start(bf16[4,192,768]{2,1,0:T(8,128)(2,1)S(1)} %bitcast.130), channel_id=1, source_target_pairs={{0,1},{1,0},{2,3},{3,2},{4,5},{5,4},{6,7},{7,6},{8,9},{9,8},{10,11... | collective-permute-start | bytes 3538952 | tf_op jit(solution)/shard_map/sum_3_0/ppermute | solution.py:766
  128.4 27.2 %collective-permute-start.24 = (bf16[4,192,768]{2,1,0:T(8,128)(2,1)S(1)}, bf16[4,192,768]{2,1,0:T(8,128)(2,1)S(1)}, u32[]{:S(2)}, u32[]{:S(2)}) collective-permute-start(bf16[4,192,768]{2,1,0:T(8,128)(2,1)S(1)} %bitcast.129), channel_id=1, source_target_pairs={{0,1},{1,0},{2,3},{3,2},{4,5},{5,4},{6,7},{7,6},{8,9},{9,8},{10,11... | collective-permute-start | bytes 3538952 | tf_op jit(solution)/shard_map/sum_3_0/ppermute | solution.py:766
  129.0 28.9 %collective-permute-start.20 = (bf16[3,32,768]{2,1,0:T(8,128)(2,1)S(1)}, bf16[3,32,768]{2,1,0:T(8,128)(2,1)S(1)}, u32[]{:S(2)}, u32[]{:S(2)}) collective-permute-start(bf16[3,32,768]{2,1,0:T(8,128)(2,1)S(1)} %add_convert_fusion), channel_id=1, source_target_pairs={{0,2},{1,3},{2,0},{3,1},{4,6},{5,7},{6,4},{7,5},{8,10},{9,11},{10,... | collective-permute-start | bytes 442376 | tf_op jit(solution)/shard_map/sum_g_2/ppermute | solution.py:766
  137.7 13.6 %collective-permute-start.26 = (bf16[192,768]{1,0:T(8,128)(2,1)S(1)}, bf16[192,768]{1,0:T(8,128)(2,1)S(1)}, u32[]{:S(2)}, u32[]{:S(2)}) collective-permute-start(bf16[192,768]{1,0:T(8,128)(2,1)S(1)} %add.203), channel_id=1, source_target_pairs={{0,8},{8,0},{16,24},{24,16},{1,9},{9,1},{17,25},{25,17},{2,10},{10... | collective-permute-start | bytes 884744 | tf_op jit(solution)/shard_map/sum_1_4/ppermute | solution.py:766
  139.3 14.7 %collective-permute-start.25 = (bf16[192,768]{1,0:T(8,128)(2,1)S(1)}, bf16[192,768]{1,0:T(8,128)(2,1)S(1)}, u32[]{:S(2)}, u32[]{:S(2)}) collective-permute-start(bf16[192,768]{1,0:T(8,128)(2,1)S(1)} %add.202), channel_id=1, source_target_pairs={{0,16},{8,24},{16,0},{24,8},{1,17},{9,25},{17,1},{25,9},{2,18},{10... | collective-permute-start | bytes 884744 | tf_op jit(solution)/shard_map/sum_1_4/ppermute | solution.py:766
  160.2 15.9 %collective-permute-start.29 = (bf16[2,192,768]{2,1,0:T(8,128)(2,1)}, bf16[2,192,768]{2,1,0:T(8,128)(2,1)S(1)}, u32[]{:S(2)}, u32[]{:S(2)}) collective-permute-start(bf16[2,192,768]{2,1,0:T(8,128)(2,1)} %get-tuple-element.365), channel_id=1, source_target_pairs={{0,4},{1,5},{2,6},{3,7},{4,0},{5,1},{6,2},{7,3},{8,12},{9,13},{10,... | collective-permute-start | bytes 1769480 | tf_op jit(solution)/shard_map/sum_3_1/ppermute | solution.py:766
  161.3 15.6 %collective-permute-start.28 = (bf16[2,192,768]{2,1,0:T(8,128)(2,1)}, bf16[2,192,768]{2,1,0:T(8,128)(2,1)S(1)}, u32[]{:S(2)}, u32[]{:S(2)}) collective-permute-start(bf16[2,192,768]{2,1,0:T(8,128)(2,1)} %get-tuple-element.367), channel_id=1, source_target_pairs={{0,2},{1,3},{2,0},{3,1},{4,6},{5,7},{6,4},{7,5},{8,10},{9,11},{10,... | collective-permute-start | bytes 1769480 | tf_op jit(solution)/shard_map/sum_3_1/ppermute | solution.py:766
  162.3 16.7 %collective-permute-start.33 = (bf16[192,768]{1,0:T(8,128)(2,1)S(1)}, bf16[192,768]{1,0:T(8,128)(2,1)S(1)}, u32[]{:S(2)}, u32[]{:S(2)}) collective-permute-start(bf16[192,768]{1,0:T(8,128)(2,1)S(1)} %add.205), channel_id=1, source_target_pairs={{0,16},{8,24},{16,0},{24,8},{1,17},{9,25},{17,1},{25,9},{2,18},{10... | collective-permute-start | bytes 884744 | tf_op jit(solution)/shard_map/sum_1_5/ppermute | solution.py:766
  162.3 16.7 %collective-permute-start.32 = (bf16[192,768]{1,0:T(8,128)(2,1)S(1)}, bf16[192,768]{1,0:T(8,128)(2,1)S(1)}, u32[]{:S(2)}, u32[]{:S(2)}) collective-permute-start(bf16[192,768]{1,0:T(8,128)(2,1)S(1)} %add.204), channel_id=1, source_target_pairs={{0,8},{8,0},{16,24},{24,16},{1,9},{9,1},{17,25},{25,17},{2,10},{10... | collective-permute-start | bytes 884744 | tf_op jit(solution)/shard_map/sum_1_5/ppermute | solution.py:766
  177.0 10.0 %collective-permute-start.31 = (bf16[1,192,768]{2,1,0:T(8,128)(2,1)S(1)}, bf16[1,192,768]{2,1,0:T(8,128)(2,1)S(1)}, u32[]{:S(2)}, u32[]{:S(2)}) collective-permute-start(bf16[1,192,768]{2,1,0:T(8,128)(2,1)S(1)} %get-tuple-element.373), channel_id=1, source_target_pairs={{0,2},{1,3},{2,0},{3,1},{4,6},{5,7},{6,4},{7,5},{8,10},{9,11},{10,... | collective-permute-start | bytes 884744 | tf_op jit(solution)/shard_map/sum_3_2/ppermute | solution.py:766
  178.1 10.0 %collective-permute-start.30 = (bf16[1,192,768]{2,1,0:T(8,128)(2,1)S(1)}, bf16[1,192,768]{2,1,0:T(8,128)(2,1)S(1)}, u32[]{:S(2)}, u32[]{:S(2)}) collective-permute-start(bf16[1,192,768]{2,1,0:T(8,128)(2,1)S(1)} %get-tuple-element.375), channel_id=1, source_target_pairs={{0,4},{1,5},{2,6},{3,7},{4,0},{5,1},{6,2},{7,3},{8,12},{9,13},{10,... | collective-permute-start | bytes 884744 | tf_op jit(solution)/shard_map/sum_3_2/ppermute | solution.py:766
  179.2 19.4 %collective-permute-start.39 = (bf16[1,384,768]{2,1,0:T(8,128)(2,1)S(1)}, bf16[1,384,768]{2,1,0:T(8,128)(2,1)S(1)}, u32[]{:S(2)}, u32[]{:S(2)}) collective-permute-start(bf16[1,384,768]{2,1,0:T(8,128)(2,1)S(1)} %bitcast.144), channel_id=1, source_target_pairs={{0,2},{1,3},{2,0},{3,1},{4,6},{5,7},{6,4},{7,5},{8,10},{9,11},{10,... | collective-permute-start | bytes 1769480 | tf_op jit(solution)/shard_map/sum_1_6/ppermute | solution.py:766
  180.5 19.2 %collective-permute-start.38 = (bf16[1,384,768]{2,1,0:T(8,128)(2,1)S(1)}, bf16[1,384,768]{2,1,0:T(8,128)(2,1)}, u32[]{:S(2)}, u32[]{:S(2)}) collective-permute-start(bf16[1,384,768]{2,1,0:T(8,128)(2,1)S(1)} %bitcast.146), channel_id=1, source_target_pairs={{0,4},{1,5},{2,6},{3,7},{4,0},{5,1},{6,2},{7,3},{8,12},{9,13},{10,... | collective-permute-start | bytes 1769480 | tf_op jit(solution)/shard_map/sum_1_6/ppermute | solution.py:766
  188.3 7.4 %collective-permute-start.35 = (bf16[96,768]{1,0:T(8,128)(2,1)S(1)}, bf16[96,768]{1,0:T(8,128)(2,1)S(1)}, u32[]{:S(2)}, u32[]{:S(2)}) collective-permute-start(bf16[96,768]{1,0:T(8,128)(2,1)S(1)} %get-tuple-element.389), channel_id=1, source_target_pairs={{0,16},{8,24},{16,0},{24,8},{1,17},{9,25},{17,1},{25,9},{2,18},{10... | collective-permute-start | bytes 442376 | tf_op jit(solution)/shard_map/sum_3_3/ppermute | solution.py:766
  188.5 7.7 %collective-permute-start.34 = (bf16[96,768]{1,0:T(8,128)(2,1)S(1)}, bf16[96,768]{1,0:T(8,128)(2,1)S(1)}, u32[]{:S(2)}, u32[]{:S(2)}) collective-permute-start(bf16[96,768]{1,0:T(8,128)(2,1)S(1)} %get-tuple-element.391), channel_id=1, source_target_pairs={{0,8},{8,0},{16,24},{24,16},{1,9},{9,1},{17,25},{25,17},{2,10},{10... | collective-permute-start | bytes 442376 | tf_op jit(solution)/shard_map/sum_3_3/ppermute | solution.py:766
  191.4 10.5 %all-to-all-start.1 = ((bf16[8,48,256]{2,1,0:T(8,128)(2,1)}), bf16[8,48,256]{2,1,0:T(8,128)(2,1)S(1)}, u32[]{:S(2)}, u32[]{:S(2)}) async-start(bf16[8,48,256]{2,1,0:T(8,128)(2,1)} %get-tuple-element.284), calls=%async_computation.1 | async-start | bytes 393216 | tf_op jit(solution)/shard_map/sum_c_0/all_to_all | solution.py:881
  196.2 8.7 %collective-permute-start.37 = (bf16[96,768]{1,0:T(8,128)(2,1)S(1)}, bf16[96,768]{1,0:T(8,128)(2,1)}, u32[]{:S(2)}, u32[]{:S(2)}) collective-permute-start(bf16[96,768]{1,0:T(8,128)(2,1)S(1)} %add.217), channel_id=1, source_target_pairs={{0,8},{8,0},{16,24},{24,16},{1,9},{9,1},{17,25},{25,17},{2,10},{10... | collective-permute-start | bytes 442376 | tf_op jit(solution)/shard_map/sum_3_4/ppermute | solution.py:766
  196.7 8.8 %collective-permute-start.36 = (bf16[96,768]{1,0:T(8,128)(2,1)S(1)}, bf16[96,768]{1,0:T(8,128)(2,1)}, u32[]{:S(2)}, u32[]{:S(2)}) collective-permute-start(bf16[96,768]{1,0:T(8,128)(2,1)S(1)} %add.216), channel_id=1, source_target_pairs={{0,16},{8,24},{16,0},{24,8},{1,17},{9,25},{17,1},{25,9},{2,18},{10... | collective-permute-start | bytes 442376 | tf_op jit(solution)/shard_map/sum_3_4/ppermute | solution.py:766
  202.0 33.8 %collective-permute-start.51 = (bf16[2,384,768]{2,1,0:T(8,128)(2,1)S(1)}, bf16[2,384,768]{2,1,0:T(8,128)(2,1)S(1)}, u32[]{:S(2)}, u32[]{:S(2)}) collective-permute-start(bf16[2,384,768]{2,1,0:T(8,128)(2,1)S(1)} %constant_dynamic-update-slice_fusion.2), channel_id=1, source_target_pairs={{0,4},{1,5},{2,6},{3,7},{4,0},{5,1},{6,2},{7,3},{8,12},{9,13},{10,... | collective-permute-start | bytes 3538952 | tf_op jit(solution)/shard_map/sum_1_7/ppermute | solution.py:766
  202.9 32.9 %collective-permute-start.50 = (bf16[2,384,768]{2,1,0:T(8,128)(2,1)S(1)}, bf16[2,384,768]{2,1,0:T(8,128)(2,1)S(1)}, u32[]{:S(2)}, u32[]{:S(2)}) collective-permute-start(bf16[2,384,768]{2,1,0:T(8,128)(2,1)S(1)} %constant_dynamic-update-slice_fusion), channel_id=1, source_target_pairs={{0,2},{1,3},{2,0},{3,1},{4,6},{5,7},{6,4},{7,5},{8,10},{9,11},{10,... | collective-permute-start | bytes 3538952 | tf_op jit(solution)/shard_map/sum_1_7/ppermute | solution.py:766
  206.5 11.7 %collective-permute-start.41 = (bf16[96,768]{1,0:T(8,128)(2,1)S(1)}, bf16[96,768]{1,0:T(8,128)(2,1)S(1)}, u32[]{:S(2)}, u32[]{:S(2)}) collective-permute-start(bf16[96,768]{1,0:T(8,128)(2,1)S(1)} %add.219), channel_id=1, source_target_pairs={{0,16},{8,24},{16,0},{24,8},{1,17},{9,25},{17,1},{25,9},{2,18},{10... | collective-permute-start | bytes 442376 | tf_op jit(solution)/shard_map/sum_3_5/ppermute | solution.py:766
  207.7 10.5 %collective-permute-start.40 = (bf16[96,768]{1,0:T(8,128)(2,1)S(1)}, bf16[96,768]{1,0:T(8,128)(2,1)S(1)}, u32[]{:S(2)}, u32[]{:S(2)}) collective-permute-start(bf16[96,768]{1,0:T(8,128)(2,1)S(1)} %add.218), channel_id=1, source_target_pairs={{0,8},{8,0},{16,24},{24,16},{1,9},{9,1},{17,25},{25,17},{2,10},{10... | collective-permute-start | bytes 442376 | tf_op jit(solution)/shard_map/sum_3_5/ppermute | solution.py:766
  209.8 6.9 %collective-permute-start.42 = (bf16[272,256]{1,0:T(8,128)(2,1)S(1)}, bf16[272,256]{1,0:T(8,128)(2,1)S(1)}, u32[]{:S(2)}, u32[]{:S(2)}) collective-permute-start(bf16[272,256]{1,0:T(8,128)(2,1)S(1)} %pad_maximum_fusion.2), channel_id=1, source_target_pairs={{0,8},{8,0},{16,24},{24,16},{1,9},{9,1},{17,25},{25,17},{2,10},{10... | collective-permute-start | bytes 417800 | tf_op jit(solution)/shard_map/sum_c_1/ppermute | solution.py:766
  216.8 7.6 %collective-permute-start.45 = (bf16[272,256]{1,0:T(8,128)(2,1)S(1)}, bf16[272,256]{1,0:T(8,128)(2,1)S(1)}, u32[]{:S(2)}, u32[]{:S(2)}) collective-permute-start(bf16[272,256]{1,0:T(8,128)(2,1)S(1)} %add.220), channel_id=1, source_target_pairs={{0,16},{8,24},{16,0},{24,8},{1,17},{9,25},{17,1},{25,9},{2,18},{10... | collective-permute-start | bytes 417800 | tf_op jit(solution)/shard_map/sum_c_2/ppermute | solution.py:766
  218.2 17.5 %collective-permute-start.44 = (bf16[1,192,768]{2,1,0:T(8,128)(2,1)S(1)}, bf16[1,192,768]{2,1,0:T(8,128)(2,1)S(1)}, u32[]{:S(2)}, u32[]{:S(2)}) collective-permute-start(bf16[1,192,768]{2,1,0:T(8,128)(2,1)S(1)} %bitcast.152), channel_id=1, source_target_pairs={{0,2},{1,3},{2,0},{3,1},{4,6},{5,7},{6,4},{7,5},{8,10},{9,11},{10,... | collective-permute-start | bytes 884744 | tf_op jit(solution)/shard_map/sum_3_6/ppermute | solution.py:766
  219.8 15.9 %collective-permute-start.43 = (bf16[1,192,768]{2,1,0:T(8,128)(2,1)S(1)}, bf16[1,192,768]{2,1,0:T(8,128)(2,1)S(1)}, u32[]{:S(2)}, u32[]{:S(2)}) collective-permute-start(bf16[1,192,768]{2,1,0:T(8,128)(2,1)S(1)} %bitcast.154), channel_id=1, source_target_pairs={{0,4},{1,5},{2,6},{3,7},{4,0},{5,1},{6,2},{7,3},{8,12},{9,13},{10,... | collective-permute-start | bytes 884744 | tf_op jit(solution)/shard_map/sum_3_6/ppermute | solution.py:766
  236.2 7.7 %collective-permute-start.52 = (bf16[4,384,768]{2,1,0:T(8,128)(2,1)S(1)}, bf16[4,384,768]{2,1,0:T(8,128)(2,1)S(1)}, u32[]{:S(2)}, u32[]{:S(2)}) collective-permute-start(bf16[4,384,768]{2,1,0:T(8,128)(2,1)S(1)} %constant_dynamic-update-slice_fusion.8), channel_id=1, source_target_pairs={{0,1},{1,0},{2,3},{3,2},{4,5},{5,4},{6,7},{7,6},{8,9},{9,8},{10,11... | collective-permute-start | bytes 7077896 | tf_op jit(solution)/shard_map/sum_1_8/ppermute | solution.py:766
  236.8 15.3 %collective-permute-start.47 = (bf16[2,192,768]{2,1,0:T(8,128)(2,1)S(1)}, bf16[2,192,768]{2,1,0:T(8,128)(2,1)S(1)}, u32[]{:S(2)}, u32[]{:S(2)}) collective-permute-start(bf16[2,192,768]{2,1,0:T(8,128)(2,1)S(1)} %constant_dynamic-update-slice_fusion.6), channel_id=1, source_target_pairs={{0,4},{1,5},{2,6},{3,7},{4,0},{5,1},{6,2},{7,3},{8,12},{9,13},{10,... | collective-permute-start | bytes 1769480 | tf_op jit(solution)/shard_map/sum_3_7/ppermute | solution.py:766
  237.7 14.4 %collective-permute-start.49 = (bf16[2,192,768]{2,1,0:T(8,128)(2,1)S(1)}, bf16[2,192,768]{2,1,0:T(8,128)(2,1)S(1)}, u32[]{:S(2)}, u32[]{:S(2)}) collective-permute-start(bf16[2,192,768]{2,1,0:T(8,128)(2,1)S(1)} %constant_dynamic-update-slice_fusion.6), channel_id=1, source_target_pairs={{0,1},{1,0},{2,3},{3,2},{4,5},{5,4},{6,7},{7,6},{8,9},{9,8},{10,11... | collective-permute-start | bytes 1769480 | tf_op jit(solution)/shard_map/sum_3_7/ppermute | solution.py:766
  237.7 15.7 %collective-permute-start.46 = (bf16[2,192,768]{2,1,0:T(8,128)(2,1)S(1)}, bf16[2,192,768]{2,1,0:T(8,128)(2,1)S(1)}, u32[]{:S(2)}, u32[]{:S(2)}) collective-permute-start(bf16[2,192,768]{2,1,0:T(8,128)(2,1)S(1)} %constant_dynamic-update-slice_fusion.4), channel_id=1, source_target_pairs={{0,2},{1,3},{2,0},{3,1},{4,6},{5,7},{6,4},{7,5},{8,10},{9,11},{10,... | collective-permute-start | bytes 1769480 | tf_op jit(solution)/shard_map/sum_3_7/ppermute | solution.py:766
  240.6 12.9 %collective-permute-start.48 = (bf16[2,192,768]{2,1,0:T(8,128)(2,1)S(1)}, bf16[2,192,768]{2,1,0:T(8,128)(2,1)S(1)}, u32[]{:S(2)}, u32[]{:S(2)}) collective-permute-start(bf16[2,192,768]{2,1,0:T(8,128)(2,1)S(1)} %constant_dynamic-update-slice_fusion.4), channel_id=1, source_target_pairs={{0,1},{1,0},{2,3},{3,2},{4,5},{5,4},{6,7},{7,6},{8,9},{9,8},{10,11... | collective-permute-start | bytes 1769480 | tf_op jit(solution)/shard_map/sum_3_7/ppermute | solution.py:766
  (43 other events, 329.2 us)

commit v4 on v3

--- a/solution.py
+++ b/solution.py
@@ -444,7 +444,7 @@
         [
             far((seqs, span, width), F32),
             far((seqs, span, width)),
-            far((seqs, span, width)),
+            shape((seqs, span, width)),
             shape((8, width), F32),
         ],
         [block, block, block, result(8, width)],
@@ -497,7 +497,7 @@
     return call(
         attend_back_body,
         (seqs,),
-        (meta, *kept_far(grad_mixed, queries, keys, values, probs), key_w, value_w),
+        (meta, grad_mixed, *kept_far(queries, keys, values, probs), key_w, value_w),
         [
             far((seqs, span, width)),
             far((seqs, rows, width)),

time: 262 us -> 262 us (level)
  no operation moved by 1% of the time
where the time goes in v4:
time: 262 us; the launch traced here: 261 us
  Pallas kernels  102 us (39%)
  waiting for transfers between devices  73.8 us (28%)
  starting transfers between devices  65.2 us (25%)
  local copies, waits for them, and re-layouts  12.2 us (5%)
  other arithmetic  6.91 us (3%)
    pallas_call x14, Pallas kernels, call(): pl.pallas_call(body, grid_spec=pltpu.PrefetchScalarGridSpec(num_scalar_pr...  102 us
    ppermute x56, waiting for transfers between devices, swap(): return lax.ppermute(value, axis, [(i, i ^ mask) for i in range(size)])  72 us
    ppermute x56, starting transfers between devices, swap(): return lax.ppermute(value, axis, [(i, i ^ mask) for i in range(size)])  56.4 us
    unnamed x73, local copies, waits for them, and re-layouts  9.29 us
  transfers between devices with their start and end apart: 58, of which 31 were waited for; matrix products, arithmetic and copies ran while one was open for 3% of the time, Pallas kernels for 28%

profile of v4, /device:TPU:0, one launch (start us, length us, event | category | flops | bytes accessed | tf_op | source)
XLA Modules:
  0.0 261.0 jit_solution(14677114988567386311)
XLA Ops:
  2.3 5.2 %all-to-all-start = ((bf16[1,32,8,256]{3,1,0,2:T(8,128)(2,1)}), bf16[1,32,8,256]{3,1,0,2:T(8,128)(2,1)S(1)}, u32[]{:S(2)}, u32[]{:S(2)}) async-start(bf16[1,32,8,256]{3,1,0,2:T(8,128)(2,1)} %copy.31), calls=%async_computation | async-start | bytes 262144 | tf_op jit(solution)/shard_map/all_to_all | solution.py:945
  11.2 1.8 all-to-all-done
  13.0 1.6 summarize_body.1
  14.7 2.0 collective-permute-done
  18.6 1.8 collective-permute-start.3
  20.4 5.9 %grad_active_body.1.grad_active = bf16[768,3072]{1,0:T(8,128)(2,1)} custom-call(bf16[768,768]{1,0:T(8,128)(2,1)S(1)} %bitcast.126, bf16[3072,768]{1,0:T(8,128)(2,1)S(1)} %bitcast.119), custom_call_target="tpu_custom_call" | custom-call | flops 15000000512 | bytes 1 | tf_op jit(solution)/shard_map/grad_active_body/pallas_call | solution.py:62
  28.4 1.6 collective-permute-start.6
  30.0 1.5 project_body.1.queries
  33.1 2.5 collective-permute-done.5
  35.9 2.0 collective-permute-done.7.other
  40.5 12.1 %attend_body.1 = (bf16[3,256,768]{2,1,0:T(8,128)(2,1)}, bf16[3,256,768]{2,1,0:T(8,128)(2,1)}, bf16[3,256,768]{2,1,0:T(8,128)(2,1)}, bf16[3,3072,256]{2,1,0:T(8,1...) custom-call(s32[4]{0:T(128)S(1)} %pad_add_fusion.1.meta, ...), custom_call_target="tpu_custom_call" | custom-call | flops 30000001024 | bytes 1 | tf_op jit(solution)/shard_map/attend_body/pallas_call | solution.py:62
  52.6 11.2 %feed_body.2 = (bf16[2,768,768]{2,1,0:T(8,128)(2,1)}, bf16[2,768,768]{2,1,0:T(8,128)(2,1)}, bf16[4,2,3,64,768]{4,3,2,1,0:T(8,128)(2,1)S(1)}, bf16[4,2,192,768]{3,2,1,0:T(8,128)(2,1)S(1)}) custom-call(s32[3]{0:T(128)S(1)} %pad_add_fusion.order, bf16[768,768]{1,0:T(8,128)(2,1)S(1)} %bitcast.140, bf16[768,768]{1,0:T(8,128)(2,1)S(1)} %bitcast.127, ...), custom_call_target="tpu_custom_call" | custom-call | flops 35999997952 | bytes 1 | tf_op jit(solution)/shard_map/feed_body/pallas_call | solution.py:62
  64.3 11.2 %feed_body.3 = (bf16[2,768,768]{2,1,0:T(8,128)(2,1)}, bf16[2,768,768]{2,1,0:T(8,128)(2,1)}, bf16[4,2,3,64,768]{4,3,2,1,0:T(8,128)(2,1)S(1)}, bf16[4,2,192,768]{3,2,1,0:T(8,128)(2,1)S(1)}) custom-call(s32[3]{0:T(128)S(1)} %pad_add_fusion.order, bf16[768,768]{1,0:T(8,128)(2,1)S(1)} %bitcast.141, bf16[768,768]{1,0:T(8,128)(2,1)S(1)} %bitcast.128, ...), custom_call_target="tpu_custom_call" | custom-call | flops 35999997952 | bytes 1 | tf_op jit(solution)/shard_map/feed_body/pallas_call | solution.py:62
  78.1 11.1 %feed_back_body.1 = (f32[3,256,768]{2,1,0:T(8,128)}, bf16[3,256,768]{2,1,0:T(8,128)(2,1)}, bf16[3,256,768]{2,1,0:T(8,128)(2,1)S(1)}, f32[8,768]{1,0:T(8,128)S(1)}) custom-call(s32[3]{0:T(128)S(1)} %pad_add_fusion.order, bf16[2,768,768]{2,1,0:T(8,128)(2,1)} %get-tuple-element.221.sent, bf16[2,768,768]{2,1,0:T(8,128)(2,1)} %get-tuple-element.222.kept, ...), custom_call_target="tpu_custom_call" | custom-call | flops 24000000000 | bytes 1 | tf_op jit(solution)/shard_map/feed_back_body/pallas_call | solution.py:62
  89.2 12.2 %attend_back_body.1 = (bf16[3,256,768]{2,1,0:T(8,128)(2,1)}, bf16[3,256,768]{2,1,0:T(8,128)(2,1)}, bf16[3,256,768]{2,1,0:T(8,128)(2,1)}, bf16[4,3,32,768]{3,2,1,0:T(8,128)(2,1)S(1)}, bf16[4,3,32,768]{3,2,1,0:T(8,128)(2,1)S(1)}) custom-call(s32[4]{0:T(128)S(1)} %pad_add_fusion.1.meta, bf16[3,256,768]{2,1,0:T(8,128)(2,1)S(1)} %get-tuple-element.228.grad_mixed, ...), custom_call_target="tpu_custom_call" | custom-call | flops 41999998976 | bytes 1 | tf_op jit(solution)/shard_map/attend_back_body/pallas_call | solution.py:62
  101.4 2.3 collective-permute-done.11
  107.2 7.5 %squares_body.1 = (bf16[4,2,96,768]{3,2,1,0:T(8,128)(2,1)S(1)}, bf16[4,2,96,768]{3,2,1,0:T(8,128)(2,1)S(1)}, bf16[4,2,96,768]{3,2,1,0:T(8,128)(2,1)S(1)}, bf16[4,2,96,768]{3,2,1,0:T(8,128)(2,1)S(1)}) custom-call(s32[3]{0:T(128)S(1)} %pad_add_fusion.order, bf16[768,768]{1,0:T(8,128)(2,1)S(1)} %bitcast.137, bf16[768,768]{1,0:T(8,128)(2,1)S(1)} %bitcast.138, ...), custom_call_target="tpu_custom_call" | custom-call | flops 20999999488 | bytes 1 | tf_op jit(solution)/shard_map/squares_body/pallas_call | solution.py:62
  114.7 4.4 %collective-permute-done.13 = bf16[1,384,768]{2,1,0:T(8,128)(2,1)S(1)} collective-permute-done((bf16[1,384,768]{2,1,0:T(8,128)(2,1)S(1)}, bf16[1,384,768]{2,1,0:T(8,128)(2,1)S(1)}, u32[]{:S(2)}, u32[]{:S(2)}) %collective-permute-start.13) | collective-permute-done | bytes 589856 | tf_op jit(solution)/shard_map/sum_1_2/ppermute | solution.py:766
  122.8 1.5 collective-permute-start.19
  124.3 2.6 collective-permute-start.15
  126.8 1.6 collective-permute-start.14
  130.0 7.5 %collective-permute-done.15 = bf16[192,768]{1,0:T(8,128)(2,1)S(1)} collective-permute-done((bf16[192,768]{1,0:T(8,128)(2,1)S(1)}, bf16[192,768]{1,0:T(8,128)(2,1)S(1)}, u32[]{:S(2)}, u32[]{:S(2)}) %collective-permute-start.15) | collective-permute-done | bytes 294944 | tf_op jit(solution)/shard_map/sum_1_3/ppermute | solution.py:766
  137.7 1.5 collective-permute-start.26
  139.3 2.4 collective-permute-start.25
  141.7 7.5 %block_out_body.1 = bf16[3,256,768]{2,1,0:T(8,128)(2,1)} custom-call(s32[3]{0:T(128)S(1)} %pad_add_fusion.order, bf16[3072,768]{1,0:T(8,128)(2,1)S(1)} %bitcast.121, f32[3,256,768]{2,1,0:T(8,128)} %get-tuple-element.205.attended, bf16[2,768,768]{2,1,0:T(8,128)(2,1)} %get-tuple-element.265.sent, bf16[2,768,768]{2,1,0:T(8,128)(2,1)} %get-tuple-element.266.kept), custom_call_target="tpu_custom_call" | custom-call | flops 17999998976 | bytes 1 | tf_op jit(solution)/shard_map/block_out_body/pallas_call | solution.py:62
  149.2 2.1 collective-permute-done.26
  152.3 1.7 collective-permute-done.25
  154.0 1.5 collective-permute-start.22
  158.0 2.1 collective-permute-done.22
  162.4 2.9 %collective-permute-start.32 = (bf16[192,768]{1,0:T(8,128)(2,1)S(1)}, bf16[192,768]{1,0:T(8,128)(2,1)S(1)}, u32[]{:S(2)}, u32[]{:S(2)}) collective-permute-start(bf16[192,768]{1,0:T(8,128)(2,1)S(1)} %add.204), channel_id=1, source_target_pairs={{0,8},{8,0},{16,24},{24,16},{1,9},{9,1},{17,25},{25,17},{2,10},{10... | collective-permute-start | bytes 884744 | tf_op jit(solution)/shard_map/sum_1_5/ppermute | solution.py:766
  165.3 6.7 %leave_body.1 = (bf16[3,256,768]{2,1,0:T(8,128)(2,1)}, bf16[8,48,256]{2,1,0:T(8,128)(2,1)}) custom-call(s32[4]{0:T(128)S(1)} %pad_add_fusion.1.meta, bf16[4,3,32,768]{3,2,1,0:T(8,128)(2,1)S(1)} %pad_maximum_fusion.1.own, bf16[4,3,32,768]{3,2,1,0:T(8,128)(2,1)S(1)} %collective-permute-done.27.other, bf16[256,256]{1,0:T(8,128)(2,1)S(1)} %bitcast.115, ...), custom_call_target="tpu_custom_call" | custom-call | flops 15000000512 | bytes 1 | tf_op jit(solution)/shard_map/leave_body/pallas_call | solution.py:62
  172.0 4.1 %collective-permute-done.29 = bf16[2,192,768]{2,1,0:T(8,128)(2,1)S(1)} collective-permute-done((bf16[2,192,768]{2,1,0:T(8,128)(2,1)}, bf16[2,192,768]{2,1,0:T(8,128)(2,1)S(1)}, u32[]{:S(2)}, u32[]{:S(2)}) %collective-permute-start.29) | collective-permute-done | bytes 589856 | tf_op jit(solution)/shard_map/sum_3_1/ppermute | solution.py:766
  181.6 5.4 %collective-permute-done.31 = bf16[1,192,768]{2,1,0:T(8,128)(2,1)S(1)} collective-permute-done((bf16[1,192,768]{2,1,0:T(8,128)(2,1)S(1)}, bf16[1,192,768]{2,1,0:T(8,128)(2,1)S(1)}, u32[]{:S(2)}, u32[]{:S(2)}) %collective-permute-start.31) | collective-permute-done | bytes 294944 | tf_op jit(solution)/shard_map/sum_3_2/ppermute | solution.py:766
  188.5 3.0 %collective-permute-start.34 = (bf16[96,768]{1,0:T(8,128)(2,1)S(1)}, bf16[96,768]{1,0:T(8,128)(2,1)S(1)}, u32[]{:S(2)}, u32[]{:S(2)}) collective-permute-start(bf16[96,768]{1,0:T(8,128)(2,1)S(1)} %get-tuple-element.391), channel_id=1, source_target_pairs={{0,8},{8,0},{16,24},{24,16},{1,9},{9,1},{17,25},{25,17},{2,10},{10... | collective-permute-start | bytes 442376 | tf_op jit(solution)/shard_map/sum_3_3/ppermute | solution.py:766
  191.5 3.6 %all-to-all-start.1 = ((bf16[8,48,256]{2,1,0:T(8,128)(2,1)}), bf16[8,48,256]{2,1,0:T(8,128)(2,1)S(1)}, u32[]{:S(2)}, u32[]{:S(2)}) async-start(bf16[8,48,256]{2,1,0:T(8,128)(2,1)} %get-tuple-element.284), calls=%async_computation.1 | async-start | bytes 393216 | tf_op jit(solution)/shard_map/sum_c_0/all_to_all | solution.py:881
  196.7 1.8 collective-permute-start.36
  202.9 1.9 collective-permute-start.50
  207.7 2.2 collective-permute-start.40
  209.9 6.9 %collective-permute-done.42 = bf16[272,256]{1,0:T(8,128)(2,1)S(1)} collective-permute-done((bf16[272,256]{1,0:T(8,128)(2,1)S(1)}, bf16[272,256]{1,0:T(8,128)(2,1)S(1)}, u32[]{:S(2)}, u32[]{:S(2)}) %collective-permute-start.42) | collective-permute-done | bytes 139296 | tf_op jit(solution)/shard_map/sum_c_1/ppermute | solution.py:766
  218.2 1.6 collective-permute-start.44
  219.8 2.3 collective-permute-start.43
  222.1 2.3 collective-permute-done.45
  225.2 10.5 %collective-permute-done.44 = bf16[1,192,768]{2,1,0:T(8,128)(2,1)S(1)} collective-permute-done((bf16[1,192,768]{2,1,0:T(8,128)(2,1)S(1)}, bf16[1,192,768]{2,1,0:T(8,128)(2,1)S(1)}, u32[]{:S(2)}, u32[]{:S(2)}) %collective-permute-start.44) | collective-permute-done | bytes 294944 | tf_op jit(solution)/shard_map/sum_3_6/ppermute | solution.py:766
  238.8 1.8 collective-permute-done.53
  240.7 3.2 %collective-permute-done.52 = bf16[4,384,768]{2,1,0:T(8,128)(2,1)S(1)} collective-permute-done((bf16[4,384,768]{2,1,0:T(8,128)(2,1)S(1)}, bf16[4,384,768]{2,1,0:T(8,128)(2,1)S(1)}, u32[]{:S(2)}, u32[]{:S(2)}) %collective-permute-start.52) | collective-permute-done | bytes 2359328 | tf_op jit(solution)/shard_map/sum_1_8/ppermute | solution.py:766
  244.0 7.5 %place_feed_body.1 = (f32[3072,768]{1,0:T(8,128)}, f32[768,3072]{1,0:T(8,128)}, f32[8,768]{1,0:T(8,128)S(1)}) custom-call(s32[3]{0:T(128)S(1)} %pad_add_fusion.order, bf16[4,2,3,64,768]{4,3,2,1,0:T(8,128)(2,1)S(1)} %bitcast.111, bf16[4,2,3,64,768]{4,3,2,1,0:T(8,128)(2,1)S(1)} %bitcast.123, bf16[4,2,192,768]{3,2,1,0:T(8,128)(2,1)S(1)} %bitcast.110, ...), custom_call_target="tpu_custom_call" | custom-call | flops 24000000000 | bytes 1 | tf_op jit(solution)/shard_map/place_feed_body/pallas_call | solution.py:62
  254.0 1.5 collective-permute-done.54
  256.3 4.6 %place_squares_body.1 = (f32[768,768]{1,0:T(8,128)}, f32[768,768]{1,0:T(8,128)}, f32[768,768]{1,0:T(8,128)}, f32[768,768]{1,0:T(8,128)}, f32[768]{0:T(1024)}, /*...) custom-call(s32[3]{0:T(128)S(1)} %pad_add_fusion.order, bf16[2,2,96,768]{3,2,1,0:T(8,128)(2,1)S(1)} %bitcast.112, ...), custom_call_target="tpu_custom_call" | custom-call | flops 15000000512 | bytes 1 | tf_op jit(solution)/shard_map/place_squares_body/pallas_call | solution.py:62
  (210 shorter events, 56.1 us)
Async XLA Ops:
  2.3 10.7 %all-to-all-start = ((bf16[1,32,8,256]{3,1,0,2:T(8,128)(2,1)}), bf16[1,32,8,256]{3,1,0,2:T(8,128)(2,1)S(1)}, u32[]{:S(2)}, u32[]{:S(2)}) async-start(bf16[1,32,8,256]{3,1,0,2:T(8,128)(2,1)} %copy.31), calls=%async_computation | async-start | bytes 262144 | tf_op jit(solution)/shard_map/all_to_all | solution.py:945
  16.8 9.5 %collective-permute-start.1 = (bf16[3,32,768]{2,1,0:T(8,128)(2,1)S(1)}, bf16[3,32,768]{2,1,0:T(8,128)(2,1)S(1)}, u32[]{:S(2)}, u32[]{:S(2)}) collective-permute-start(bf16[3,32,768]{2,1,0:T(8,128)(2,1)S(1)} %get-tuple-element.382), channel_id=1, source_target_pairs={{0,2},{1,3},{2,0},{3,1},{4,6},{5,7},{6,4},{7,5},{8,10},{9,11},{10,... | collective-permute-start | bytes 442376 | tf_op jit(solution)/shard_map/ppermute | solution.py:766
  17.5 8.9 %collective-permute-start.2 = (bf16[3,32,768]{2,1,0:T(8,128)(2,1)S(1)}, bf16[3,32,768]{2,1,0:T(8,128)(2,1)S(1)}, u32[]{:S(2)}, u32[]{:S(2)}) collective-permute-start(bf16[3,32,768]{2,1,0:T(8,128)(2,1)S(1)} %get-tuple-element.381), channel_id=1, source_target_pairs={{0,4},{1,5},{2,6},{3,7},{4,0},{5,1},{6,2},{7,3},{8,12},{9,13},{10,... | collective-permute-start | bytes 442376 | tf_op jit(solution)/shard_map/ppermute | solution.py:766
  18.6 7.7 %collective-permute-start.3 = (bf16[3,32,768]{2,1,0:T(8,128)(2,1)S(1)}, bf16[3,32,768]{2,1,0:T(8,128)(2,1)S(1)}, u32[]{:S(2)}, u32[]{:S(2)}) collective-permute-start(bf16[3,32,768]{2,1,0:T(8,128)(2,1)S(1)} %get-tuple-element.380), channel_id=1, source_target_pairs={{0,6},{1,7},{2,4},{3,5},{4,2},{5,3},{6,0},{7,1},{8,14},{9,15},{10,... | collective-permute-start | bytes 442376 | tf_op jit(solution)/shard_map/ppermute | solution.py:766
  27.8 7.8 %collective-permute-start.5 = (bf16[3,32,768]{2,1,0:T(8,128)(2,1)S(1)}, bf16[3,32,768]{2,1,0:T(8,128)(2,1)S(1)}, u32[]{:S(2)}, u32[]{:S(2)}) collective-permute-start(bf16[3,32,768]{2,1,0:T(8,128)(2,1)S(1)} %add_convert_fusion.4), channel_id=1, source_target_pairs={{0,4},{1,5},{2,6},{3,7},{4,0},{5,1},{6,2},{7,3},{8,12},{9,13},{10,... | collective-permute-start | bytes 442376 | tf_op jit(solution)/shard_map/ppermute | solution.py:766
  28.4 7.2 %collective-permute-start.6 = (bf16[3,32,768]{2,1,0:T(8,128)(2,1)S(1)}, bf16[3,32,768]{2,1,0:T(8,128)(2,1)S(1)}, u32[]{:S(2)}, u32[]{:S(2)}) collective-permute-start(bf16[3,32,768]{2,1,0:T(8,128)(2,1)S(1)} %add_convert_fusion.4), channel_id=1, source_target_pairs={{0,6},{1,7},{2,4},{3,5},{4,2},{5,3},{6,0},{7,1},{8,14},{9,15},{10,... | collective-permute-start | bytes 442376 | tf_op jit(solution)/shard_map/ppermute | solution.py:766
  63.8 11.7 %collective-permute-start.8 = (bf16[4,384,768]{2,1,0:T(8,128)(2,1)S(1)}, bf16[4,384,768]{2,1,0:T(8,128)(2,1)S(1)}, u32[]{:S(2)}, u32[]{:S(2)}) collective-permute-start(bf16[4,384,768]{2,1,0:T(8,128)(2,1)S(1)} %bitcast.125), channel_id=1, source_target_pairs={{0,1},{1,0},{2,3},{3,2},{4,5},{5,4},{6,7},{7,6},{8,9},{9,8},{10,11... | collective-permute-start | bytes 7077896 | tf_op jit(solution)/shard_map/sum_1_0/ppermute | solution.py:766
  63.9 11.5 %collective-permute-start.9 = (bf16[4,384,768]{2,1,0:T(8,128)(2,1)S(1)}, bf16[4,384,768]{2,1,0:T(8,128)(2,1)S(1)}, u32[]{:S(2)}, u32[]{:S(2)}) collective-permute-start(bf16[4,384,768]{2,1,0:T(8,128)(2,1)S(1)} %bitcast.124), channel_id=1, source_target_pairs={{0,1},{1,0},{2,3},{3,2},{4,5},{5,4},{6,7},{7,6},{8,9},{9,8},{10,11... | collective-permute-start | bytes 7077896 | tf_op jit(solution)/shard_map/sum_1_0/ppermute | solution.py:766
  75.7 28.1 %collective-permute-start.11 = (bf16[2,384,768]{2,1,0:T(8,128)(2,1)S(1)}, bf16[2,384,768]{2,1,0:T(8,128)(2,1)S(1)}, u32[]{:S(2)}, u32[]{:S(2)}) collective-permute-start(bf16[2,384,768]{2,1,0:T(8,128)(2,1)S(1)} %get-tuple-element.361), channel_id=1, source_target_pairs={{0,4},{1,5},{2,6},{3,7},{4,0},{5,1},{6,2},{7,3},{8,12},{9,13},{10,... | collective-permute-start | bytes 3538952 | tf_op jit(solution)/shard_map/sum_1_1/ppermute | solution.py:766
  76.9 27.8 %collective-permute-start.10 = (bf16[2,384,768]{2,1,0:T(8,128)(2,1)S(1)}, bf16[2,384,768]{2,1,0:T(8,128)(2,1)S(1)}, u32[]{:S(2)}, u32[]{:S(2)}) collective-permute-start(bf16[2,384,768]{2,1,0:T(8,128)(2,1)S(1)} %get-tuple-element.363), channel_id=1, source_target_pairs={{0,2},{1,3},{2,0},{3,1},{4,6},{5,7},{6,4},{7,5},{8,10},{9,11},{10,... | collective-permute-start | bytes 3538952 | tf_op jit(solution)/shard_map/sum_1_1/ppermute | solution.py:766
  101.4 19.1 %collective-permute-start.16 = (bf16[4,3,32,768]{3,2,1,0:T(8,128)(2,1)S(1)}, bf16[4,3,32,768]{3,2,1,0:T(8,128)(2,1)S(1)}, u32[]{:S(2)}, u32[]{:S(2)}) collective-permute-start(bf16[4,3,32,768]{3,2,1,0:T(8,128)(2,1)S(1)} %get-tuple-element.236), channel_id=1, source_target_pairs={{0,1},{1,0},{2,3},{3,2},{4,5},{5,4},{6,7},{7,6},{8,9},{9,8},{10,11... | collective-permute-start | bytes 1769480 | tf_op jit(solution)/shard_map/sum_g_0/ppermute | solution.py:766
  104.8 14.3 %collective-permute-start.13 = (bf16[1,384,768]{2,1,0:T(8,128)(2,1)S(1)}, bf16[1,384,768]{2,1,0:T(8,128)(2,1)S(1)}, u32[]{:S(2)}, u32[]{:S(2)}) collective-permute-start(bf16[1,384,768]{2,1,0:T(8,128)(2,1)S(1)} %get-tuple-element.369), channel_id=1, source_target_pairs={{0,2},{1,3},{2,0},{3,1},{4,6},{5,7},{6,4},{7,5},{8,10},{9,11},{10,... | collective-permute-start | bytes 1769480 | tf_op jit(solution)/shard_map/sum_1_2/ppermute | solution.py:766
  106.1 14.0 %collective-permute-start.12 = (bf16[1,384,768]{2,1,0:T(8,128)(2,1)S(1)}, bf16[1,384,768]{2,1,0:T(8,128)(2,1)S(1)}, u32[]{:S(2)}, u32[]{:S(2)}) collective-permute-start(bf16[1,384,768]{2,1,0:T(8,128)(2,1)S(1)} %get-tuple-element.371), channel_id=1, source_target_pairs={{0,4},{1,5},{2,6},{3,7},{4,0},{5,1},{6,2},{7,3},{8,12},{9,13},{10,... | collective-permute-start | bytes 1769480 | tf_op jit(solution)/shard_map/sum_1_2/ppermute | solution.py:766
  120.7 7.7 %collective-permute-start.17 = (bf16[3,32,768]{2,1,0:T(8,128)(2,1)S(1)}, bf16[3,32,768]{2,1,0:T(8,128)(2,1)S(1)}, u32[]{:S(2)}, u32[]{:S(2)}) collective-permute-start(bf16[3,32,768]{2,1,0:T(8,128)(2,1)S(1)} %get-tuple-element.378), channel_id=1, source_target_pairs={{0,2},{1,3},{2,0},{3,1},{4,6},{5,7},{6,4},{7,5},{8,10},{9,11},{10,... | collective-permute-start | bytes 442376 | tf_op jit(solution)/shard_map/sum_g_1/ppermute | solution.py:766
  121.7 6.8 %collective-permute-start.18 = (bf16[3,32,768]{2,1,0:T(8,128)(2,1)S(1)}, bf16[3,32,768]{2,1,0:T(8,128)(2,1)S(1)}, u32[]{:S(2)}, u32[]{:S(2)}) collective-permute-start(bf16[3,32,768]{2,1,0:T(8,128)(2,1)S(1)} %get-tuple-element.377), channel_id=1, source_target_pairs={{0,4},{1,5},{2,6},{3,7},{4,0},{5,1},{6,2},{7,3},{8,12},{9,13},{10,... | collective-permute-start | bytes 442376 | tf_op jit(solution)/shard_map/sum_g_1/ppermute | solution.py:766
  124.3 13.2 %collective-permute-start.15 = (bf16[192,768]{1,0:T(8,128)(2,1)S(1)}, bf16[192,768]{1,0:T(8,128)(2,1)S(1)}, u32[]{:S(2)}, u32[]{:S(2)}) collective-permute-start(bf16[192,768]{1,0:T(8,128)(2,1)S(1)} %get-tuple-element.385), channel_id=1, source_target_pairs={{0,16},{8,24},{16,0},{24,8},{1,17},{9,25},{17,1},{25,9},{2,18},{10... | collective-permute-start | bytes 884744 | tf_op jit(solution)/shard_map/sum_1_3/ppermute | solution.py:766
  126.8 10.8 %collective-permute-start.14 = (bf16[192,768]{1,0:T(8,128)(2,1)S(1)}, bf16[192,768]{1,0:T(8,128)(2,1)S(1)}, u32[]{:S(2)}, u32[]{:S(2)}) collective-permute-start(bf16[192,768]{1,0:T(8,128)(2,1)S(1)} %get-tuple-element.387), channel_id=1, source_target_pairs={{0,8},{8,0},{16,24},{24,16},{1,9},{9,1},{17,25},{25,17},{2,10},{10... | collective-permute-start | bytes 884744 | tf_op jit(solution)/shard_map/sum_1_3/ppermute | solution.py:766
  128.4 27.2 %collective-permute-start.23 = (bf16[4,192,768]{2,1,0:T(8,128)(2,1)S(1)}, bf16[4,192,768]{2,1,0:T(8,128)(2,1)S(1)}, u32[]{:S(2)}, u32[]{:S(2)}) collective-permute-start(bf16[4,192,768]{2,1,0:T(8,128)(2,1)S(1)} %bitcast.130), channel_id=1, source_target_pairs={{0,1},{1,0},{2,3},{3,2},{4,5},{5,4},{6,7},{7,6},{8,9},{9,8},{10,11... | collective-permute-start | bytes 3538952 | tf_op jit(solution)/shard_map/sum_3_0/ppermute | solution.py:766
  128.5 27.2 %collective-permute-start.24 = (bf16[4,192,768]{2,1,0:T(8,128)(2,1)S(1)}, bf16[4,192,768]{2,1,0:T(8,128)(2,1)S(1)}, u32[]{:S(2)}, u32[]{:S(2)}) collective-permute-start(bf16[4,192,768]{2,1,0:T(8,128)(2,1)S(1)} %bitcast.129), channel_id=1, source_target_pairs={{0,1},{1,0},{2,3},{3,2},{4,5},{5,4},{6,7},{7,6},{8,9},{9,8},{10,11... | collective-permute-start | bytes 3538952 | tf_op jit(solution)/shard_map/sum_3_0/ppermute | solution.py:766
  129.0 28.9 %collective-permute-start.20 = (bf16[3,32,768]{2,1,0:T(8,128)(2,1)S(1)}, bf16[3,32,768]{2,1,0:T(8,128)(2,1)S(1)}, u32[]{:S(2)}, u32[]{:S(2)}) collective-permute-start(bf16[3,32,768]{2,1,0:T(8,128)(2,1)S(1)} %add_convert_fusion), channel_id=1, source_target_pairs={{0,2},{1,3},{2,0},{3,1},{4,6},{5,7},{6,4},{7,5},{8,10},{9,11},{10,... | collective-permute-start | bytes 442376 | tf_op jit(solution)/shard_map/sum_g_2/ppermute | solution.py:766
  137.7 13.6 %collective-permute-start.26 = (bf16[192,768]{1,0:T(8,128)(2,1)S(1)}, bf16[192,768]{1,0:T(8,128)(2,1)S(1)}, u32[]{:S(2)}, u32[]{:S(2)}) collective-permute-start(bf16[192,768]{1,0:T(8,128)(2,1)S(1)} %add.203), channel_id=1, source_target_pairs={{0,8},{8,0},{16,24},{24,16},{1,9},{9,1},{17,25},{25,17},{2,10},{10... | collective-permute-start | bytes 884744 | tf_op jit(solution)/shard_map/sum_1_4/ppermute | solution.py:766
  139.3 14.7 %collective-permute-start.25 = (bf16[192,768]{1,0:T(8,128)(2,1)S(1)}, bf16[192,768]{1,0:T(8,128)(2,1)S(1)}, u32[]{:S(2)}, u32[]{:S(2)}) collective-permute-start(bf16[192,768]{1,0:T(8,128)(2,1)S(1)} %add.202), channel_id=1, source_target_pairs={{0,16},{8,24},{16,0},{24,8},{1,17},{9,25},{17,1},{25,9},{2,18},{10... | collective-permute-start | bytes 884744 | tf_op jit(solution)/shard_map/sum_1_4/ppermute | solution.py:766
  160.2 15.9 %collective-permute-start.29 = (bf16[2,192,768]{2,1,0:T(8,128)(2,1)}, bf16[2,192,768]{2,1,0:T(8,128)(2,1)S(1)}, u32[]{:S(2)}, u32[]{:S(2)}) collective-permute-start(bf16[2,192,768]{2,1,0:T(8,128)(2,1)} %get-tuple-element.365), channel_id=1, source_target_pairs={{0,4},{1,5},{2,6},{3,7},{4,0},{5,1},{6,2},{7,3},{8,12},{9,13},{10,... | collective-permute-start | bytes 1769480 | tf_op jit(solution)/shard_map/sum_3_1/ppermute | solution.py:766
  161.3 15.6 %collective-permute-start.28 = (bf16[2,192,768]{2,1,0:T(8,128)(2,1)}, bf16[2,192,768]{2,1,0:T(8,128)(2,1)S(1)}, u32[]{:S(2)}, u32[]{:S(2)}) collective-permute-start(bf16[2,192,768]{2,1,0:T(8,128)(2,1)} %get-tuple-element.367), channel_id=1, source_target_pairs={{0,2},{1,3},{2,0},{3,1},{4,6},{5,7},{6,4},{7,5},{8,10},{9,11},{10,... | collective-permute-start | bytes 1769480 | tf_op jit(solution)/shard_map/sum_3_1/ppermute | solution.py:766
  162.4 16.7 %collective-permute-start.33 = (bf16[192,768]{1,0:T(8,128)(2,1)S(1)}, bf16[192,768]{1,0:T(8,128)(2,1)S(1)}, u32[]{:S(2)}, u32[]{:S(2)}) collective-permute-start(bf16[192,768]{1,0:T(8,128)(2,1)S(1)} %add.205), channel_id=1, source_target_pairs={{0,16},{8,24},{16,0},{24,8},{1,17},{9,25},{17,1},{25,9},{2,18},{10... | collective-permute-start | bytes 884744 | tf_op jit(solution)/shard_map/sum_1_5/ppermute | solution.py:766
  162.4 16.7 %collective-permute-start.32 = (bf16[192,768]{1,0:T(8,128)(2,1)S(1)}, bf16[192,768]{1,0:T(8,128)(2,1)S(1)}, u32[]{:S(2)}, u32[]{:S(2)}) collective-permute-start(bf16[192,768]{1,0:T(8,128)(2,1)S(1)} %add.204), channel_id=1, source_target_pairs={{0,8},{8,0},{16,24},{24,16},{1,9},{9,1},{17,25},{25,17},{2,10},{10... | collective-permute-start | bytes 884744 | tf_op jit(solution)/shard_map/sum_1_5/ppermute | solution.py:766
  177.0 10.0 %collective-permute-start.31 = (bf16[1,192,768]{2,1,0:T(8,128)(2,1)S(1)}, bf16[1,192,768]{2,1,0:T(8,128)(2,1)S(1)}, u32[]{:S(2)}, u32[]{:S(2)}) collective-permute-start(bf16[1,192,768]{2,1,0:T(8,128)(2,1)S(1)} %get-tuple-element.373), channel_id=1, source_target_pairs={{0,2},{1,3},{2,0},{3,1},{4,6},{5,7},{6,4},{7,5},{8,10},{9,11},{10,... | collective-permute-start | bytes 884744 | tf_op jit(solution)/shard_map/sum_3_2/ppermute | solution.py:766
  178.1 10.0 %collective-permute-start.30 = (bf16[1,192,768]{2,1,0:T(8,128)(2,1)S(1)}, bf16[1,192,768]{2,1,0:T(8,128)(2,1)S(1)}, u32[]{:S(2)}, u32[]{:S(2)}) collective-permute-start(bf16[1,192,768]{2,1,0:T(8,128)(2,1)S(1)} %get-tuple-element.375), channel_id=1, source_target_pairs={{0,4},{1,5},{2,6},{3,7},{4,0},{5,1},{6,2},{7,3},{8,12},{9,13},{10,... | collective-permute-start | bytes 884744 | tf_op jit(solution)/shard_map/sum_3_2/ppermute | solution.py:766
  179.2 19.4 %collective-permute-start.39 = (bf16[1,384,768]{2,1,0:T(8,128)(2,1)S(1)}, bf16[1,384,768]{2,1,0:T(8,128)(2,1)S(1)}, u32[]{:S(2)}, u32[]{:S(2)}) collective-permute-start(bf16[1,384,768]{2,1,0:T(8,128)(2,1)S(1)} %bitcast.144), channel_id=1, source_target_pairs={{0,2},{1,3},{2,0},{3,1},{4,6},{5,7},{6,4},{7,5},{8,10},{9,11},{10,... | collective-permute-start | bytes 1769480 | tf_op jit(solution)/shard_map/sum_1_6/ppermute | solution.py:766
  180.5 19.2 %collective-permute-start.38 = (bf16[1,384,768]{2,1,0:T(8,128)(2,1)S(1)}, bf16[1,384,768]{2,1,0:T(8,128)(2,1)}, u32[]{:S(2)}, u32[]{:S(2)}) collective-permute-start(bf16[1,384,768]{2,1,0:T(8,128)(2,1)S(1)} %bitcast.146), channel_id=1, source_target_pairs={{0,4},{1,5},{2,6},{3,7},{4,0},{5,1},{6,2},{7,3},{8,12},{9,13},{10,... | collective-permute-start | bytes 1769480 | tf_op jit(solution)/shard_map/sum_1_6/ppermute | solution.py:766
  188.3 7.4 %collective-permute-start.35 = (bf16[96,768]{1,0:T(8,128)(2,1)S(1)}, bf16[96,768]{1,0:T(8,128)(2,1)S(1)}, u32[]{:S(2)}, u32[]{:S(2)}) collective-permute-start(bf16[96,768]{1,0:T(8,128)(2,1)S(1)} %get-tuple-element.389), channel_id=1, source_target_pairs={{0,16},{8,24},{16,0},{24,8},{1,17},{9,25},{17,1},{25,9},{2,18},{10... | collective-permute-start | bytes 442376 | tf_op jit(solution)/shard_map/sum_3_3/ppermute | solution.py:766
  188.5 7.7 %collective-permute-start.34 = (bf16[96,768]{1,0:T(8,128)(2,1)S(1)}, bf16[96,768]{1,0:T(8,128)(2,1)S(1)}, u32[]{:S(2)}, u32[]{:S(2)}) collective-permute-start(bf16[96,768]{1,0:T(8,128)(2,1)S(1)} %get-tuple-element.391), channel_id=1, source_target_pairs={{0,8},{8,0},{16,24},{24,16},{1,9},{9,1},{17,25},{25,17},{2,10},{10... | collective-permute-start | bytes 442376 | tf_op jit(solution)/shard_map/sum_3_3/ppermute | solution.py:766
  191.5 10.5 %all-to-all-start.1 = ((bf16[8,48,256]{2,1,0:T(8,128)(2,1)}), bf16[8,48,256]{2,1,0:T(8,128)(2,1)S(1)}, u32[]{:S(2)}, u32[]{:S(2)}) async-start(bf16[8,48,256]{2,1,0:T(8,128)(2,1)} %get-tuple-element.284), calls=%async_computation.1 | async-start | bytes 393216 | tf_op jit(solution)/shard_map/sum_c_0/all_to_all | solution.py:881
  196.2 8.6 %collective-permute-start.37 = (bf16[96,768]{1,0:T(8,128)(2,1)S(1)}, bf16[96,768]{1,0:T(8,128)(2,1)}, u32[]{:S(2)}, u32[]{:S(2)}) collective-permute-start(bf16[96,768]{1,0:T(8,128)(2,1)S(1)} %add.217), channel_id=1, source_target_pairs={{0,8},{8,0},{16,24},{24,16},{1,9},{9,1},{17,25},{25,17},{2,10},{10... | collective-permute-start | bytes 442376 | tf_op jit(solution)/shard_map/sum_3_4/ppermute | solution.py:766
  196.7 8.8 %collective-permute-start.36 = (bf16[96,768]{1,0:T(8,128)(2,1)S(1)}, bf16[96,768]{1,0:T(8,128)(2,1)}, u32[]{:S(2)}, u32[]{:S(2)}) collective-permute-start(bf16[96,768]{1,0:T(8,128)(2,1)S(1)} %add.216), channel_id=1, source_target_pairs={{0,16},{8,24},{16,0},{24,8},{1,17},{9,25},{17,1},{25,9},{2,18},{10... | collective-permute-start | bytes 442376 | tf_op jit(solution)/shard_map/sum_3_4/ppermute | solution.py:766
  202.0 33.8 %collective-permute-start.51 = (bf16[2,384,768]{2,1,0:T(8,128)(2,1)S(1)}, bf16[2,384,768]{2,1,0:T(8,128)(2,1)S(1)}, u32[]{:S(2)}, u32[]{:S(2)}) collective-permute-start(bf16[2,384,768]{2,1,0:T(8,128)(2,1)S(1)} %constant_dynamic-update-slice_fusion.2), channel_id=1, source_target_pairs={{0,4},{1,5},{2,6},{3,7},{4,0},{5,1},{6,2},{7,3},{8,12},{9,13},{10,... | collective-permute-start | bytes 3538952 | tf_op jit(solution)/shard_map/sum_1_7/ppermute | solution.py:766
  202.9 32.9 %collective-permute-start.50 = (bf16[2,384,768]{2,1,0:T(8,128)(2,1)S(1)}, bf16[2,384,768]{2,1,0:T(8,128)(2,1)S(1)}, u32[]{:S(2)}, u32[]{:S(2)}) collective-permute-start(bf16[2,384,768]{2,1,0:T(8,128)(2,1)S(1)} %constant_dynamic-update-slice_fusion), channel_id=1, source_target_pairs={{0,2},{1,3},{2,0},{3,1},{4,6},{5,7},{6,4},{7,5},{8,10},{9,11},{10,... | collective-permute-start | bytes 3538952 | tf_op jit(solution)/shard_map/sum_1_7/ppermute | solution.py:766
  206.5 11.7 %collective-permute-start.41 = (bf16[96,768]{1,0:T(8,128)(2,1)S(1)}, bf16[96,768]{1,0:T(8,128)(2,1)S(1)}, u32[]{:S(2)}, u32[]{:S(2)}) collective-permute-start(bf16[96,768]{1,0:T(8,128)(2,1)S(1)} %add.219), channel_id=1, source_target_pairs={{0,16},{8,24},{16,0},{24,8},{1,17},{9,25},{17,1},{25,9},{2,18},{10... | collective-permute-start | bytes 442376 | tf_op jit(solution)/shard_map/sum_3_5/ppermute | solution.py:766
  207.7 10.5 %collective-permute-start.40 = (bf16[96,768]{1,0:T(8,128)(2,1)S(1)}, bf16[96,768]{1,0:T(8,128)(2,1)S(1)}, u32[]{:S(2)}, u32[]{:S(2)}) collective-permute-start(bf16[96,768]{1,0:T(8,128)(2,1)S(1)} %add.218), channel_id=1, source_target_pairs={{0,8},{8,0},{16,24},{24,16},{1,9},{9,1},{17,25},{25,17},{2,10},{10... | collective-permute-start | bytes 442376 | tf_op jit(solution)/shard_map/sum_3_5/ppermute | solution.py:766
  209.8 6.9 %collective-permute-start.42 = (bf16[272,256]{1,0:T(8,128)(2,1)S(1)}, bf16[272,256]{1,0:T(8,128)(2,1)S(1)}, u32[]{:S(2)}, u32[]{:S(2)}) collective-permute-start(bf16[272,256]{1,0:T(8,128)(2,1)S(1)} %pad_maximum_fusion.2), channel_id=1, source_target_pairs={{0,8},{8,0},{16,24},{24,16},{1,9},{9,1},{17,25},{25,17},{2,10},{10... | collective-permute-start | bytes 417800 | tf_op jit(solution)/shard_map/sum_c_1/ppermute | solution.py:766
  216.8 7.6 %collective-permute-start.45 = (bf16[272,256]{1,0:T(8,128)(2,1)S(1)}, bf16[272,256]{1,0:T(8,128)(2,1)S(1)}, u32[]{:S(2)}, u32[]{:S(2)}) collective-permute-start(bf16[272,256]{1,0:T(8,128)(2,1)S(1)} %add.220), channel_id=1, source_target_pairs={{0,16},{8,24},{16,0},{24,8},{1,17},{9,25},{17,1},{25,9},{2,18},{10... | collective-permute-start | bytes 417800 | tf_op jit(solution)/shard_map/sum_c_2/ppermute | solution.py:766
  218.2 17.5 %collective-permute-start.44 = (bf16[1,192,768]{2,1,0:T(8,128)(2,1)S(1)}, bf16[1,192,768]{2,1,0:T(8,128)(2,1)S(1)}, u32[]{:S(2)}, u32[]{:S(2)}) collective-permute-start(bf16[1,192,768]{2,1,0:T(8,128)(2,1)S(1)} %bitcast.152), channel_id=1, source_target_pairs={{0,2},{1,3},{2,0},{3,1},{4,6},{5,7},{6,4},{7,5},{8,10},{9,11},{10,... | collective-permute-start | bytes 884744 | tf_op jit(solution)/shard_map/sum_3_6/ppermute | solution.py:766
  219.8 15.9 %collective-permute-start.43 = (bf16[1,192,768]{2,1,0:T(8,128)(2,1)S(1)}, bf16[1,192,768]{2,1,0:T(8,128)(2,1)S(1)}, u32[]{:S(2)}, u32[]{:S(2)}) collective-permute-start(bf16[1,192,768]{2,1,0:T(8,128)(2,1)S(1)} %bitcast.154), channel_id=1, source_target_pairs={{0,4},{1,5},{2,6},{3,7},{4,0},{5,1},{6,2},{7,3},{8,12},{9,13},{10,... | collective-permute-start | bytes 884744 | tf_op jit(solution)/shard_map/sum_3_6/ppermute | solution.py:766
  236.3 7.7 %collective-permute-start.52 = (bf16[4,384,768]{2,1,0:T(8,128)(2,1)S(1)}, bf16[4,384,768]{2,1,0:T(8,128)(2,1)S(1)}, u32[]{:S(2)}, u32[]{:S(2)}) collective-permute-start(bf16[4,384,768]{2,1,0:T(8,128)(2,1)S(1)} %constant_dynamic-update-slice_fusion.8), channel_id=1, source_target_pairs={{0,1},{1,0},{2,3},{3,2},{4,5},{5,4},{6,7},{7,6},{8,9},{9,8},{10,11... | collective-permute-start | bytes 7077896 | tf_op jit(solution)/shard_map/sum_1_8/ppermute | solution.py:766
  236.8 15.3 %collective-permute-start.47 = (bf16[2,192,768]{2,1,0:T(8,128)(2,1)S(1)}, bf16[2,192,768]{2,1,0:T(8,128)(2,1)S(1)}, u32[]{:S(2)}, u32[]{:S(2)}) collective-permute-start(bf16[2,192,768]{2,1,0:T(8,128)(2,1)S(1)} %constant_dynamic-update-slice_fusion.6), channel_id=1, source_target_pairs={{0,4},{1,5},{2,6},{3,7},{4,0},{5,1},{6,2},{7,3},{8,12},{9,13},{10,... | collective-permute-start | bytes 1769480 | tf_op jit(solution)/shard_map/sum_3_7/ppermute | solution.py:766
  237.7 14.4 %collective-permute-start.49 = (bf16[2,192,768]{2,1,0:T(8,128)(2,1)S(1)}, bf16[2,192,768]{2,1,0:T(8,128)(2,1)S(1)}, u32[]{:S(2)}, u32[]{:S(2)}) collective-permute-start(bf16[2,192,768]{2,1,0:T(8,128)(2,1)S(1)} %constant_dynamic-update-slice_fusion.6), channel_id=1, source_target_pairs={{0,1},{1,0},{2,3},{3,2},{4,5},{5,4},{6,7},{7,6},{8,9},{9,8},{10,11... | collective-permute-start | bytes 1769480 | tf_op jit(solution)/shard_map/sum_3_7/ppermute | solution.py:766
  237.7 15.7 %collective-permute-start.46 = (bf16[2,192,768]{2,1,0:T(8,128)(2,1)S(1)}, bf16[2,192,768]{2,1,0:T(8,128)(2,1)S(1)}, u32[]{:S(2)}, u32[]{:S(2)}) collective-permute-start(bf16[2,192,768]{2,1,0:T(8,128)(2,1)S(1)} %constant_dynamic-update-slice_fusion.4), channel_id=1, source_target_pairs={{0,2},{1,3},{2,0},{3,1},{4,6},{5,7},{6,4},{7,5},{8,10},{9,11},{10,... | collective-permute-start | bytes 1769480 | tf_op jit(solution)/shard_map/sum_3_7/ppermute | solution.py:766
  240.6 12.9 %collective-permute-start.48 = (bf16[2,192,768]{2,1,0:T(8,128)(2,1)S(1)}, bf16[2,192,768]{2,1,0:T(8,128)(2,1)S(1)}, u32[]{:S(2)}, u32[]{:S(2)}) collective-permute-start(bf16[2,192,768]{2,1,0:T(8,128)(2,1)S(1)} %constant_dynamic-update-slice_fusion.4), channel_id=1, source_target_pairs={{0,1},{1,0},{2,3},{3,2},{4,5},{5,4},{6,7},{7,6},{8,9},{9,8},{10,11... | collective-permute-start | bytes 1769480 | tf_op jit(solution)/shard_map/sum_3_7/ppermute | solution.py:766
  (43 other events, 328.9 us)
